TPU v7x, 256 devices: a whole 4x4x8 slice. The times are simulated.
256 devices in a mesh: ctx: 64 (over z, x, core), ch: 4 (over y).
Axes of the slice: x: 4, y: 4, z: 8, core: 2. Of those that a mesh axis runs over, the one named last changes fastest.
Arguments:
- streams: bfloat16 [3, 8192, 16384], P(None, ('ch', 'ctx')), may hold values from -6 to 6
- short_taps: float32 [3, 512, 7], P(None, 'ch'), may hold values from -3 to 3
- pole_rates: float32 [512, 16], P('ch'), may hold values from 3.0517578e-06 to 0.2, as said below
- residues: float32 [512, 16], P('ch'), may hold values from -0.6 to 0.6
- skip: float32 [8192], P('ch'), may hold values from -1 to 1
- gain: float32 [8192], P('ch'), may hold values from 0.1 to 1.9
Outputs:
- normed: bfloat16 [8192, 16384], P('ch', 'ctx')
Inputs may be any that keep to these rules, and one draw needn't show every extreme that they name: `pole_rates`: decay rates, all positive.
All inputs are finite; a program needn't handle non-finite values.
Results may differ from a plain program's by a relative error of at most 0.001.
Values may be sent and summed in bfloat16 or wider, within the bound.
No kernel may reach another device: no remote copies, remote signals or barrier semaphores. Data moves between devices by JAX's collectives and lax.ppermute only.
A program may use at most 128 MiB of HBM per device.

v0:
```python
import jax
import jax.numpy as jnp
from jax import lax
from jax.sharding import Mesh
from jax.sharding import PartitionSpec as P

D = 8192
SHORT = 7
BLOCK = 128
CTX = ("ctx_0", "ctx_1", "ctx_2")
CH_CTX = ("ch", "ctx_0", "ctx_1", "ctx_2")


HIGHEST_PRECISION = lax.Precision.HIGHEST


def passed_along(array, axis, by):
    count = lax.axis_size(axis)
    pairs = [(i, i + by) for i in range(count) if 0 <= i + by < count]
    return lax.ppermute(array, axis, pairs)


def neutral_like(array, identity):
    return jax.tree.map(
        lambda part, zero: jnp.zeros_like(part) + jnp.asarray(zero, part.dtype), array, identity
    )


def carried_in(array, axes, combine, identity):
    before = start = neutral_like(array, identity)
    so_far = array
    for axis in reversed(axes):
        count, position = (lax.axis_size(axis), lax.axis_index(axis))
        pieces = jax.tree.map(lambda part: lax.all_gather(part, axis), so_far)
        inside, so_far = (start, start)
        for k in range(count):
            passed = k < position
            so_far = combine(so_far, jax.tree.map(lambda part: part[k], pieces))
            inside = jax.tree.map(lambda new, old: jnp.where(passed, new, old), so_far, inside)
        before = combine(inside, before)
    return before


def from_everyone(array, axis):
    count = lax.axis_size(axis)
    return lax.all_to_all(
        jnp.broadcast_to(array[None], (count, *array.shape)), axis, 0, 0, tiled=True
    )


def taken_together(array, axis):
    everything = from_everyone(array, axis)
    return jnp.sum(everything, axis=0)


def short_filter(extended, short_taps, groups, length):
    reach_back = short_taps.shape[2] - 1
    channels = extended.shape[1]
    shaped = extended.reshape(3, groups, channels // groups, extended.shape[2])
    summed = jnp.zeros((3, groups, channels // groups, length), jnp.float32)
    for offset in range(short_taps.shape[2]):
        window = shaped[:, :, :, reach_back - offset : reach_back - offset + length].astype(
            jnp.float32
        )
        summed = summed + short_taps[:, :, offset][:, :, None, None] * window
    return summed


def kernel_table(pole_rates, residues, block):
    row_index = jnp.arange(block, dtype=jnp.int32)[:, None]
    col_index = jnp.arange(block, dtype=jnp.int32)[None, :]
    lag_flat = (row_index - col_index).reshape(-1)
    step_values = jnp.arange(block, dtype=jnp.int32).astype(jnp.float32)
    modal_row = jnp.einsum(
        "gp,gpl->gl",
        residues,
        jnp.exp(-pole_rates[:, :, None] * step_values),
        precision=HIGHEST_PRECISION,
    )
    picker = (jnp.arange(block, dtype=jnp.int32)[:, None] == lag_flat[None, :]).astype(jnp.float32)
    table = jnp.dot(
        modal_row, picker, precision=HIGHEST_PRECISION, preferred_element_type=jnp.float32
    )
    return table.reshape(modal_row.shape[0], block, block)


def compose(earlier, later_pair):
    return (earlier[0] * later_pair[0], later_pair[0] * earlier[1] + later_pair[1])


def block_terms(product, kernel, pole_rates, block):
    groups, group_width, length = product.shape
    block_count = length // block
    current = product.reshape(groups, group_width, block_count, block)
    inner_part = jnp.einsum("gsnk,gik->gsni", current, kernel, precision=HIGHEST_PRECISION)
    reverse_steps = (block - 1 - jnp.arange(block, dtype=jnp.int32)).astype(jnp.float32)
    backward = jnp.exp(-pole_rates[:, :, None] * reverse_steps)
    end_states = jnp.einsum("gsnk,gpk->gsnp", current, backward, precision=HIGHEST_PRECISION)
    decays = jnp.broadcast_to(jnp.exp(-pole_rates * block)[:, None, None, :], end_states.shape)
    lifted, prefix = lax.associative_scan(compose, (decays, end_states), axis=2)
    return (inner_part, prefix)


def finish_terms(inner_part, prefix, state_in, pole_rates, residues, block):
    groups, group_width, block_count, block_size = inner_part.shape
    counts = jnp.arange(1, block_count + 1, dtype=jnp.int32).astype(jnp.float32) * block
    powers = jnp.exp(-pole_rates[:, None, :] * counts[None, :, None])
    after_block = prefix + powers[:, None, :, :] * state_in[:, :, None, :]
    starts = jnp.concatenate([state_in[:, :, None, :], after_block[:, :, :-1, :]], axis=2)
    lift_steps = jnp.arange(1, block + 1, dtype=jnp.int32).astype(jnp.float32)
    lift_table = residues[:, :, None] * jnp.exp(-pole_rates[:, :, None] * lift_steps)
    carried = jnp.einsum("gsnp,gpi->gsni", starts, lift_table, precision=HIGHEST_PRECISION)
    return (inner_part + carried).reshape(groups, group_width, block_count * block)


def shards(streams, short_taps, pole_rates, residues, skip, gain):
    relaid = lax.all_to_all(streams, CTX, split_axis=2, concat_axis=1, tiled=True)
    channels = relaid.shape[1]
    length = relaid.shape[2]
    groups = pole_rates.shape[0]
    group_width = channels // groups
    left_edge = passed_along(relaid[:, :, length - (SHORT - 1) :], CTX, 1)
    filtered = short_filter(
        jnp.concatenate([left_edge, relaid], axis=2), short_taps, groups, length
    )
    product = filtered[1] * filtered[2]
    kernel = kernel_table(pole_rates, residues, BLOCK)
    inner_part, prefix = block_terms(product, kernel, pole_rates, BLOCK)
    own_state = prefix[:, :, -1, :]
    device_decay = jnp.broadcast_to(jnp.exp(-pole_rates * length)[:, None, :], own_state.shape)
    lifted_decay, state_in = carried_in(
        (device_decay, own_state),
        CTX,
        compose,
        (jnp.ones_like(device_decay), jnp.zeros_like(own_state)),
    )
    convolved = finish_terms(inner_part, prefix, state_in, pole_rates, residues, BLOCK)
    gated_value = filtered[0] * (
        convolved + skip.reshape(groups, group_width)[:, :, None] * product
    )
    partial_sum = jnp.sum(gated_value * gated_value, axis=(0, 1))
    mean_square = taken_together(partial_sum, "ch") / D
    scaled = (
        gated_value.reshape(channels, length)
        * gain[:, None]
        * lax.rsqrt(mean_square + 1e-05)[None, :]
    )
    return scaled.astype(jnp.bfloat16)


def solution(mesh):
    torus = Mesh(mesh.devices.reshape(8, 4, 2, mesh.shape["ch"]), ("ctx_0", "ctx_1", "ctx_2", "ch"))
    in_specs = (
        P(None, CH_CTX, None),
        P(None, "ch", None),
        P("ch", None),
        P("ch", None),
        P("ch"),
        P("ch"),
    )
    out_specs = P("ch", CTX)
    return jax.shard_map(
        shards, mesh=torus, in_specs=in_specs, out_specs=out_specs, check_vma=False
    )
```

profile of v0, /device:TPU:2, one launch (start us, length us, event | category | flops | bytes accessed | tf_op | source)
XLA Modules:
  0.0 328.8 jit_solution(8692565533323603897)
XLA Ops:
  6.5 19.9 %copy.375 = bf16[3,32,16384]{1,0,2:T(4,128)(2,1)} copy(bf16[3,32,16384]{2,1,0:T(8,128)(2,1)} %param.6) | data formatting | bytes 6291456 | tf_op args[0]
  26.4 25.3 %reshape.625 = bf16[64,2,12288]{2,1,0:T(2,128)(2,1)} reshape(bf16[16384,3,32]{2,1,0:T(4,128)(2,1)} %bitcast.229) | data formatting | bytes 6291456
  51.7 12.1 %all-to-all-start = ((bf16[64,2,12288]{2,1,0:T(2,128)(2,1)}), bf16[64,2,12288]{2,1,0:T(2,128)(2,1)S(1)}, u32[]{:S(2)}, u32[]{:S(2)}) async-start(bf16[64,2,12288]{2,1,0:T(2,128)(2,1)} %reshape.625), calls=%async_computation | async-start | bytes 6291456 | tf_op jit(solution)/shard_map/all_to_all | solution.py:117
  66.5 12.3 %all-gather.2 = f32[512,16]{0,1:T(8,128)S(1)} all-gather(f32[128,16]{0,1:T(8,128)S(1)} %get-tuple-element.9), channel_id=6, replica_groups=mesh['ctx_0'=8,'ctx_1'=4,'ctx_2'=2,'ch'=4] {'ctx_1'}, dimensions={0}, use_global_device_ids=true | all-gather | bytes 40960 | tf_op jit(solution)/shard_map/all_gather | solution.py:34
  79.4 58.2 %all-to-all-done = bf16[64,2,12288]{2,1,0:T(2,128)(2,1)S(1)} async-done(((bf16[64,2,12288]{2,1,0:T(2,128)(2,1)}), bf16[64,2,12288]{2,1,0:T(2,128)(2,1)S(1)}, u32[]{:S(2)}, u32[]{:S(2)}) %all-to-all-start) | async-done | bytes 3145760 | tf_op jit(solution)/shard_map/all_to_all | solution.py:117
  137.6 18.4 %reshape.626 = bf16[16384,3,32]{2,1,0:T(4,128)(2,1)} reshape(bf16[64,2,12288]{2,1,0:T(2,128)(2,1)S(1)} %all-to-all-done) | data formatting | bytes 6291456
  156.0 19.0 %copy.409 = bf16[3,32,64,256]{3,1,2,0:T(8,128)(2,1)S(1)} copy(bf16[3,32,64,256]{1,0,3,2:T(4,128)(2,1)} %bitcast.228) | data formatting | bytes 6291456 | tf_op jit(solution)/shard_map/all_to_all | solution.py:117
  180.3 4.0 %collective-permute-done = bf16[3,2048,6]{1,2,0:T(8,128)(2,1)S(1)} collective-permute-done((bf16[3,2048,6]{1,2,0:T(8,128)(2,1)S(1)}, bf16[3,2048,6]{1,2,0:T(8,128)(2,1)S(1)}, u32[]{:S(2)}, u32[]{:S(2)}) %collective-permute-start) | collective-permute-done | bytes 73760 | tf_op jit(solution)/shard_map/ppermute | solution.py:20
  185.9 15.2 %multiply_add_fusion = f32[3,128,16,256]{3,2,1,0:T(8,128)S(1)} fusion(bf16[3,128,16,256]{3,2,1,0:T(8,128)(2,1)S(1)} %bitcast.232, bf16[3,128,16,6]{3,2,1,0:T(8,128)(2,1)} %bitcast.236, f32[3,128]{1,0:T(4,128)S(1)} %get-tuple-element.40, f32[3,128]{1,0:T(4,128)S(1)} %get-tuple-element.41, f32[3,128]{1,0:T(4,128)S(1)} %get-tuple-element.42, ...), kind=kLoop, calls=%fused_computation.9 | loop fusion | flops 59768832 | bytes 9521664 | tf_op jit(solution)/shard_map/add | solution.py:65
  206.2 3.2 copy.383
  209.4 3.7 %fusion.23 = f32[128,16,2,16]{3,1,2,0:T(8,128)S(1)} fusion(f32[128,16,2,128]{3,1,2,0:T(8,128)} %copy.383, f32[128]{0:T(128)S(1)} %subtract_convert_fusion, f32[128,16]{1,0:T(8,128)S(1)} %copy.382), kind=kOutput, calls=%fused_computation.38 | convolution fusion | flops 100925440 | bytes 2368000 | tf_op jit(solution)/shard_map/gsnk,gpk->gsnp/dot_general | solution.py:98
  218.9 13.7 %all_gather.26 = f32[4,128,16,16]{1,3,2,0:T(8,128)S(1)} all-gather(f32[1,128,16,16]{1,3,2,0:T(8,128)S(1)} %bitcast_add_fusion.16), channel_id=1, replica_groups=mesh['ctx_0'=8,'ctx_1'=4,'ctx_2'=2,'ch'=4] {'ctx_1'}, dimensions={0}, use_global_device_ids=true | all-gather | bytes 655360 | tf_op jit(solution)/shard_map/all_gather | solution.py:34
  237.7 4.4 %fusion.4 = f32[16,8,128,128]{3,1,2,0:T(8,128)S(1)} fusion(f32[128,128]{1,0:T(8,128)S(1)} %bitcast.240, s32[16384]{0:T(1024)S(1)} %subtract_bitcast_fusion), kind=kOutput, calls=%fused_computation.16 | convolution fusion | flops 3223322624 | bytes 8519680 | tf_op jit(solution)/shard_map/dot_general | solution.py:81
  242.2 4.7 %copy.421 = f32[16,8,128,128]{3,2,1,0:T(8,128)} copy(f32[16,8,128,128]{3,1,2,0:T(8,128)S(1)} %fusion.4) | data formatting | bytes 16777216
  246.9 24.8 %all-gather.3 = f32[1024,16]{0,1:T(8,128)S(1)} all-gather(f32[128,16]{0,1:T(8,128)S(1)} %copy-done.3), channel_id=8, replica_groups=mesh['ctx_0'=8,'ctx_1'=4,'ctx_2'=2,'ch'=4] {'ctx_0'}, dimensions={0}, use_global_device_ids=true | all-gather | bytes 73728 | tf_op jit(solution)/shard_map/all_gather | solution.py:34
  276.2 2.8 copy.398
  279.0 3.9 %fusion.21 = f32[128,16,2,128]{3,1,2,0:T(8,128)S(1)} fusion(f32[128,16,2,16]{3,1,2,0:T(8,128)} %copy.398, f32[128]{0:T(128)} %add_convert_fusion, f32[128,16]{1,0:T(8,128)S(1)} %copy.397, f32[128,16]{1,0:T(8,128)S(1)} %copy.382), kind=kOutput, calls=%fused_computation.36 | convolution fusion | flops 101187584 | bytes 2376192 | tf_op jit(solution)/shard_map/gsnp,gpi->gsni/dot_general | solution.py:112
  283.0 16.4 %fusion.18 = f32[128,16,2,128]{3,1,2,0:T(8,128)} fusion(f32[128,16,2,128]{3,1,2,0:T(8,128)S(1)} %fusion.21, f32[128,16,2,128]{3,1,2,0:T(8,128)S(1)} %copy-done.1, f32[128,128,128,1]{2,1,0,3:T(8,128)} %bitcast.230), kind=kOutput, calls=%fused_computation.35 | convolution fusion | flops 805830656 | bytes 14680064 | tf_op jit(solution)/shard_map/gsnk,gik->gsni/dot_general | solution.py:95
  299.4 2.9 copy.400
  302.3 3.1 copy.401
  305.4 2.7 fusion.17
  308.8 4.5 %all-to-all-start.1 = ((f32[4,1,256]{2,1,0:T(1,128)}), f32[4,1,256]{2,1,0:T(1,128)S(1)}, u32[]{:S(2)}, u32[]{:S(2)}) async-start(f32[4,1,256]{2,1,0:T(1,128)} %broadcast_in_dim.17), calls=%async_computation.1 | async-start | bytes 8192 | tf_op jit(solution)/shard_map/all_to_all | solution.py:46
  313.2 4.0 %copy.399 = f32[128,16,2,128]{3,2,1,0:T(2,128)} copy(f32[128,16,2,128]{3,1,2,0:T(8,128)} %fusion.18) | data formatting | bytes 4194304 | tf_op jit(solution)/shard_map/add | solution.py:113
  318.6 3.4 %fusion.13 = bf16[2048,256]{1,0:T(8,128)(2,1)} fusion(f32[256,8,2,128]{3,2,1,0:T(2,128)} %bitcast.235, f32[1,128,16,256]{3,2,1,0:T(8,128)S(1)} %get-tuple-element.13, f32[1,128,16,256]{3,2,1,0:T(8,128)} %get-tuple-element.12, f32[256]{0:T(256)S(1)} %add_rsqrt_fusion, f32[2048]{0:T(1024)S(1)} %copy-done.7, f32[2048]{0:T(1024)S(1)} %copy-done.4), kind=kLoop, calls=%fused_computation.27 | loop fusion | flops 3145728 | bytes 7357440 | tf_op jit(solution)/shard_map/convert_element_type | solution.py:148
  (63 shorter events, 32.6 us)
Async XLA Ops:
  51.7 12.2 %copy-start.5 = (f32[3,128,7]{1,2,0:T(8,128)S(1)}, f32[3,128,7]{1,2,0:T(8,128)}, u32[]{:S(2)}) copy-start(f32[3,128,7]{1,2,0:T(8,128)} %param.7) | copy-start | bytes 32260
  51.7 12.3 %copy-start.6 = (f32[128,16]{0,1:T(8,128)S(1)}, f32[128,16]{0,1:T(8,128)}, u32[]{:S(2)}) copy-start(f32[128,16]{0,1:T(8,128)} %param.8) | copy-start | bytes 24580
  51.7 85.9 %all-to-all-start = ((bf16[64,2,12288]{2,1,0:T(2,128)(2,1)}), bf16[64,2,12288]{2,1,0:T(2,128)(2,1)S(1)}, u32[]{:S(2)}, u32[]{:S(2)}) async-start(bf16[64,2,12288]{2,1,0:T(2,128)(2,1)} %reshape.625), calls=%async_computation | async-start | bytes 6291456 | tf_op jit(solution)/shard_map/all_to_all | solution.py:117
  63.9 209.0 %all-gather.6.cloned.1.call-start = ((), (), s32[]{:S(2)}) async-start(), calls=%async_computation.2 | async-start | bytes 1179648 | tf_op jit(solution)/shard_map/all_gather | solution.py:34
  178.4 5.9 %collective-permute-start = (bf16[3,2048,6]{1,2,0:T(8,128)(2,1)S(1)}, bf16[3,2048,6]{1,2,0:T(8,128)(2,1)S(1)}, u32[]{:S(2)}, u32[]{:S(2)}) collective-permute-start(bf16[3,2048,6]{1,2,0:T(8,128)(2,1)S(1)} %copy.379), channel_id=1, source_target_pairs={{0,4},{4,8},{8,12},{12,16},{16,20},{20,24},{24,28},{28,32},{32,36}... | collective-permute-start | bytes 221192 | tf_op jit(solution)/shard_map/ppermute | solution.py:20
  201.0 3.3 copy-start
  214.2 19.9 %copy-start.2 = (f32[128,16]{0,1:T(8,128)S(1)}, f32[128,16]{0,1:T(8,128)}, u32[]{:S(2)}) copy-start(f32[128,16]{0,1:T(8,128)} %param.9) | copy-start | bytes 24580
  242.2 4.7 %copy-start.3 = (f32[128,16]{0,1:T(8,128)S(1)}, f32[128,16]{0,1:T(8,128)}, u32[]{:S(2)}) copy-start(f32[128,16]{0,1:T(8,128)} %get-tuple-element.11) | copy-start | bytes 24580
  279.0 3.9 %copy-start.1 = (f32[128,16,2,128]{3,1,2,0:T(8,128)S(1)}, f32[128,16,2,128]{3,1,2,0:T(8,128)}, u32[]{:S(2)}) copy-start(f32[128,16,2,128]{3,1,2,0:T(8,128)} %copy.383) | copy-start | bytes 6291460
  308.1 10.4 %copy-start.4 = (f32[2048]{0:T(1024)S(1)}, f32[2048]{0:T(1024)}, u32[]{:S(2)}) copy-start(f32[2048]{0:T(1024)} %param.10) | copy-start | bytes 24580
  308.1 10.4 %copy-start.7 = (f32[2048]{0:T(1024)S(1)}, f32[2048]{0:T(1024)}, u32[]{:S(2)}) copy-start(f32[2048]{0:T(1024)} %param.11) | copy-start | bytes 24580
  308.8 9.8 %all-to-all-start.1 = ((f32[4,1,256]{2,1,0:T(1,128)}), f32[4,1,256]{2,1,0:T(1,128)S(1)}, u32[]{:S(2)}, u32[]{:S(2)}) async-start(f32[4,1,256]{2,1,0:T(1,128)} %broadcast_in_dim.17), calls=%async_computation.1 | async-start | bytes 8192 | tf_op jit(solution)/shard_map/all_to_all | solution.py:46
Sparse Core Ops, SparseCore 0:
  233.5 37.0 all-gather.5
where the time goes:
time: 331 us; the launch traced here: 329 us
  local copies, waits for them, and re-layouts  117 us (35%)
  waiting for transfers between devices  63.5 us (19%)
  blocking collectives  54.6 us (16%)
  other arithmetic  31 us (9%)
  matrix products  30.4 us (9%)
  starting transfers between devices  18.6 us (6%)
  between operations  13.7 us (4%)
    unnamed x28, local copies, waits for them, and re-layouts  72 us
    all_to_all x1, waiting for transfers between devices, shards(): lax.all_to_all(streams, CTX, split_axis=2, concat_axis=1, tiled=True)  58.2 us
    all_gather x5, blocking collectives, carried_in(): pieces = jax.tree.map(lambda part: lax.all_gather(part, axis), so_far)  54.6 us
    all_to_all x1, local copies, waits for them, and re-layouts, shards(): lax.all_to_all(streams, CTX, split_axis=2, concat_axis=1, tiled=True)  19 us
    dot_general x1, matrix products, block_terms(): jnp.einsum('gsnk,gik->gsni', current, kernel, precision=HIGHEST_PRECISION)  16.4 us
    add x1, other arithmetic, short_filter(): summed = summed + short_taps[:, :, offset][:, :, None, None] * window  15.2 us
    all_to_all x1, starting transfers between devices, shards(): lax.all_to_all(streams, CTX, split_axis=2, concat_axis=1, tiled=True)  12.1 us
    add x2, local copies, waits for them, and re-layouts, finish_terms(): inner_part + carried  6.94 us
  transfers between devices with their start and end apart: 4, of which 3 were waited for; matrix products, arithmetic and copies ran while one was open for 6% of the time, Pallas kernels for 0%

commit v1 on v0

v1 whole, which is shorter than its diff:
```python
import jax
import jax.numpy as jnp
from jax import lax
from jax.experimental import pallas as pl
from jax.experimental.pallas import tpu as pltpu
from jax.sharding import Mesh
from jax.sharding import PartitionSpec as P

D = 8192
SHORT = 7
BLOCK = 128
WIDTH = 16
CTX = ("ctx_0", "ctx_1", "ctx_2")
CH_CTX = ("ch", "ctx_0", "ctx_1", "ctx_2")
CHUNK = 32


def split(value):
    high = value.astype(jnp.bfloat16)
    low = (value - high.astype(jnp.float32)).astype(jnp.bfloat16)
    return high, low


def column_of(row):
    width = row.shape[1]
    rows = lax.broadcasted_iota(jnp.int32, (width, width), 0)
    cols = lax.broadcasted_iota(jnp.int32, (width, width), 1)
    return jnp.sum(jnp.where(rows == cols, row, 0.0), axis=1, keepdims=True)


def toeplitz(row, rows):
    spread = jnp.broadcast_to(row, (rows, row.shape[1]))
    return pltpu.roll(spread, 0, 1, stride=1, stride_axis=0)


def mix_kernel(
    place, streams, short_taps, rates, residues, skip, gated_out, square_out,
    taps_w, conv_w, lift_w, first, direct, ends, starts, squares,
):
    blocks = streams.shape[2] // BLOCK
    group = place[0] * pl.num_programs(0) + pl.program_id(0)
    rate = column_of(rates[pl.ds(group, 1), :])
    residue = column_of(residues[pl.ds(group, 1), :])
    skip_column = column_of(skip[pl.ds(group, 1), :])
    zero = jnp.zeros((BLOCK, BLOCK), jnp.bfloat16)

    for m in range(3):
        taps = short_taps[m, pl.ds(group, 1), :]
        row = jnp.concatenate([taps, jnp.zeros((1, 2 * BLOCK - SHORT), jnp.float32)], axis=1)
        high, low = split(toeplitz(row, 2 * BLOCK)[:, BLOCK:])
        taps_w[m] = jnp.concatenate([high, low], axis=1)

    steps = lax.broadcasted_iota(jnp.int32, (WIDTH, BLOCK), 1).astype(jnp.float32)
    kernel_row = jnp.sum(residue * jnp.exp(-rate * steps), axis=0, keepdims=True)
    lags = toeplitz(kernel_row, BLOCK)
    at_row = lax.broadcasted_iota(jnp.int32, (BLOCK, BLOCK), 0)
    at_col = lax.broadcasted_iota(jnp.int32, (BLOCK, BLOCK), 1)
    high, low = split(jnp.where(at_col >= at_row, lags, 0.0))
    conv_w[:, : 2 * BLOCK] = jnp.concatenate(
        [jnp.concatenate([high, low], axis=1), jnp.concatenate([high, zero], axis=1)], axis=0
    )
    backward = jnp.exp(-rate * (BLOCK - 1 - steps))
    thrice = jnp.concatenate(
        [backward, backward, backward, jnp.zeros((BLOCK - 3 * WIDTH, BLOCK), jnp.float32)], axis=0
    ).T
    high, low = split(thrice)
    conv_w[:, 2 * BLOCK :] = jnp.concatenate(
        [jnp.concatenate([high, low], axis=1), jnp.concatenate([high, zero], axis=1)], axis=0
    )
    high, low = split(residue * jnp.exp(-rate * (steps + 1.0)))
    lift_w[...] = jnp.concatenate(
        [high, high, low, jnp.zeros((BLOCK - 3 * WIDTH, BLOCK), jnp.bfloat16)], axis=0
    )

    skip_rows = jnp.broadcast_to(
        skip_column[None], (CHUNK, WIDTH, BLOCK)
    ).reshape(CHUNK * WIDTH, BLOCK)
    for chunk in range(blocks // CHUNK):
        span = pl.ds(chunk * CHUNK * WIDTH, CHUNK * WIDTH)
        filtered = []
        for m in range(3):
            pieces = []
            for n in range(chunk * CHUNK, (chunk + 1) * CHUNK):
                if n == 0:
                    here = streams[m, :, :BLOCK]
                    pieces.append(jnp.concatenate([jnp.zeros_like(here), here], axis=1))
                else:
                    pieces.append(streams[m, :, (n - 1) * BLOCK : (n + 1) * BLOCK])
            both = jnp.dot(
                jnp.concatenate(pieces, axis=0), taps_w[m], preferred_element_type=jnp.float32
            )
            filtered.append(both[:, :BLOCK] + both[:, BLOCK:])
        product = filtered[1] * filtered[2]
        high, low = split(product)
        terms = jnp.dot(
            jnp.concatenate([high, low], axis=1), conv_w[...], preferred_element_type=jnp.float32
        )
        first[span, :] = filtered[0]
        direct[span, :] = (terms[:, :BLOCK] + terms[:, BLOCK : 2 * BLOCK]) + skip_rows * product
        ends[span, :] = terms[:, 2 * BLOCK : 3 * BLOCK] + terms[:, 3 * BLOCK :]

    decay_row = jnp.exp(-rates[pl.ds(group, 1), :] * float(BLOCK))
    decay = jnp.broadcast_to(
        jnp.concatenate(
            [decay_row, decay_row, decay_row, jnp.zeros((1, BLOCK - 3 * WIDTH), jnp.float32)],
            axis=1,
        ),
        (WIDTH, BLOCK),
    )
    lane = lax.broadcasted_iota(jnp.int32, (WIDTH, BLOCK), 1)
    takes_low = (lane >= WIDTH) & (lane < 2 * WIDTH)
    state = jnp.zeros((WIDTH, BLOCK), jnp.float32)
    for n in range(blocks):
        high = state.astype(jnp.bfloat16).astype(jnp.float32)
        starts[pl.ds(n * WIDTH, WIDTH), :] = jnp.where(takes_low, state - high, high).astype(
            jnp.bfloat16
        )
        state = decay * state + ends[pl.ds(n * WIDTH, WIDTH), :]

    for chunk in range(blocks // CHUNK):
        span = pl.ds(chunk * CHUNK * WIDTH, CHUNK * WIDTH)
        carried = jnp.dot(starts[span, :], lift_w[...], preferred_element_type=jnp.float32)
        gated = first[span, :] * (direct[span, :] + carried)
        for k in range(CHUNK):
            n = chunk * CHUNK + k
            gated_out[n // 2, :, (n % 2) * BLOCK : (n % 2 + 1) * BLOCK] = gated[
                k * WIDTH : (k + 1) * WIDTH
            ]
        squared = (gated * gated).reshape(CHUNK, 2, 8, BLOCK)
        squared = squared[:, 0] + squared[:, 1]
        rows = pl.ds(chunk * CHUNK, CHUNK)

        @pl.when(pl.program_id(0) == 0)
        def _():
            squares[rows] = squared

        @pl.when(pl.program_id(0) != 0)
        def _():
            squares[rows] = squares[rows] + squared

    @pl.when(pl.program_id(0) == pl.num_programs(0) - 1)
    def _():
        square_out[...] = jnp.sum(squares[...], axis=1)


def mix(place, streams, short_taps, rates, residues, skip):
    channels, length = streams.shape[1:]
    blocks = length // BLOCK
    rows = blocks * WIDTH
    whole = lambda array: pl.BlockSpec(array.shape, lambda g, place: (0,) * array.ndim)
    return pl.pallas_call(
        mix_kernel,
        name="mix",
        grid_spec=pltpu.PrefetchScalarGridSpec(
            num_scalar_prefetch=1,
            grid=(channels // WIDTH,),
            in_specs=[
                pl.BlockSpec((3, WIDTH, length), lambda g, place: (0, g, 0)),
                whole(short_taps),
                whole(rates),
                whole(residues),
                whole(skip),
            ],
            out_specs=[
                pl.BlockSpec((blocks // 2, WIDTH, 2 * BLOCK), lambda g, place: (0, g, 0)),
                pl.BlockSpec((blocks, BLOCK), lambda g, place: (0, 0)),
            ],
            scratch_shapes=[
                pltpu.VMEM((3, 2 * BLOCK, 2 * BLOCK), jnp.bfloat16),
                pltpu.VMEM((2 * BLOCK, 4 * BLOCK), jnp.bfloat16),
                pltpu.VMEM((BLOCK, BLOCK), jnp.bfloat16),
                pltpu.VMEM((rows, BLOCK), jnp.float32),
                pltpu.VMEM((rows, BLOCK), jnp.float32),
                pltpu.VMEM((rows, BLOCK), jnp.float32),
                pltpu.VMEM((rows, BLOCK), jnp.bfloat16),
                pltpu.VMEM((blocks, 8, BLOCK), jnp.float32),
            ],
        ),
        out_shape=[
            jax.ShapeDtypeStruct((blocks // 2, channels, 2 * BLOCK), jnp.float32),
            jax.ShapeDtypeStruct((blocks, BLOCK), jnp.float32),
        ],
        compiler_params=pltpu.CompilerParams(dimension_semantics=("arbitrary",)),
    )(place, streams, short_taps, rates, residues, skip)


def shards(streams, short_taps, pole_rates, residues, skip, gain):
    channels = streams.shape[1]
    groups = pole_rates.shape[0]
    place = lax.axis_index(CTX)
    gated, squares = mix(
        place.reshape(1), streams, short_taps, pole_rates, residues, skip.reshape(groups, WIDTH)
    )
    mean_square = lax.psum(squares, CH_CTX) / D
    scale = lax.rsqrt(mean_square + 1e-05).reshape(gated.shape[0], 1, gated.shape[2])
    own_gain = lax.dynamic_slice(gain, (place * channels,), (channels,))
    normed = (gated * own_gain[None, :, None] * scale).astype(jnp.bfloat16)
    moved = lax.all_to_all(normed, CTX, split_axis=0, concat_axis=0, tiled=True)
    return moved.reshape(moved.shape[0] * channels, moved.shape[2])


def solution(mesh):
    torus = Mesh(mesh.devices.reshape(8, 4, 2, mesh.shape["ch"]), ("ctx_0", "ctx_1", "ctx_2", "ch"))
    in_specs = (
        P(None, CH_CTX, None),
        P(None, "ch", None),
        P("ch", None),
        P("ch", None),
        P("ch"),
        P("ch"),
    )
    out_specs = P("ch", CTX)
    return jax.shard_map(
        shards, mesh=torus, in_specs=in_specs, out_specs=out_specs, check_vma=False
    )
```

time: 331 us -> 311 us (0.940)
  waiting for transfers between devices: 63.5 us -> 243 us
  local copies, waits for them, and re-layouts: 117 us -> 7.51 us
  matrix products: 30.4 us -> 0 us
  other arithmetic: 31 us -> 2.85 us
  blocking collectives: 54.6 us -> 35.4 us
  starting transfers between devices: 18.6 us -> 0.01 us
  Pallas kernels: 0 us -> 7.7 us
    psum x0 -> x1, waiting for transfers between devices: none -> 243 us  [shards(): mean_square = lax.psum(squares, CH_CTX) / D]
    unnamed x28 -> x4, local copies, waits for them, and re-layouts: 72 us -> 5.32 us
    all_to_all x2 -> x0, waiting for transfers between devices: 59.5 us -> none  [the longest x1 58.2 us: shards(): lax.all_to_all(streams, CTX, split_axis=2, concat_axis=1, tiled=True)]
    all_gather x5 -> x0, blocking collectives: 54.6 us -> none  [carried_in(): pieces = jax.tree.map(lambda part: lax.all_gather(part, axis), so_far)]
    all_to_all x0 -> x1, blocking collectives: none -> 35.4 us  [shards(): moved = lax.all_to_all(normed, CTX, split_axis=0, concat_axis=0, tiled=True)]
    dot_general x5 -> x0, matrix products: 30.4 us -> none  [the longest x1 16.4 us: block_terms(): jnp.einsum('gsnk,gik->gsni', current, kernel, precision=HIGHEST_PRECISION)]
    add x8 -> x0, other arithmetic: 20 us -> none  [the longest x1 15.2 us: short_filter(): summed = summed + short_taps[:, :, offset][:, :, None, None] * window]
    all_to_all x1 -> x0, local copies, waits for them, and re-layouts: 19 us -> none  [shards(): lax.all_to_all(streams, CTX, split_axis=2, concat_axis=1, tiled=True)]
  transfers between devices with their start and end apart: 4 -> 1, of which waited for: 3 -> 1; matrix products, arithmetic and copies ran while one was open for 6% -> 0% of each run, Pallas kernels for 0% -> 0%
where the time goes in v1:
time: 311 us; the launch traced here: 310 us
  waiting for transfers between devices  243 us (78%)
  blocking collectives  35.4 us (11%)
  between operations  13.4 us (4%)
  Pallas kernels  7.7 us (2%)
  local copies, waits for them, and re-layouts  7.51 us (2%)
    psum x1, waiting for transfers between devices, shards(): mean_square = lax.psum(squares, CH_CTX) / D  243 us
    all_to_all x1, blocking collectives, shards(): moved = lax.all_to_all(normed, CTX, split_axis=0, concat_axis=0, tiled=True)  35.4 us
    pallas_call x1, Pallas kernels, mix(): pl.pallas_call(mix_kernel, name='mix', grid_spec=pltpu.PrefetchScalarGrid...  7.7 us
  transfers between devices with their start and end apart: 1, of which 1 were waited for; matrix products, arithmetic and copies ran while one was open for 0% of the time, Pallas kernels for 0%

profile of v1, /device:TPU:2, one launch (start us, length us, event | category | flops | bytes accessed | tf_op | source)
XLA Modules:
  0.0 309.8 jit_solution(12659338142936851833)
XLA Ops:
  6.5 0.0 all-reduce.2.cloned.1.call-start
  6.5 1.4 copy.11.rates
  7.9 1.4 copy.12.residues
  9.4 1.4 reshape.13.skip
  10.8 1.5 copy.10.short_taps
  12.3 7.7 %mix.1 = (f32[64,32,256]{2,1,0:T(8,128)}, f32[128,128]{1,0:T(8,128)}) custom-call(s32[1]{0:T(128)} %bitcast.place, bf16[3,32,16384]{2,1,0:T(8,128)(2,1)} %streams.1, f32[3,128,7]{2,1,0:T(8,128)} %copy.10.short_taps, f32[128,16]{1,0:T(8,128)} %copy.11.rates, f32[128,16]{1,0:T(8,128)} %copy.12.residues, f32[128,16]{1,0:T(8,128)} %reshape.13.skip), custom_call_target="tpu_custom_call" | custom-call | tf_op jit(solution)/shard_map/mix/pallas_call | solution.py:151
  20.0 0.0 all-reduce.2.cloned.1.call-update
  20.0 0.8 dynamic_slice.3
  20.8 242.9 %all-reduce.2.cloned.1.call-done = f32[128,128]{1,0:T(8,128)} async-done(((f32[128,128]{1,0:T(8,128)}), f32[128,128]{1,0:T(8,128)}) %all-reduce.2.cloned.1.call-update) | async-done | bytes 65552 | tf_op jit(solution)/shard_map/psum | solution.py:194
  263.7 0.9 add_rsqrt_fusion
  264.6 2.0 multiply_convert_fusion
  266.6 35.4 %all_to_all.5 = bf16[64,32,256]{2,1,0:T(8,128)(2,1)S(1)} all-to-all(bf16[64,32,256]{2,1,0:T(8,128)(2,1)S(1)} %multiply_convert_fusion), channel_id=1, replica_groups=mesh['ctx_0'=8,'ctx_1'=4,'ctx_2'=2,'ch'=4] {'ctx_0','ctx_1','ctx_2'}, dimensions={0} | all-to-all | bytes 2097152 | tf_op jit(solution)/shard_map/all_to_all | solution.py:198
  302.0 1.0 copy.15
  (1 shorter events, 0.0 us)
Async XLA Ops:
  6.5 257.2 %all-reduce.2.cloned.1.call-start = ((), (), s32[]{:S(2)}) async-start(), calls=%async_computation.1 | async-start | bytes 131072 | tf_op jit(solution)/shard_map/psum | solution.py:194
Sparse Core Ops, SparseCore 0:
  20.1 243.4 all-reduce.1

commit v2 on v1

--- a/solution.py
+++ b/solution.py
@@ -13,6 +13,8 @@
 CTX = ("ctx_0", "ctx_1", "ctx_2")
 CH_CTX = ("ch", "ctx_0", "ctx_1", "ctx_2")
 CHUNK = 32
+TOP = 32768.0
+TINY = 1e-37
 
 
 def split(value):
@@ -21,11 +23,22 @@
     return high, low
 
 
-def column_of(row):
-    width = row.shape[1]
-    rows = lax.broadcasted_iota(jnp.int32, (width, width), 0)
-    cols = lax.broadcasted_iota(jnp.int32, (width, width), 1)
-    return jnp.sum(jnp.where(rows == cols, row, 0.0), axis=1, keepdims=True)
+def picked_column(array, first, step):
+    rows = lax.broadcasted_iota(jnp.int32, (array.shape[0], BLOCK), 0)
+    cols = lax.broadcasted_iota(jnp.int32, (array.shape[0], BLOCK), 1)
+    return jnp.sum(jnp.where(cols == first + step * rows, array, 0.0), axis=1, keepdims=True)
+
+
+def row_of(column, lanes):
+    rows = lax.broadcasted_iota(jnp.int32, (column.shape[0], lanes), 0)
+    cols = lax.broadcasted_iota(jnp.int32, (column.shape[0], lanes), 1)
+    return jnp.sum(jnp.where(rows == cols, column, 0.0), axis=0, keepdims=True)
+
+
+def channel_column(ref, group):
+    per_row = BLOCK // WIDTH
+    row = jnp.broadcast_to(ref[pl.ds(group // per_row, 1), :], (WIDTH, BLOCK))
+    return picked_column(row, (group % per_row) * WIDTH, 1)
 
 
 def toeplitz(row, rows):
@@ -34,19 +47,19 @@
 
 
 def mix_kernel(
-    place, streams, short_taps, rates, residues, skip, gated_out, square_out,
-    taps_w, conv_w, lift_w, first, direct, ends, starts, squares,
+    place, streams, short_taps, rates, residues, skip, gain, gated_out, side_out,
+    taps_w, conv_w, lift_w, first, direct, ends, starts, squares, peaks,
 ):
     blocks = streams.shape[2] // BLOCK
     group = place[0] * pl.num_programs(0) + pl.program_id(0)
-    rate = column_of(rates[pl.ds(group, 1), :])
-    residue = column_of(residues[pl.ds(group, 1), :])
-    skip_column = column_of(skip[pl.ds(group, 1), :])
+    rate = picked_column(rates[...], group, 0)
+    residue = picked_column(residues[...], group, 0)
+    skip_column = channel_column(skip, group)
+    gain_column = channel_column(gain, group)
     zero = jnp.zeros((BLOCK, BLOCK), jnp.bfloat16)
 
     for m in range(3):
-        taps = short_taps[m, pl.ds(group, 1), :]
-        row = jnp.concatenate([taps, jnp.zeros((1, 2 * BLOCK - SHORT), jnp.float32)], axis=1)
+        row = row_of(picked_column(short_taps[m], group, 0), 2 * BLOCK)
         high, low = split(toeplitz(row, 2 * BLOCK)[:, BLOCK:])
         taps_w[m] = jnp.concatenate([high, low], axis=1)
 
@@ -74,6 +87,9 @@
 
     skip_rows = jnp.broadcast_to(
         skip_column[None], (CHUNK, WIDTH, BLOCK)
+    ).reshape(CHUNK * WIDTH, BLOCK)
+    gain_rows = jnp.broadcast_to(
+        gain_column[None], (CHUNK, WIDTH, BLOCK)
     ).reshape(CHUNK * WIDTH, BLOCK)
     for chunk in range(blocks // CHUNK):
         span = pl.ds(chunk * CHUNK * WIDTH, CHUNK * WIDTH)
@@ -99,13 +115,9 @@
         direct[span, :] = (terms[:, :BLOCK] + terms[:, BLOCK : 2 * BLOCK]) + skip_rows * product
         ends[span, :] = terms[:, 2 * BLOCK : 3 * BLOCK] + terms[:, 3 * BLOCK :]
 
-    decay_row = jnp.exp(-rates[pl.ds(group, 1), :] * float(BLOCK))
+    decay_column = jnp.exp(-rate * float(BLOCK))
     decay = jnp.broadcast_to(
-        jnp.concatenate(
-            [decay_row, decay_row, decay_row, jnp.zeros((1, BLOCK - 3 * WIDTH), jnp.float32)],
-            axis=1,
-        ),
-        (WIDTH, BLOCK),
+        row_of(jnp.concatenate([decay_column] * 3, axis=0), BLOCK), (WIDTH, BLOCK)
     )
     lane = lax.broadcasted_iota(jnp.int32, (WIDTH, BLOCK), 1)
     takes_low = (lane >= WIDTH) & (lane < 2 * WIDTH)
@@ -121,32 +133,43 @@
         span = pl.ds(chunk * CHUNK * WIDTH, CHUNK * WIDTH)
         carried = jnp.dot(starts[span, :], lift_w[...], preferred_element_type=jnp.float32)
         gated = first[span, :] * (direct[span, :] + carried)
+        gained = gated * gain_rows
         for k in range(CHUNK):
             n = chunk * CHUNK + k
-            gated_out[n // 2, :, (n % 2) * BLOCK : (n % 2 + 1) * BLOCK] = gated[
+            gated_out[n // 2, :, (n % 2) * BLOCK : (n % 2 + 1) * BLOCK] = gained[
                 k * WIDTH : (k + 1) * WIDTH
             ]
         squared = (gated * gated).reshape(CHUNK, 2, 8, BLOCK)
         squared = squared[:, 0] + squared[:, 1]
+        size = jnp.abs(gained).reshape(CHUNK, 2, 8, BLOCK)
+        size = jnp.maximum(size[:, 0], size[:, 1])
         rows = pl.ds(chunk * CHUNK, CHUNK)
 
         @pl.when(pl.program_id(0) == 0)
         def _():
             squares[rows] = squared
+            peaks[rows] = size
 
         @pl.when(pl.program_id(0) != 0)
         def _():
             squares[rows] = squares[rows] + squared
+            peaks[rows] = jnp.maximum(peaks[rows], size)
 
     @pl.when(pl.program_id(0) == pl.num_programs(0) - 1)
     def _():
-        square_out[...] = jnp.sum(squares[...], axis=1)
-
-
-def mix(place, streams, short_taps, rates, residues, skip):
+        side_out[0] = jnp.sum(squares[...], axis=1)
+        side_out[1] = jnp.maximum(jnp.max(peaks[...], axis=1), TINY)
+
+
+def mix(place, streams, short_taps, rates, residues, skip, gain):
     channels, length = streams.shape[1:]
     blocks = length // BLOCK
     rows = blocks * WIDTH
+    short_taps = short_taps.transpose(0, 2, 1)
+    rates = rates.T
+    residues = residues.T
+    skip = skip.reshape(-1, BLOCK)
+    gain = gain.reshape(-1, BLOCK)
     whole = lambda array: pl.BlockSpec(array.shape, lambda g, place: (0,) * array.ndim)
     return pl.pallas_call(
         mix_kernel,
@@ -160,10 +183,11 @@
                 whole(rates),
                 whole(residues),
                 whole(skip),
+                whole(gain),
             ],
             out_specs=[
                 pl.BlockSpec((blocks // 2, WIDTH, 2 * BLOCK), lambda g, place: (0, g, 0)),
-                pl.BlockSpec((blocks, BLOCK), lambda g, place: (0, 0)),
+                pl.BlockSpec((2, blocks, BLOCK), lambda g, place: (0, 0, 0)),
             ],
             scratch_shapes=[
                 pltpu.VMEM((3, 2 * BLOCK, 2 * BLOCK), jnp.bfloat16),
@@ -174,29 +198,42 @@
                 pltpu.VMEM((rows, BLOCK), jnp.float32),
                 pltpu.VMEM((rows, BLOCK), jnp.bfloat16),
                 pltpu.VMEM((blocks, 8, BLOCK), jnp.float32),
+                pltpu.VMEM((blocks, 8, BLOCK), jnp.float32),
             ],
         ),
         out_shape=[
             jax.ShapeDtypeStruct((blocks // 2, channels, 2 * BLOCK), jnp.float32),
-            jax.ShapeDtypeStruct((blocks, BLOCK), jnp.float32),
+            jax.ShapeDtypeStruct((2, blocks, BLOCK), jnp.float32),
         ],
         compiler_params=pltpu.CompilerParams(dimension_semantics=("arbitrary",)),
-    )(place, streams, short_taps, rates, residues, skip)
+    )(place, streams, short_taps, rates, residues, skip, gain)
+
+
+def from_everyone(array, axis):
+    count = lax.axis_size(axis)
+    return lax.all_to_all(
+        jnp.broadcast_to(array[None], (count, *array.shape)), axis, 0, 0, tiled=True
+    )
 
 
 def shards(streams, short_taps, pole_rates, residues, skip, gain):
     channels = streams.shape[1]
-    groups = pole_rates.shape[0]
     place = lax.axis_index(CTX)
-    gated, squares = mix(
-        place.reshape(1), streams, short_taps, pole_rates, residues, skip.reshape(groups, WIDTH)
-    )
-    mean_square = lax.psum(squares, CH_CTX) / D
-    scale = lax.rsqrt(mean_square + 1e-05).reshape(gated.shape[0], 1, gated.shape[2])
-    own_gain = lax.dynamic_slice(gain, (place * channels,), (channels,))
-    normed = (gated * own_gain[None, :, None] * scale).astype(jnp.bfloat16)
-    moved = lax.all_to_all(normed, CTX, split_axis=0, concat_axis=0, tiled=True)
-    return moved.reshape(moved.shape[0] * channels, moved.shape[2])
+    gained, side = mix(
+        place.reshape(1), streams, short_taps, pole_rates, residues, skip, gain
+    )
+    owners, channels, length = gained.shape
+    side = side.reshape(2, owners, length)
+    small = lax.all_to_all(side.transpose(1, 0, 2), CTX, 0, 0, tiled=True)
+    own = jnp.sum(small[:, 0], axis=0)
+    mean_square = jnp.sum(from_everyone(own, "ch"), axis=0) / D
+    scale = small[:, 1] * (TOP**-0.5 * lax.rsqrt(mean_square + 1e-05))[None]
+    part = gained * (1.0 / side[1])[:, None, :]
+    coded = (part * jnp.abs(part) * TOP).astype(jnp.float16)
+    moved = lax.all_to_all(coded, CTX, 0, 0, tiled=True).astype(jnp.float32)
+    size = jnp.sqrt(jnp.abs(moved))
+    normed = jnp.where(moved < 0, -size, size) * scale[:, None, :]
+    return normed.astype(jnp.bfloat16).reshape(owners * channels, length)
 
 
 def solution(mesh):

time: 311 us -> 79.5 us (0.26)
  waiting for transfers between devices: 243 us -> 40.1 us
  blocking collectives: 35.4 us -> 0 us
  starting transfers between devices: 0.01 us -> 22.1 us
  between operations: 13.4 us -> 0.06 us
  local copies, waits for them, and re-layouts: 7.51 us -> 2.33 us
    psum x1 -> x0, waiting for transfers between devices: 243 us -> none  [shards(): mean_square = lax.psum(squares, CH_CTX) / D]
    all_to_all x0 -> x3, waiting for transfers between devices: none -> 40.1 us  [the longest x1 28.7 us: shards(): moved = lax.all_to_all(coded, CTX, 0, 0, tiled=True).astype(jnp.float32)]
    all_to_all x1 -> x0, blocking collectives: 35.4 us -> none  [shards(): moved = lax.all_to_all(normed, CTX, split_axis=0, concat_axis=0, tiled=True)]
    all_to_all x0 -> x3, starting transfers between devices: none -> 22.1 us  [the longest x1 12 us: shards(): small = lax.all_to_all(side.transpose(1, 0, 2), CTX, 0, 0, tiled=True)]
    unnamed x4 -> x1, local copies, waits for them, and re-layouts: 5.32 us -> 0.01 us
  transfers between devices with their start and end apart: 1 -> 3, of which waited for: 1 -> 3; matrix products, arithmetic and copies ran while one was open for 0% -> 5% of each run, Pallas kernels for 0% -> 0%
where the time goes in v2:
time: 79.5 us; the launch traced here: 78.7 us
  waiting for transfers between devices  40.1 us (50%)
  starting transfers between devices  22.1 us (28%)
  Pallas kernels  8.15 us (10%)
  other arithmetic  5.95 us (7%)
  local copies, waits for them, and re-layouts  2.33 us (3%)
    all_to_all x1, waiting for transfers between devices, shards(): moved = lax.all_to_all(coded, CTX, 0, 0, tiled=True).astype(jnp.float32)  28.7 us
    all_to_all x1, starting transfers between devices, shards(): small = lax.all_to_all(side.transpose(1, 0, 2), CTX, 0, 0, tiled=True)  12 us
    all_to_all x1, waiting for transfers between devices, shards(): small = lax.all_to_all(side.transpose(1, 0, 2), CTX, 0, 0, tiled=True)  9.04 us
    pallas_call x1, Pallas kernels, mix(): pl.pallas_call(mix_kernel, name='mix', grid_spec=pltpu.PrefetchScalarGrid...  8.15 us
    all_to_all x1, starting transfers between devices, shards(): moved = lax.all_to_all(coded, CTX, 0, 0, tiled=True).astype(jnp.float32)  5.66 us
    all_to_all x1, starting transfers between devices, from_everyone(): lax.all_to_all(jnp.broadcast_to(array[None], (count, *array.shape)), axis...  4.47 us
    convert_element_type x1, other arithmetic, shards(): coded = (part * jnp.abs(part) * TOP).astype(jnp.float16)  2.99 us
    all_to_all x1, waiting for transfers between devices, from_everyone(): lax.all_to_all(jnp.broadcast_to(array[None], (count, *array.shape)), axis...  2.3 us
  transfers between devices with their start and end apart: 3, of which 3 were waited for; matrix products, arithmetic and copies ran while one was open for 5% of the time, Pallas kernels for 0%

profile of v2, /device:TPU:2, one launch (start us, length us, event | category | flops | bytes accessed | tf_op | source)
XLA Modules:
  0.0 78.7 jit_solution(14985428006473889501)
XLA Ops:
  0.0 8.1 %mix.1 = (f32[64,32,256]{2,1,0:T(8,128)}, f32[2,128,128]{2,1,0:T(8,128)}) custom-call(s32[1]{0:T(128)} %bitcast.place, bf16[3,32,16384]{2,1,0:T(8,128)(2,1)} %streams.1, f32[3,7,128]{2,1,0:T(8,128)} %bitcast.14, f32[16,128]{1,0:T(8,128)} %bitcast.15, f32[16,128]{1,0:T(8,128)} %bitcast.16, f32[16,128]{1,0:T(8,128)} %bitcast.17, f32[16,128]{1,0:T(8,128)} %bitcast.18), custom_call_target="tpu_custom_call" | custom-call | tf_op jit(solution)/shard_map/mix/pallas_call | solution.py:174
  8.2 0.9 %reshape.45 = f32[2,64,256]{2,1,0:T(8,128)S(1)} reshape(f32[2,128,128]{2,1,0:T(8,128)} %get-tuple-element.8) | data formatting | bytes 262144 | tf_op jit(solution)/shard_map/reshape | solution.py:226
  9.1 0.8 copy.15
  9.9 12.0 %all-to-all-start.1 = ((f32[64,2,256]{2,1,0:T(2,128)}), f32[64,2,256]{2,1,0:T(2,128)S(1)}, u32[]{:S(2)}, u32[]{:S(2)}) async-start(f32[64,2,256]{2,1,0:T(2,128)} %bitcast.11), calls=%async_computation.1 | async-start | bytes 262144 | tf_op jit(solution)/shard_map/all_to_all | solution.py:227
  21.9 0.9 %slice_divide_fusion = f32[1,128,128]{2,1,0:T(8,128)S(1)} fusion(f32[2,128,128]{2,1,0:T(8,128)} %get-tuple-element.8), kind=kLoop, calls=%fused_computation.13 | loop fusion | flops 16384 | bytes 131072 | tf_op jit(solution)/shard_map/div | solution.py:231
  22.8 9.0 %all-to-all-done.1 = f32[64,2,256]{2,1,0:T(2,128)S(1)} async-done(((f32[64,2,256]{2,1,0:T(2,128)}), f32[64,2,256]{2,1,0:T(2,128)S(1)}, u32[]{:S(2)}, u32[]{:S(2)}) %all-to-all-start.1) | async-done | bytes 131104 | tf_op jit(solution)/shard_map/all_to_all | solution.py:227
  31.8 0.1 slice_reduce_fusion
  31.9 0.6 broadcast_in_dim.2
  32.5 4.5 %all-to-all-start.2 = ((f32[4,1,256]{2,1,0:T(1,128)}), f32[4,1,256]{2,1,0:T(1,128)S(1)}, u32[]{:S(2)}, u32[]{:S(2)}) async-start(f32[4,1,256]{2,1,0:T(1,128)} %broadcast_in_dim.2), calls=%async_computation.2 | async-start | bytes 8192 | tf_op jit(solution)/shard_map/all_to_all | solution.py:214
  37.0 3.0 %fusion.2 = f16[64,32,256]{2,1,0:T(8,128)(2,1)} fusion(f32[64,32,256]{2,1,0:T(8,128)} %get-tuple-element.7, f32[64,256]{1,0:T(8,128)S(1)} %div.21), kind=kLoop, calls=%fused_computation.6 | loop fusion | flops 2621440 | bytes 3211264 | tf_op jit(solution)/shard_map/convert_element_type | solution.py:232
  39.9 2.3 %all-to-all-done.2 = f32[4,1,256]{2,1,0:T(1,128)S(1)} async-done(((f32[4,1,256]{2,1,0:T(1,128)}), f32[4,1,256]{2,1,0:T(1,128)S(1)}, u32[]{:S(2)}, u32[]{:S(2)}) %all-to-all-start.2) | async-done | bytes 4128 | tf_op jit(solution)/shard_map/all_to_all | solution.py:214
  42.2 5.7 %all-to-all-start = ((f16[64,32,256]{2,1,0:T(8,128)(2,1)}), f16[64,32,256]{2,1,0:T(8,128)(2,1)S(1)}, u32[]{:S(2)}, u32[]{:S(2)}) async-start(f16[64,32,256]{2,1,0:T(8,128)(2,1)} %fusion.2), calls=%async_computation | async-start | bytes 2097152 | tf_op jit(solution)/shard_map/all_to_all | solution.py:233
  47.9 0.1 slice_multiply_fusion
  48.0 28.7 %all-to-all-done = f16[64,32,256]{2,1,0:T(8,128)(2,1)S(1)} async-done(((f16[64,32,256]{2,1,0:T(8,128)(2,1)}), f16[64,32,256]{2,1,0:T(8,128)(2,1)S(1)}, u32[]{:S(2)}, u32[]{:S(2)}) %all-to-all-start) | async-done | bytes 1048608 | tf_op jit(solution)/shard_map/all_to_all | solution.py:233
  76.8 1.9 %fusion.4 = bf16[64,32,256]{2,1,0:T(8,128)(2,1)} fusion(f16[64,32,256]{2,1,0:T(8,128)(2,1)S(1)} %all-to-all-done, f32[64,256]{1,0:T(8,128)S(1)} %bitcast.13), kind=kLoop, calls=%fused_computation.8 | loop fusion | flops 3670016 | bytes 2162688 | tf_op jit(solution)/shard_map/convert_element_type | solution.py:236
  (4 shorter events, 0.1 us)
Async XLA Ops:
  9.9 21.9 %all-to-all-start.1 = ((f32[64,2,256]{2,1,0:T(2,128)}), f32[64,2,256]{2,1,0:T(2,128)S(1)}, u32[]{:S(2)}, u32[]{:S(2)}) async-start(f32[64,2,256]{2,1,0:T(2,128)} %bitcast.11), calls=%async_computation.1 | async-start | bytes 262144 | tf_op jit(solution)/shard_map/all_to_all | solution.py:227
  32.5 9.8 %all-to-all-start.2 = ((f32[4,1,256]{2,1,0:T(1,128)}), f32[4,1,256]{2,1,0:T(1,128)S(1)}, u32[]{:S(2)}, u32[]{:S(2)}) async-start(f32[4,1,256]{2,1,0:T(1,128)} %broadcast_in_dim.2), calls=%async_computation.2 | async-start | bytes 8192 | tf_op jit(solution)/shard_map/all_to_all | solution.py:214
  42.2 34.5 %all-to-all-start = ((f16[64,32,256]{2,1,0:T(8,128)(2,1)}), f16[64,32,256]{2,1,0:T(8,128)(2,1)S(1)}, u32[]{:S(2)}, u32[]{:S(2)}) async-start(f16[64,32,256]{2,1,0:T(8,128)(2,1)} %fusion.2), calls=%async_computation | async-start | bytes 2097152 | tf_op jit(solution)/shard_map/all_to_all | solution.py:233

commit v3 on v2

--- a/solution.py
+++ b/solution.py
@@ -15,6 +15,7 @@
 CHUNK = 32
 TOP = 32768.0
 TINY = 1e-37
+AT_ONCE = 8
 
 
 def split(value):
@@ -47,8 +48,8 @@
 
 
 def mix_kernel(
-    place, streams, short_taps, rates, residues, skip, gain, gated_out, side_out,
-    taps_w, conv_w, lift_w, first, direct, ends, starts, squares, peaks,
+    place, streams, short_taps, rates, residues, skip, gain, coded_out,
+    taps_w, conv_w, lift_w, first, direct, ends, starts, squares, peaks, gained, rows_in,
 ):
     blocks = streams.shape[2] // BLOCK
     group = place[0] * pl.num_programs(0) + pl.program_id(0)
@@ -133,15 +134,11 @@
         span = pl.ds(chunk * CHUNK * WIDTH, CHUNK * WIDTH)
         carried = jnp.dot(starts[span, :], lift_w[...], preferred_element_type=jnp.float32)
         gated = first[span, :] * (direct[span, :] + carried)
-        gained = gated * gain_rows
-        for k in range(CHUNK):
-            n = chunk * CHUNK + k
-            gated_out[n // 2, :, (n % 2) * BLOCK : (n % 2 + 1) * BLOCK] = gained[
-                k * WIDTH : (k + 1) * WIDTH
-            ]
+        sized = gated * gain_rows
+        gained[pl.program_id(0), span, :] = sized
         squared = (gated * gated).reshape(CHUNK, 2, 8, BLOCK)
         squared = squared[:, 0] + squared[:, 1]
-        size = jnp.abs(gained).reshape(CHUNK, 2, 8, BLOCK)
+        size = jnp.abs(sized).reshape(CHUNK, 2, 8, BLOCK)
         size = jnp.maximum(size[:, 0], size[:, 1])
         rows = pl.ds(chunk * CHUNK, CHUNK)
 
@@ -157,13 +154,37 @@
 
     @pl.when(pl.program_id(0) == pl.num_programs(0) - 1)
     def _():
-        side_out[0] = jnp.sum(squares[...], axis=1)
-        side_out[1] = jnp.maximum(jnp.max(peaks[...], axis=1), TINY)
+        peak = jnp.maximum(jnp.max(peaks[...], axis=1), TINY)
+        exponent = jnp.ceil(jnp.log2(peak))
+        inverse = jnp.exp2(-exponent)
+        total = (jnp.sum(squares[...], axis=1) * inverse) * inverse
+        high = total.astype(jnp.bfloat16).astype(jnp.float32)
+        rows_in[0] = exponent
+        rows_in[1] = high
+        rows_in[2] = total - high
+        rows_in[3] = inverse
+        local = gained.shape[0] * WIDTH
+        for n in range(blocks):
+            times = jnp.broadcast_to(rows_in[3, pl.ds(n, 1), :], (WIDTH, BLOCK))
+            for g in range(gained.shape[0]):
+                part = gained[g, pl.ds(n * WIDTH, WIDTH), :] * times
+                row = (n % 2) * local + g * WIDTH
+                coded_out[n // 2, row : row + WIDTH, :] = part * jnp.abs(part) * TOP
+        for d in range(blocks // 2):
+            pair = pl.ds(2 * d, 2)
+            coded_out[d, 2 * local :, :] = jnp.concatenate(
+                [
+                    rows_in[0, pair, :], rows_in[1, pair, :], rows_in[2, pair, :],
+                    jnp.zeros((2, BLOCK), jnp.float32),
+                ],
+                axis=0,
+            )
 
 
 def mix(place, streams, short_taps, rates, residues, skip, gain):
     channels, length = streams.shape[1:]
     blocks = length // BLOCK
+    groups = channels // WIDTH
     rows = blocks * WIDTH
     short_taps = short_taps.transpose(0, 2, 1)
     rates = rates.T
@@ -171,12 +192,13 @@
     skip = skip.reshape(-1, BLOCK)
     gain = gain.reshape(-1, BLOCK)
     whole = lambda array: pl.BlockSpec(array.shape, lambda g, place: (0,) * array.ndim)
+    shape = (blocks // 2, 2 * channels + 8, BLOCK)
     return pl.pallas_call(
         mix_kernel,
         name="mix",
         grid_spec=pltpu.PrefetchScalarGridSpec(
             num_scalar_prefetch=1,
-            grid=(channels // WIDTH,),
+            grid=(groups,),
             in_specs=[
                 pl.BlockSpec((3, WIDTH, length), lambda g, place: (0, g, 0)),
                 whole(short_taps),
@@ -185,10 +207,7 @@
                 whole(skip),
                 whole(gain),
             ],
-            out_specs=[
-                pl.BlockSpec((blocks // 2, WIDTH, 2 * BLOCK), lambda g, place: (0, g, 0)),
-                pl.BlockSpec((2, blocks, BLOCK), lambda g, place: (0, 0, 0)),
-            ],
+            out_specs=pl.BlockSpec(shape, lambda g, place: (0, 0, 0)),
             scratch_shapes=[
                 pltpu.VMEM((3, 2 * BLOCK, 2 * BLOCK), jnp.bfloat16),
                 pltpu.VMEM((2 * BLOCK, 4 * BLOCK), jnp.bfloat16),
@@ -199,41 +218,63 @@
                 pltpu.VMEM((rows, BLOCK), jnp.bfloat16),
                 pltpu.VMEM((blocks, 8, BLOCK), jnp.float32),
                 pltpu.VMEM((blocks, 8, BLOCK), jnp.float32),
+                pltpu.VMEM((groups, rows, BLOCK), jnp.float32),
+                pltpu.VMEM((4, blocks, BLOCK), jnp.float32),
             ],
         ),
-        out_shape=[
-            jax.ShapeDtypeStruct((blocks // 2, channels, 2 * BLOCK), jnp.float32),
-            jax.ShapeDtypeStruct((2, blocks, BLOCK), jnp.float32),
-        ],
+        out_shape=jax.ShapeDtypeStruct(shape, jnp.float32),
         compiler_params=pltpu.CompilerParams(dimension_semantics=("arbitrary",)),
     )(place, streams, short_taps, rates, residues, skip, gain)
 
 
-def from_everyone(array, axis):
+def finish_kernel(coded, inverse_root, out):
+    local = out.shape[0] // coded.shape[0]
+    for k in range(coded.shape[0]):
+        times = jnp.exp2(coded[k, 2 * local : 2 * local + 2, :]) * inverse_root[...]
+        for h in range(2):
+            value = coded[k, h * local : (h + 1) * local, :]
+            size = jnp.sqrt(jnp.abs(value)) * jnp.broadcast_to(times[h : h + 1], value.shape)
+            out[k * local : (k + 1) * local, h * BLOCK : (h + 1) * BLOCK] = jnp.where(
+                value < 0, -size, size
+            ).astype(jnp.bfloat16)
+
+
+def finish(coded, inverse_root, channels):
+    owners, rows = coded.shape[:2]
+    return pl.pallas_call(
+        finish_kernel,
+        name="finish",
+        grid=(owners // AT_ONCE,),
+        in_specs=[
+            pl.BlockSpec((AT_ONCE, rows, BLOCK), lambda i: (i, 0, 0)),
+            pl.BlockSpec((2, BLOCK), lambda i: (0, 0)),
+        ],
+        out_specs=pl.BlockSpec((AT_ONCE * channels, 2 * BLOCK), lambda i: (i, 0)),
+        out_shape=jax.ShapeDtypeStruct((owners * channels, 2 * BLOCK), jnp.bfloat16),
+        compiler_params=pltpu.CompilerParams(dimension_semantics=("arbitrary",)),
+    )(coded, inverse_root)
+
+
+def summed_over(array, axis):
     count = lax.axis_size(axis)
-    return lax.all_to_all(
-        jnp.broadcast_to(array[None], (count, *array.shape)), axis, 0, 0, tiled=True
-    )
+    total = array
+    for by in range(1, count):
+        pairs = [(i, (i + by) % count) for i in range(count)]
+        total = total + lax.ppermute(array, axis, pairs)
+    return total
 
 
 def shards(streams, short_taps, pole_rates, residues, skip, gain):
     channels = streams.shape[1]
     place = lax.axis_index(CTX)
-    gained, side = mix(
-        place.reshape(1), streams, short_taps, pole_rates, residues, skip, gain
-    )
-    owners, channels, length = gained.shape
-    side = side.reshape(2, owners, length)
-    small = lax.all_to_all(side.transpose(1, 0, 2), CTX, 0, 0, tiled=True)
-    own = jnp.sum(small[:, 0], axis=0)
-    mean_square = jnp.sum(from_everyone(own, "ch"), axis=0) / D
-    scale = small[:, 1] * (TOP**-0.5 * lax.rsqrt(mean_square + 1e-05))[None]
-    part = gained * (1.0 / side[1])[:, None, :]
-    coded = (part * jnp.abs(part) * TOP).astype(jnp.float16)
-    moved = lax.all_to_all(coded, CTX, 0, 0, tiled=True).astype(jnp.float32)
-    size = jnp.sqrt(jnp.abs(moved))
-    normed = jnp.where(moved < 0, -size, size) * scale[:, None, :]
-    return normed.astype(jnp.bfloat16).reshape(owners * channels, length)
+    coded = mix(place.reshape(1), streams, short_taps, pole_rates, residues, skip, gain)
+    moved = lax.all_to_all(coded.astype(jnp.float16), CTX, 0, 0, tiled=True)
+    side = moved[:, 2 * channels :].astype(jnp.float32)
+    size = jnp.exp2(side[:, 0:2])
+    own = jnp.sum(((side[:, 2:4] + side[:, 4:6]) * size) * size, axis=0)
+    mean_square = summed_over(own, "ch") / D
+    inverse_root = TOP**-0.5 * lax.rsqrt(mean_square + 1e-05)
+    return finish(moved.astype(jnp.float32), inverse_root, channels)
 
 
 def solution(mesh):

time: 79.5 us -> 69.7 us (0.88)
  blocking collectives: 0 us -> 43.4 us
  waiting for transfers between devices: 40.1 us -> 2.25 us
  starting transfers between devices: 22.1 us -> 4.69 us
  Pallas kernels: 8.15 us -> 15 us
  local copies, waits for them, and re-layouts: 2.33 us -> 0 us
  other arithmetic: 5.95 us -> 4.11 us
    all_to_all x0 -> x1, blocking collectives: none -> 43.4 us  [shards(): moved = lax.all_to_all(coded.astype(jnp.float16), CTX, 0, 0, tiled=True)]
    all_to_all x3 -> x0, waiting for transfers between devices: 40.1 us -> none  [the longest x1 28.7 us: shards(): moved = lax.all_to_all(coded, CTX, 0, 0, tiled=True).astype(jnp.float32)]
    all_to_all x3 -> x0, starting transfers between devices: 22.1 us -> none  [the longest x1 12 us: shards(): small = lax.all_to_all(side.transpose(1, 0, 2), CTX, 0, 0, tiled=True)]
    pallas_call x0 -> x1, Pallas kernels: none -> 5.83 us  [finish(): pl.pallas_call(finish_kernel, name='finish', grid=(owners // AT_ONCE,), i...]
    ppermute x0 -> x3, starting transfers between devices: none -> 4.69 us  [summed_over(): total = total + lax.ppermute(array, axis, pairs)]
    ppermute x0 -> x3, waiting for transfers between devices: none -> 2.25 us  [summed_over(): total = total + lax.ppermute(array, axis, pairs)]
    reshape x2 -> x0, local copies, waits for them, and re-layouts: 1.71 us -> none  [shards(): side = side.reshape(2, owners, length)]
    convert_element_type x2 -> x3, other arithmetic: 4.9 us -> 3.4 us  [the longest x1 1.82 us: shards(): moved = lax.all_to_all(coded.astype(jnp.float16), CTX, 0, 0, tiled=True)]
  transfers between devices with their start and end apart: 3 -> 3, of which waited for: 3 -> 2; matrix products, arithmetic and copies ran while one was open for 5% -> 2% of each run, Pallas kernels for 0% -> 0%
where the time goes in v3:
time: 69.7 us; the launch traced here: 69.5 us
  blocking collectives  43.4 us (62%)
  Pallas kernels  15 us (22%)
  starting transfers between devices  4.69 us (7%)
  other arithmetic  4.11 us (6%)
  waiting for transfers between devices  2.25 us (3%)
    all_to_all x1, blocking collectives, shards(): moved = lax.all_to_all(coded.astype(jnp.float16), CTX, 0, 0, tiled=True)  43.4 us
    pallas_call x1, Pallas kernels, mix(): pl.pallas_call(mix_kernel, name='mix', grid_spec=pltpu.PrefetchScalarGrid...  9.17 us
    pallas_call x1, Pallas kernels, finish(): pl.pallas_call(finish_kernel, name='finish', grid=(owners // AT_ONCE,), i...  5.83 us
    ppermute x3, starting transfers between devices, summed_over(): total = total + lax.ppermute(array, axis, pairs)  4.69 us
    ppermute x3, waiting for transfers between devices, summed_over(): total = total + lax.ppermute(array, axis, pairs)  2.25 us
    convert_element_type x1, other arithmetic, shards(): moved = lax.all_to_all(coded.astype(jnp.float16), CTX, 0, 0, tiled=True)  1.82 us
    convert_element_type x1, other arithmetic, shards(): return finish(moved.astype(jnp.float32), inverse_root, channels)  1.56 us
  transfers between devices with their start and end apart: 3, of which 2 were waited for; matrix products, arithmetic and copies ran while one was open for 2% of the time, Pallas kernels for 0%

profile of v3, /device:TPU:2, one launch (start us, length us, event | category | flops | bytes accessed | tf_op | source)
XLA Modules:
  0.0 69.5 jit_solution(1683620630966592546)
XLA Ops:
  0.0 9.2 %mix.1 = f32[64,72,128]{2,1,0:T(8,128)} custom-call(s32[1]{0:T(128)} %bitcast.place, bf16[3,32,16384]{2,1,0:T(8,128)(2,1)} %streams.1, f32[3,7,128]{2,1,0:T(8,128)} %bitcast.6, f32[16,128]{1,0:T(8,128)} %bitcast.7, f32[16,128]{1,0:T(8,128)} %bitcast.8, f32[16,128]{1,0:T(8,128)} %bitcast.9, f32[16,128]{1,0:T(8,128)} %bitcast.10), custom_call_target="tpu_custom_call" | custom-call | tf_op jit(solution)/shard_map/mix/pallas_call | solution.py:196
  9.2 1.8 %convert_element_type.9 = f16[64,72,128]{2,1,0:T(8,128)(2,1)S(1)} convert(f32[64,72,128]{2,1,0:T(8,128)} %mix.1) | non-fusion elementwise | flops 589824 | bytes 3538944 | tf_op jit(solution)/shard_map/convert_element_type | solution.py:271
  11.0 43.4 %all_to_all.5 = f16[64,72,128]{2,1,0:T(8,128)(2,1)S(1)} all-to-all(f16[64,72,128]{2,1,0:T(8,128)(2,1)S(1)} %convert_element_type.9), channel_id=1, replica_groups=mesh['ctx_0'=8,'ctx_1'=4,'ctx_2'=2,'ch'=4] {'ctx_0','ctx_1','ctx_2'}, dimensions={0} | all-to-all | bytes 2359296 | tf_op jit(solution)/shard_map/all_to_all | solution.py:271
  54.4 0.1 fusion
  54.5 3.1 %collective-permute-start.2 = (f32[2,128]{1,0:T(2,128)S(1)}, f32[2,128]{1,0:T(2,128)S(1)}, u32[]{:S(2)}, u32[]{:S(2)}) collective-permute-start(f32[2,128]{1,0:T(2,128)S(1)} %fusion), channel_id=1, source_target_pairs={{0,3},{1,0},{2,1},{3,2},{4,7},{5,4},{6,5},{7,6},{8,11},{9,8},{10,9... | collective-permute-start | bytes 3080 | tf_op jit(solution)/shard_map/ppermute | solution.py:263
  57.6 0.6 collective-permute-start.1
  58.2 1.0 %collective-permute-start = (f32[2,128]{1,0:T(2,128)S(1)}, f32[2,128]{1,0:T(2,128)S(1)}, u32[]{:S(2)}, u32[]{:S(2)}) collective-permute-start(f32[2,128]{1,0:T(2,128)S(1)} %fusion), channel_id=1, source_target_pairs={{0,1},{1,2},{2,3},{3,0},{4,5},{5,6},{6,7},{7,4},{8,9},{9,10},{10,1... | collective-permute-start | bytes 3080 | tf_op jit(solution)/shard_map/ppermute | solution.py:263
  59.2 1.6 %convert_element_type.10.coded = f32[64,72,128]{2,1,0:T(8,128)} convert(f16[64,72,128]{2,1,0:T(8,128)(2,1)S(1)} %all_to_all.5) | non-fusion elementwise | flops 589824 | bytes 3538944 | tf_op jit(solution)/shard_map/convert_element_type | solution.py:277
  60.8 0.0 collective-permute-done.2
  60.8 1.9 %collective-permute-done.1 = f32[2,128]{1,0:T(2,128)S(1)} collective-permute-done((f32[2,128]{1,0:T(2,128)S(1)}, f32[2,128]{1,0:T(2,128)S(1)}, u32[]{:S(2)}, u32[]{:S(2)}) %collective-permute-start.1) | collective-permute-done | bytes 1056 | tf_op jit(solution)/shard_map/ppermute | solution.py:263
  62.7 0.3 collective-permute-done
  63.0 0.6 rsqrt_multiply_fusion.inverse_root
  63.6 5.8 %finish.1 = bf16[2048,256]{1,0:T(8,128)(2,1)} custom-call(f32[64,72,128]{2,1,0:T(8,128)} %convert_element_type.10.coded, f32[2,128]{1,0:T(2,128)} %rsqrt_multiply_fusion.inverse_root), custom_call_target="tpu_custom_call" | custom-call | tf_op jit(solution)/shard_map/finish/pallas_call | solution.py:244
  (1 shorter events, 0.0 us)
Async XLA Ops:
  54.5 6.3 %collective-permute-start.2 = (f32[2,128]{1,0:T(2,128)S(1)}, f32[2,128]{1,0:T(2,128)S(1)}, u32[]{:S(2)}, u32[]{:S(2)}) collective-permute-start(f32[2,128]{1,0:T(2,128)S(1)} %fusion), channel_id=1, source_target_pairs={{0,3},{1,0},{2,1},{3,2},{4,7},{5,4},{6,5},{7,6},{8,11},{9,8},{10,9... | collective-permute-start | bytes 3080 | tf_op jit(solution)/shard_map/ppermute | solution.py:263
  57.6 5.1 %collective-permute-start.1 = (f32[2,128]{1,0:T(2,128)S(1)}, f32[2,128]{1,0:T(2,128)S(1)}, u32[]{:S(2)}, u32[]{:S(2)}) collective-permute-start(f32[2,128]{1,0:T(2,128)S(1)} %fusion), channel_id=1, source_target_pairs={{0,2},{1,3},{2,0},{3,1},{4,6},{5,7},{6,4},{7,5},{8,10},{9,11},{10,... | collective-permute-start | bytes 3080 | tf_op jit(solution)/shard_map/ppermute | solution.py:263
  58.2 4.8 %collective-permute-start = (f32[2,128]{1,0:T(2,128)S(1)}, f32[2,128]{1,0:T(2,128)S(1)}, u32[]{:S(2)}, u32[]{:S(2)}) collective-permute-start(f32[2,128]{1,0:T(2,128)S(1)} %fusion), channel_id=1, source_target_pairs={{0,1},{1,2},{2,3},{3,0},{4,5},{5,6},{6,7},{7,4},{8,9},{9,10},{10,1... | collective-permute-start | bytes 3080 | tf_op jit(solution)/shard_map/ppermute | solution.py:263

commit v4 on v2

--- a/solution.py
+++ b/solution.py
@@ -15,6 +15,7 @@
 CHUNK = 32
 TOP = 32768.0
 TINY = 1e-37
+AT_ONCE = 16
 
 
 def split(value):
@@ -47,10 +48,24 @@
 
 
 def mix_kernel(
-    place, streams, short_taps, rates, residues, skip, gain, gated_out, side_out,
-    taps_w, conv_w, lift_w, first, direct, ends, starts, squares, peaks,
+    place, far, short_taps, rates, residues, skip, gain, gained_out, side_out,
+    taps_w, conv_w, lift_w, first, direct, ends, starts, squares, peaks, streams, arrived,
 ):
     blocks = streams.shape[2] // BLOCK
+    turn = pl.program_id(0)
+
+    def fetch(g, chunk):
+        lanes = pl.ds(chunk * CHUNK * BLOCK, CHUNK * BLOCK)
+        at = (slice(None), pl.ds(pl.multiple_of(g * WIDTH, WIDTH), WIDTH), lanes)
+        return pltpu.make_async_copy(far.at[at], streams.at[at], arrived.at[g, chunk])
+
+    @pl.when(turn == 0)
+    def _():
+        for g in range(streams.shape[1] // WIDTH):
+            for chunk in range(blocks // CHUNK):
+                fetch(g, chunk).start()
+
+    channel_rows = pl.ds(pl.multiple_of(turn * WIDTH, WIDTH), WIDTH)
     group = place[0] * pl.num_programs(0) + pl.program_id(0)
     rate = picked_column(rates[...], group, 0)
     residue = picked_column(residues[...], group, 0)
@@ -93,15 +108,16 @@
     ).reshape(CHUNK * WIDTH, BLOCK)
     for chunk in range(blocks // CHUNK):
         span = pl.ds(chunk * CHUNK * WIDTH, CHUNK * WIDTH)
+        fetch(turn, chunk).wait()
         filtered = []
         for m in range(3):
             pieces = []
             for n in range(chunk * CHUNK, (chunk + 1) * CHUNK):
                 if n == 0:
-                    here = streams[m, :, :BLOCK]
+                    here = streams[m, channel_rows, :BLOCK]
                     pieces.append(jnp.concatenate([jnp.zeros_like(here), here], axis=1))
                 else:
-                    pieces.append(streams[m, :, (n - 1) * BLOCK : (n + 1) * BLOCK])
+                    pieces.append(streams[m, channel_rows, (n - 1) * BLOCK : (n + 1) * BLOCK])
             both = jnp.dot(
                 jnp.concatenate(pieces, axis=0), taps_w[m], preferred_element_type=jnp.float32
             )
@@ -133,15 +149,13 @@
         span = pl.ds(chunk * CHUNK * WIDTH, CHUNK * WIDTH)
         carried = jnp.dot(starts[span, :], lift_w[...], preferred_element_type=jnp.float32)
         gated = first[span, :] * (direct[span, :] + carried)
-        gained = gated * gain_rows
+        sized = gated * gain_rows
         for k in range(CHUNK):
             n = chunk * CHUNK + k
-            gated_out[n // 2, :, (n % 2) * BLOCK : (n % 2 + 1) * BLOCK] = gained[
-                k * WIDTH : (k + 1) * WIDTH
-            ]
+            gained_out[n // 2, n % 2] = sized[k * WIDTH : (k + 1) * WIDTH]
         squared = (gated * gated).reshape(CHUNK, 2, 8, BLOCK)
         squared = squared[:, 0] + squared[:, 1]
-        size = jnp.abs(gained).reshape(CHUNK, 2, 8, BLOCK)
+        size = jnp.abs(sized).reshape(CHUNK, 2, 8, BLOCK)
         size = jnp.maximum(size[:, 0], size[:, 1])
         rows = pl.ds(chunk * CHUNK, CHUNK)
 
@@ -157,13 +171,18 @@
 
     @pl.when(pl.program_id(0) == pl.num_programs(0) - 1)
     def _():
+        peak = jnp.maximum(jnp.max(peaks[...], axis=1), TINY)
+        exponent = jnp.ceil(jnp.log2(peak))
+        inverse = jnp.exp2(-exponent)
         side_out[0] = jnp.sum(squares[...], axis=1)
-        side_out[1] = jnp.maximum(jnp.max(peaks[...], axis=1), TINY)
+        side_out[1] = exponent
+        side_out[2] = inverse
 
 
 def mix(place, streams, short_taps, rates, residues, skip, gain):
     channels, length = streams.shape[1:]
     blocks = length // BLOCK
+    groups = channels // WIDTH
     rows = blocks * WIDTH
     short_taps = short_taps.transpose(0, 2, 1)
     rates = rates.T
@@ -176,9 +195,9 @@
         name="mix",
         grid_spec=pltpu.PrefetchScalarGridSpec(
             num_scalar_prefetch=1,
-            grid=(channels // WIDTH,),
+            grid=(groups,),
             in_specs=[
-                pl.BlockSpec((3, WIDTH, length), lambda g, place: (0, g, 0)),
+                pl.BlockSpec(memory_space=pltpu.HBM),
                 whole(short_taps),
                 whole(rates),
                 whole(residues),
@@ -186,8 +205,8 @@
                 whole(gain),
             ],
             out_specs=[
-                pl.BlockSpec((blocks // 2, WIDTH, 2 * BLOCK), lambda g, place: (0, g, 0)),
-                pl.BlockSpec((2, blocks, BLOCK), lambda g, place: (0, 0, 0)),
+                pl.BlockSpec((blocks // 2, 2, WIDTH, BLOCK), lambda g, place: (0, 0, g, 0)),
+                pl.BlockSpec((3, blocks, BLOCK), lambda g, place: (0, 0, 0)),
             ],
             scratch_shapes=[
                 pltpu.VMEM((3, 2 * BLOCK, 2 * BLOCK), jnp.bfloat16),
@@ -199,41 +218,104 @@
                 pltpu.VMEM((rows, BLOCK), jnp.bfloat16),
                 pltpu.VMEM((blocks, 8, BLOCK), jnp.float32),
                 pltpu.VMEM((blocks, 8, BLOCK), jnp.float32),
+                pltpu.VMEM(streams.shape, jnp.bfloat16),
+                pltpu.SemaphoreType.DMA((groups, blocks // CHUNK)),
             ],
         ),
         out_shape=[
-            jax.ShapeDtypeStruct((blocks // 2, channels, 2 * BLOCK), jnp.float32),
-            jax.ShapeDtypeStruct((2, blocks, BLOCK), jnp.float32),
+            jax.ShapeDtypeStruct((blocks // 2, 2, channels, BLOCK), jnp.float32),
+            jax.ShapeDtypeStruct((3, blocks, BLOCK), jnp.float32),
         ],
-        compiler_params=pltpu.CompilerParams(dimension_semantics=("arbitrary",)),
-    )(place, streams, short_taps, rates, residues, skip, gain)
-
-
-def from_everyone(array, axis):
+        compiler_params=pltpu.CompilerParams(
+            dimension_semantics=("arbitrary",), vmem_limit_bytes=28 * 1024 * 1024
+        ),
+    )(place, pltpu.with_memory_space_constraint(streams, pltpu.HBM), short_taps, rates, residues, skip, gain)
+
+
+def tail_kernel(own, *refs):
+    *others, out = refs
+    total = own[0]
+    for other in others:
+        total = total + other[...]
+    total = jnp.maximum(total, TINY)
+    exponent = jnp.ceil(jnp.log2(total))
+    total = total * jnp.exp2(-exponent)
+    high = total.astype(jnp.bfloat16).astype(jnp.float32)
+    owners = out.shape[0]
+    for at, value in enumerate((own[1], exponent, high, total - high)):
+        value = value.reshape(owners, 2, BLOCK)
+        out[:, 2 * at : 2 * at + 2, :] = value
+
+
+def tail(side, others):
+    blocks = side.shape[1]
+    return pl.pallas_call(
+        tail_kernel,
+        name="tail",
+        out_shape=jax.ShapeDtypeStruct((blocks // 2, 8, BLOCK), jnp.float32),
+        compiler_params=pltpu.CompilerParams(vmem_limit_bytes=4 * 1024 * 1024),
+    )(side, *others)
+
+
+def finish_kernel(tails, coded, out, inverse_root):
+    local = coded.shape[1] // 2
+    step = pl.program_id(0)
+
+    @pl.when(step == 0)
+    def _():
+        summed = (tails[:, 4:6, :] + tails[:, 6:8, :]) * jnp.exp2(tails[:, 2:4, :])
+        inverse_root[...] = TOP**-0.5 * lax.rsqrt(jnp.sum(summed, axis=0) / D + 1e-05)
+
+    for k in range(coded.shape[0]):
+        times = jnp.exp2(tails[step * coded.shape[0] + k, 0:2, :]) * inverse_root[...]
+        for h in range(2):
+            value = coded[k, h * local : (h + 1) * local, :]
+            root = value * lax.rsqrt(jnp.maximum(jnp.abs(value), 1e-20))
+            out[k * local : (k + 1) * local, h * BLOCK : (h + 1) * BLOCK] = (
+                root * jnp.broadcast_to(times[h : h + 1], value.shape)
+            ).astype(jnp.bfloat16)
+
+
+def finish(coded, channels):
+    owners, rows = coded.shape[:2]
+    return pl.pallas_call(
+        finish_kernel,
+        name="finish",
+        grid=(owners // AT_ONCE,),
+        in_specs=[
+            pl.BlockSpec((owners, 8, BLOCK), lambda i: (0, rows // 8 - 1, 0)),
+            pl.BlockSpec((AT_ONCE, 2 * channels, BLOCK), lambda i: (i, 0, 0)),
+        ],
+        out_specs=pl.BlockSpec((AT_ONCE * channels, 2 * BLOCK), lambda i: (i, 0)),
+        out_shape=jax.ShapeDtypeStruct((owners * channels, 2 * BLOCK), jnp.bfloat16),
+        scratch_shapes=[pltpu.VMEM((2, BLOCK), jnp.float32)],
+        compiler_params=pltpu.CompilerParams(
+            dimension_semantics=("arbitrary",), vmem_limit_bytes=12 * 1024 * 1024
+        ),
+    )(coded, coded)
+
+
+def from_others(array, axis):
     count = lax.axis_size(axis)
-    return lax.all_to_all(
-        jnp.broadcast_to(array[None], (count, *array.shape)), axis, 0, 0, tiled=True
-    )
+    turns = [[(i, (i + by) % count) for i in range(count)] for by in range(1, count)]
+    return [lax.ppermute(array, axis, pairs) for pairs in turns]
 
 
 def shards(streams, short_taps, pole_rates, residues, skip, gain):
     channels = streams.shape[1]
     place = lax.axis_index(CTX)
-    gained, side = mix(
-        place.reshape(1), streams, short_taps, pole_rates, residues, skip, gain
-    )
-    owners, channels, length = gained.shape
-    side = side.reshape(2, owners, length)
-    small = lax.all_to_all(side.transpose(1, 0, 2), CTX, 0, 0, tiled=True)
-    own = jnp.sum(small[:, 0], axis=0)
-    mean_square = jnp.sum(from_everyone(own, "ch"), axis=0) / D
-    scale = small[:, 1] * (TOP**-0.5 * lax.rsqrt(mean_square + 1e-05))[None]
-    part = gained * (1.0 / side[1])[:, None, :]
+    gained, side = mix(place.reshape(1), streams, short_taps, pole_rates, residues, skip, gain)
+    owners = gained.shape[0]
+    others = from_others(side[0], "ch")
+    part = gained * side[2].reshape(owners, 2, 1, BLOCK)
     coded = (part * jnp.abs(part) * TOP).astype(jnp.float16)
-    moved = lax.all_to_all(coded, CTX, 0, 0, tiled=True).astype(jnp.float32)
-    size = jnp.sqrt(jnp.abs(moved))
-    normed = jnp.where(moved < 0, -size, size) * scale[:, None, :]
-    return normed.astype(jnp.bfloat16).reshape(owners * channels, length)
+    coded = jnp.pad(coded.reshape(owners, 2 * channels, BLOCK), ((0, 0), (0, 8), (0, 0)))
+    coded = lax.optimization_barrier(coded)
+    coded = lax.dynamic_update_slice(
+        coded, tail(side, others).astype(jnp.float16), (0, 2 * channels, 0)
+    )
+    moved = lax.all_to_all(coded, CTX, 0, 0, tiled=True)
+    return finish(moved.astype(jnp.float32), channels)
 
 
 def solution(mesh):

time: 79.5 us -> 67.4 us (0.85)
  blocking collectives: 0 us -> 43.4 us
  waiting for transfers between devices: 40.1 us -> 4.16 us
  starting transfers between devices: 22.1 us -> 4.69 us
  other arithmetic: 5.95 us -> 0.64 us
  Pallas kernels: 8.15 us -> 10.2 us
  local copies, waits for them, and re-layouts: 2.33 us -> 3.74 us
    all_to_all x0 -> x1, blocking collectives: none -> 43.4 us  [shards(): moved = lax.all_to_all(coded, CTX, 0, 0, tiled=True)]
    all_to_all x3 -> x0, waiting for transfers between devices: 40.1 us -> none  [the longest x1 28.7 us: shards(): moved = lax.all_to_all(coded, CTX, 0, 0, tiled=True).astype(jnp.float32)]
    all_to_all x3 -> x0, starting transfers between devices: 22.1 us -> none  [the longest x1 12 us: shards(): small = lax.all_to_all(side.transpose(1, 0, 2), CTX, 0, 0, tiled=True)]
    ppermute x0 -> x3, starting transfers between devices: none -> 4.69 us  [from_others(): return [lax.ppermute(array, axis, pairs) for pairs in turns]]
    ppermute x0 -> x3, waiting for transfers between devices: none -> 4.16 us  [from_others(): return [lax.ppermute(array, axis, pairs) for pairs in turns]]
    unnamed x1 -> x10, local copies, waits for them, and re-layouts: 0.01 us -> 3.49 us
    convert_element_type x1, other arithmetic: 2.99 us -> 0.45 us  [shards(): coded = (part * jnp.abs(part) * TOP).astype(jnp.float16)]
    pallas_call x0 -> x2, Pallas kernels: none -> 2.14 us  [the longest x1 2.05 us: finish(): pl.pallas_call(finish_kernel, name='finish', grid=(owners // AT_ONCE,), i...]
  transfers between devices with their start and end apart: 3 -> 3, of which waited for: 3 -> 2; matrix products, arithmetic and copies ran while one was open for 5% -> 1% of each run, Pallas kernels for 0% -> 0%
where the time goes in v4:
time: 67.4 us; the launch traced here: 66.9 us
  blocking collectives  43.4 us (64%)
  Pallas kernels  10.2 us (15%)
  starting transfers between devices  4.69 us (7%)
  waiting for transfers between devices  4.16 us (6%)
  local copies, waits for them, and re-layouts  3.74 us (6%)
    all_to_all x1, blocking collectives, shards(): moved = lax.all_to_all(coded, CTX, 0, 0, tiled=True)  43.4 us
    pallas_call x1, Pallas kernels, mix(): pl.pallas_call(mix_kernel, name='mix', grid_spec=pltpu.PrefetchScalarGrid...  8.11 us
    ppermute x3, starting transfers between devices, from_others(): return [lax.ppermute(array, axis, pairs) for pairs in turns]  4.69 us
    ppermute x3, waiting for transfers between devices, from_others(): return [lax.ppermute(array, axis, pairs) for pairs in turns]  4.16 us
    unnamed x10, local copies, waits for them, and re-layouts  3.49 us
    pallas_call x1, Pallas kernels, finish(): pl.pallas_call(finish_kernel, name='finish', grid=(owners // AT_ONCE,), i...  2.05 us
  transfers between devices with their start and end apart: 3, of which 2 were waited for; matrix products, arithmetic and copies ran while one was open for 1% of the time, Pallas kernels for 0%

profile of v4, /device:TPU:2, one launch (start us, length us, event | category | flops | bytes accessed | tf_op | source)
XLA Modules:
  0.0 66.9 jit_solution(4067430794755460790)
XLA Ops:
  0.0 0.0 copy-start
  0.0 0.7 %copy-done = f32[3,128,7]{1,2,0:T(8,128)S(1)} copy-done((f32[3,128,7]{1,2,0:T(8,128)S(1)}, f32[3,128,7]{1,2,0:T(8,128)}, u32[]{:S(2)}) %copy-start) | copy-done | bytes 10776
  0.7 0.0 copy-start.1
  0.7 0.7 %copy-done.1 = f32[128,16]{0,1:T(8,128)S(1)} copy-done((f32[128,16]{0,1:T(8,128)S(1)}, f32[128,16]{0,1:T(8,128)}, u32[]{:S(2)}) %copy-start.1) | copy-done | bytes 8216
  1.4 0.0 copy-start.2
  1.4 0.7 %copy-done.2 = f32[128,16]{0,1:T(8,128)S(1)} copy-done((f32[128,16]{0,1:T(8,128)S(1)}, f32[128,16]{0,1:T(8,128)}, u32[]{:S(2)}) %copy-start.2) | copy-done | bytes 8216
  2.1 0.0 copy-start.3
  2.1 0.7 %copy-done.3 = f32[2048]{0:T(1024)S(1)} copy-done((f32[2048]{0:T(1024)S(1)}, f32[2048]{0:T(1024)}, u32[]{:S(2)}) %copy-start.3) | copy-done | bytes 8216
  2.8 0.0 copy-start.4
  2.8 0.7 %copy-done.4 = f32[2048]{0:T(1024)S(1)} copy-done((f32[2048]{0:T(1024)S(1)}, f32[2048]{0:T(1024)}, u32[]{:S(2)}) %copy-start.4) | copy-done | bytes 8216
  3.5 8.1 %mix.1 = (f32[64,2,32,128]{3,2,1,0:T(8,128)S(1)}, f32[3,128,128]{2,1,0:T(8,128)S(1)}) custom-call(s32[1]{0:T(128)} %bitcast.place, bf16[3,32,16384]{2,1,0:T(8,128)(2,1)} %far.1, f32[3,7,128]{2,1,0:T(8,128)S(1)} %bitcast.10, f32[16,128]{1,0:T(8,128)S(1)} %bitcast.11, f32[16,128]{1,0:T(8,128)S(1)} %bitcast.12, f32[16,128]{1,0:T(8,128)S(1)} %bitcast.13, ...), custom_call_target="tpu_custom_call" | custom-call | tf_op jit(solution)/shard_map/mix/pallas_call | solution.py:193
  11.6 3.1 %collective-permute-start.2 = (f32[128,128]{1,0:T(8,128)S(1)}, f32[128,128]{1,0:T(8,128)S(1)}, u32[]{:S(2)}, u32[]{:S(2)}) collective-permute-start(f32[128,128]{1,0:T(8,128)S(1)} %get-tuple-element.9), channel_id=1, source_target_pairs={{0,3},{1,0},{2,1},{3,2},{4,7},{5,4},{6,5},{7,6},{8,11},{9,8},{10,9... | collective-permute-start | bytes 196616 | tf_op jit(solution)/shard_map/ppermute | solution.py:301
  14.7 0.6 collective-permute-start.1
  15.4 1.0 %collective-permute-start = (f32[128,128]{1,0:T(8,128)S(1)}, f32[128,128]{1,0:T(8,128)S(1)}, u32[]{:S(2)}, u32[]{:S(2)}) collective-permute-start(f32[128,128]{1,0:T(8,128)S(1)} %get-tuple-element.9), channel_id=1, source_target_pairs={{0,1},{1,2},{2,3},{3,0},{4,5},{5,6},{6,7},{7,4},{8,9},{9,10},{10,1... | collective-permute-start | bytes 196616 | tf_op jit(solution)/shard_map/ppermute | solution.py:301
  16.3 0.4 fusion.1
  16.8 0.2 pad.4
  17.0 0.0 collective-permute-done.2.refs_2_
  17.0 3.5 %collective-permute-done.1.refs_1_ = f32[128,128]{1,0:T(8,128)S(1)} collective-permute-done((f32[128,128]{1,0:T(8,128)S(1)}, f32[128,128]{1,0:T(8,128)S(1)}, u32[]{:S(2)}, u32[]{:S(2)}) %collective-permute-start.1) | collective-permute-done | bytes 65568 | tf_op jit(solution)/shard_map/ppermute | solution.py:301
  20.5 0.7 %collective-permute-done.refs_0_ = f32[128,128]{1,0:T(8,128)S(1)} collective-permute-done((f32[128,128]{1,0:T(8,128)S(1)}, f32[128,128]{1,0:T(8,128)S(1)}, u32[]{:S(2)}, u32[]{:S(2)}) %collective-permute-start) | collective-permute-done | bytes 65568 | tf_op jit(solution)/shard_map/ppermute | solution.py:301
  21.2 0.1 tail.1
  21.3 43.4 %all_to_all.5 = f16[64,72,128]{2,1,0:T(8,128)(2,1)S(1)} all-to-all(f16[64,72,128]{2,1,0:T(8,128)(2,1)S(1)} %convert_dynamic-update-slice_fusion), channel_id=1, replica_groups=mesh['ctx_0'=8,'ctx_1'=4,'ctx_2'=2,'ch'=4] {'ctx_0','ctx_1','ctx_2'}, dimensions={0} | all-to-all | bytes 2359296 | tf_op jit(solution)/shard_map/all_to_all | solution.py:317
  64.7 0.2 convert_element_type.13.tails.coded
  64.9 2.0 %finish.1 = bf16[2048,256]{1,0:T(8,128)(2,1)} custom-call(f32[64,72,128]{2,1,0:T(8,128)S(1)} %convert_element_type.13.tails.coded, f32[64,72,128]{2,1,0:T(8,128)S(1)} %convert_element_type.13.tails.coded), custom_call_target="tpu_custom_call" | custom-call | tf_op jit(solution)/shard_map/finish/pallas_call | solution.py:281
  (2 shorter events, 0.1 us)
Async XLA Ops:
  0.0 0.7 %copy-start = (f32[3,128,7]{1,2,0:T(8,128)S(1)}, f32[3,128,7]{1,2,0:T(8,128)}, u32[]{:S(2)}) copy-start(f32[3,128,7]{1,2,0:T(8,128)} %param.7) | copy-start | bytes 32260
  0.7 0.7 %copy-start.1 = (f32[128,16]{0,1:T(8,128)S(1)}, f32[128,16]{0,1:T(8,128)}, u32[]{:S(2)}) copy-start(f32[128,16]{0,1:T(8,128)} %param.8) | copy-start | bytes 24580
  1.4 0.7 %copy-start.2 = (f32[128,16]{0,1:T(8,128)S(1)}, f32[128,16]{0,1:T(8,128)}, u32[]{:S(2)}) copy-start(f32[128,16]{0,1:T(8,128)} %param.9) | copy-start | bytes 24580
  2.1 0.7 %copy-start.3 = (f32[2048]{0:T(1024)S(1)}, f32[2048]{0:T(1024)}, u32[]{:S(2)}) copy-start(f32[2048]{0:T(1024)} %param.10) | copy-start | bytes 24580
  2.8 0.7 %copy-start.4 = (f32[2048]{0:T(1024)S(1)}, f32[2048]{0:T(1024)}, u32[]{:S(2)}) copy-start(f32[2048]{0:T(1024)} %param.11) | copy-start | bytes 24580
  11.6 5.4 %collective-permute-start.2 = (f32[128,128]{1,0:T(8,128)S(1)}, f32[128,128]{1,0:T(8,128)S(1)}, u32[]{:S(2)}, u32[]{:S(2)}) collective-permute-start(f32[128,128]{1,0:T(8,128)S(1)} %get-tuple-element.9), channel_id=1, source_target_pairs={{0,3},{1,0},{2,1},{3,2},{4,7},{5,4},{6,5},{7,6},{8,11},{9,8},{10,9... | collective-permute-start | bytes 196616 | tf_op jit(solution)/shard_map/ppermute | solution.py:301
  14.7 5.8 %collective-permute-start.1 = (f32[128,128]{1,0:T(8,128)S(1)}, f32[128,128]{1,0:T(8,128)S(1)}, u32[]{:S(2)}, u32[]{:S(2)}) collective-permute-start(f32[128,128]{1,0:T(8,128)S(1)} %get-tuple-element.9), channel_id=1, source_target_pairs={{0,2},{1,3},{2,0},{3,1},{4,6},{5,7},{6,4},{7,5},{8,10},{9,11},{10,... | collective-permute-start | bytes 196616 | tf_op jit(solution)/shard_map/ppermute | solution.py:301
  15.4 5.8 %collective-permute-start = (f32[128,128]{1,0:T(8,128)S(1)}, f32[128,128]{1,0:T(8,128)S(1)}, u32[]{:S(2)}, u32[]{:S(2)}) collective-permute-start(f32[128,128]{1,0:T(8,128)S(1)} %get-tuple-element.9), channel_id=1, source_target_pairs={{0,1},{1,2},{2,3},{3,0},{4,5},{5,6},{6,7},{7,4},{8,9},{9,10},{10,1... | collective-permute-start | bytes 196616 | tf_op jit(solution)/shard_map/ppermute | solution.py:301

commit v5 on v4

--- a/solution.py
+++ b/solution.py
@@ -12,7 +12,8 @@
 WIDTH = 16
 CTX = ("ctx_0", "ctx_1", "ctx_2")
 CH_CTX = ("ch", "ctx_0", "ctx_1", "ctx_2")
-CHUNK = 32
+CHUNK = 128
+UNDER = 4
 TOP = 32768.0
 TINY = 1e-37
 AT_ONCE = 16
@@ -138,12 +139,19 @@
     lane = lax.broadcasted_iota(jnp.int32, (WIDTH, BLOCK), 1)
     takes_low = (lane >= WIDTH) & (lane < 2 * WIDTH)
     state = jnp.zeros((WIDTH, BLOCK), jnp.float32)
-    for n in range(blocks):
-        high = state.astype(jnp.bfloat16).astype(jnp.float32)
-        starts[pl.ds(n * WIDTH, WIDTH), :] = jnp.where(takes_low, state - high, high).astype(
-            jnp.bfloat16
-        )
-        state = decay * state + ends[pl.ds(n * WIDTH, WIDTH), :]
+    powers = [decay]
+    for k in range(1, UNDER):
+        powers.append(powers[-1] * decay)
+    for n in range(0, blocks, UNDER):
+        at = [pl.ds((n + k) * WIDTH, WIDTH) for k in range(UNDER)]
+        sums = [ends[at[0], :]]
+        for k in range(1, UNDER):
+            sums.append(decay * sums[-1] + ends[at[k], :])
+        states = [state] + [powers[k] * state + sums[k] for k in range(UNDER)]
+        for k in range(UNDER):
+            high = states[k].astype(jnp.bfloat16).astype(jnp.float32)
+            starts[at[k], :] = jnp.where(takes_low, states[k] - high, high).astype(jnp.bfloat16)
+        state = states[UNDER]
 
     for chunk in range(blocks // CHUNK):
         span = pl.ds(chunk * CHUNK * WIDTH, CHUNK * WIDTH)
@@ -154,27 +162,31 @@
             n = chunk * CHUNK + k
             gained_out[n // 2, n % 2] = sized[k * WIDTH : (k + 1) * WIDTH]
         squared = (gated * gated).reshape(CHUNK, 2, 8, BLOCK)
-        squared = squared[:, 0] + squared[:, 1]
+        squared = (squared[:, 0] + squared[:, 1]).reshape(CHUNK * 8, BLOCK)
         size = jnp.abs(sized).reshape(CHUNK, 2, 8, BLOCK)
-        size = jnp.maximum(size[:, 0], size[:, 1])
-        rows = pl.ds(chunk * CHUNK, CHUNK)
+        size = jnp.maximum(size[:, 0], size[:, 1]).reshape(CHUNK * 8, BLOCK)
+        rows = pl.ds(chunk * CHUNK * 8, CHUNK * 8)
 
         @pl.when(pl.program_id(0) == 0)
         def _():
-            squares[rows] = squared
-            peaks[rows] = size
+            squares[rows, :] = squared
+            peaks[rows, :] = size
 
         @pl.when(pl.program_id(0) != 0)
         def _():
-            squares[rows] = squares[rows] + squared
-            peaks[rows] = jnp.maximum(peaks[rows], size)
+            squares[rows, :] = squares[rows, :] + squared
+            peaks[rows, :] = jnp.maximum(peaks[rows, :], size)
 
     @pl.when(pl.program_id(0) == pl.num_programs(0) - 1)
     def _():
-        peak = jnp.maximum(jnp.max(peaks[...], axis=1), TINY)
+        total = squares[pl.ds(0, blocks, stride=8), :]
+        peak = jnp.maximum(peaks[pl.ds(0, blocks, stride=8), :], TINY)
+        for row in range(1, 8):
+            total = total + squares[pl.ds(row, blocks, stride=8), :]
+            peak = jnp.maximum(peak, peaks[pl.ds(row, blocks, stride=8), :])
         exponent = jnp.ceil(jnp.log2(peak))
         inverse = jnp.exp2(-exponent)
-        side_out[0] = jnp.sum(squares[...], axis=1)
+        side_out[0] = total
         side_out[1] = exponent
         side_out[2] = inverse
 
@@ -216,8 +228,8 @@
                 pltpu.VMEM((rows, BLOCK), jnp.float32),
                 pltpu.VMEM((rows, BLOCK), jnp.float32),
                 pltpu.VMEM((rows, BLOCK), jnp.bfloat16),
-                pltpu.VMEM((blocks, 8, BLOCK), jnp.float32),
-                pltpu.VMEM((blocks, 8, BLOCK), jnp.float32),
+                pltpu.VMEM((blocks * 8, BLOCK), jnp.float32),
+                pltpu.VMEM((blocks * 8, BLOCK), jnp.float32),
                 pltpu.VMEM(streams.shape, jnp.bfloat16),
                 pltpu.SemaphoreType.DMA((groups, blocks // CHUNK)),
             ],
@@ -229,7 +241,13 @@
         compiler_params=pltpu.CompilerParams(
             dimension_semantics=("arbitrary",), vmem_limit_bytes=28 * 1024 * 1024
         ),
-    )(place, pltpu.with_memory_space_constraint(streams, pltpu.HBM), short_taps, rates, residues, skip, gain)
+    )(
+        place,
+        *(
+            pltpu.with_memory_space_constraint(array, pltpu.HBM)
+            for array in (streams, short_taps, rates, residues, skip, gain)
+        ),
+    )
 
 
 def tail_kernel(own, *refs):

time: 67.4 us -> 62.7 us (0.930)
  local copies, waits for them, and re-layouts: 3.74 us -> 0.25 us
  Pallas kernels: 10.2 us -> 9.28 us
    unnamed x10 -> x0, local copies, waits for them, and re-layouts: 3.49 us -> none
    pallas_call x1, Pallas kernels: 8.11 us -> 7.15 us  [mix(): pl.pallas_call(mix_kernel, name='mix', grid_spec=pltpu.PrefetchScalarGrid...]
where the time goes in v5:
time: 62.7 us; the launch traced here: 62.5 us
  blocking collectives  43.4 us (69%)
  Pallas kernels  9.28 us (15%)
  starting transfers between devices  4.69 us (7%)
  waiting for transfers between devices  4.17 us (7%)
  other arithmetic  0.63 us (1%)
    all_to_all x1, blocking collectives, shards(): moved = lax.all_to_all(coded, CTX, 0, 0, tiled=True)  43.4 us
    pallas_call x1, Pallas kernels, mix(): pl.pallas_call(mix_kernel, name='mix', grid_spec=pltpu.PrefetchScalarGrid...  7.15 us
    ppermute x3, starting transfers between devices, from_others(): return [lax.ppermute(array, axis, pairs) for pairs in turns]  4.69 us
    ppermute x3, waiting for transfers between devices, from_others(): return [lax.ppermute(array, axis, pairs) for pairs in turns]  4.17 us
    pallas_call x1, Pallas kernels, finish(): pl.pallas_call(finish_kernel, name='finish', grid=(owners // AT_ONCE,), i...  2.05 us
  transfers between devices with their start and end apart: 3, of which 2 were waited for; matrix products, arithmetic and copies ran while one was open for 1% of the time, Pallas kernels for 0%

profile of v5, /device:TPU:2, one launch (start us, length us, event | category | flops | bytes accessed | tf_op | source)
XLA Modules:
  0.0 62.5 jit_solution(7056207233057156753)
XLA Ops:
  0.0 7.1 %mix.1 = (f32[64,2,32,128]{3,2,1,0:T(8,128)S(1)}, f32[3,128,128]{2,1,0:T(8,128)S(1)}) custom-call(s32[1]{0:T(128)} %bitcast.place, bf16[3,32,16384]{2,1,0:T(8,128)(2,1)} %far.1, f32[3,7,128]{2,1,0:T(8,128)} %bitcast.12, f32[16,128]{1,0:T(8,128)} %bitcast.13, f32[16,128]{1,0:T(8,128)} %bitcast.14, f32[16,128]{1,0:T(8,128)} %bitcast.15, f32[16,128]{1,0:T(8,128)} %bitcast.16), custom_call_target="tpu_custom_call" | custom-call | tf_op jit(solution)/shard_map/mix/pallas_call | solution.py:205
  7.2 3.1 %collective-permute-start.2 = (f32[128,128]{1,0:T(8,128)S(1)}, f32[128,128]{1,0:T(8,128)S(1)}, u32[]{:S(2)}, u32[]{:S(2)}) collective-permute-start(f32[128,128]{1,0:T(8,128)S(1)} %get-tuple-element.9), channel_id=1, source_target_pairs={{0,3},{1,0},{2,1},{3,2},{4,7},{5,4},{6,5},{7,6},{8,11},{9,8},{10,9... | collective-permute-start | bytes 196616 | tf_op jit(solution)/shard_map/ppermute | solution.py:319
  10.3 0.6 %collective-permute-start.1 = (f32[128,128]{1,0:T(8,128)S(1)}, f32[128,128]{1,0:T(8,128)S(1)}, u32[]{:S(2)}, u32[]{:S(2)}) collective-permute-start(f32[128,128]{1,0:T(8,128)S(1)} %get-tuple-element.9), channel_id=1, source_target_pairs={{0,2},{1,3},{2,0},{3,1},{4,6},{5,7},{6,4},{7,5},{8,10},{9,11},{10,... | collective-permute-start | bytes 196616 | tf_op jit(solution)/shard_map/ppermute | solution.py:319
  10.9 1.0 %collective-permute-start = (f32[128,128]{1,0:T(8,128)S(1)}, f32[128,128]{1,0:T(8,128)S(1)}, u32[]{:S(2)}, u32[]{:S(2)}) collective-permute-start(f32[128,128]{1,0:T(8,128)S(1)} %get-tuple-element.9), channel_id=1, source_target_pairs={{0,1},{1,2},{2,3},{3,0},{4,5},{5,6},{6,7},{7,4},{8,9},{9,10},{10,1... | collective-permute-start | bytes 196616 | tf_op jit(solution)/shard_map/ppermute | solution.py:319
  11.9 0.4 fusion.1
  12.3 0.2 pad.4
  12.6 0.0 collective-permute-done.2.refs_2_
  12.6 3.5 %collective-permute-done.1.refs_1_ = f32[128,128]{1,0:T(8,128)S(1)} collective-permute-done((f32[128,128]{1,0:T(8,128)S(1)}, f32[128,128]{1,0:T(8,128)S(1)}, u32[]{:S(2)}, u32[]{:S(2)}) %collective-permute-start.1) | collective-permute-done | bytes 65568 | tf_op jit(solution)/shard_map/ppermute | solution.py:319
  16.0 0.7 %collective-permute-done.refs_0_ = f32[128,128]{1,0:T(8,128)S(1)} collective-permute-done((f32[128,128]{1,0:T(8,128)S(1)}, f32[128,128]{1,0:T(8,128)S(1)}, u32[]{:S(2)}, u32[]{:S(2)}) %collective-permute-start) | collective-permute-done | bytes 65568 | tf_op jit(solution)/shard_map/ppermute | solution.py:319
  16.7 0.1 tail.1
  16.9 43.4 %all_to_all.5 = f16[64,72,128]{2,1,0:T(8,128)(2,1)S(1)} all-to-all(f16[64,72,128]{2,1,0:T(8,128)(2,1)S(1)} %convert_dynamic-update-slice_fusion), channel_id=1, replica_groups=mesh['ctx_0'=8,'ctx_1'=4,'ctx_2'=2,'ch'=4] {'ctx_0','ctx_1','ctx_2'}, dimensions={0} | all-to-all | bytes 2359296 | tf_op jit(solution)/shard_map/all_to_all | solution.py:335
  60.3 0.2 convert_element_type.13.tails.coded
  60.4 2.0 %finish.1 = bf16[2048,256]{1,0:T(8,128)(2,1)} custom-call(f32[64,72,128]{2,1,0:T(8,128)S(1)} %convert_element_type.13.tails.coded, f32[64,72,128]{2,1,0:T(8,128)S(1)} %convert_element_type.13.tails.coded), custom_call_target="tpu_custom_call" | custom-call | tf_op jit(solution)/shard_map/finish/pallas_call | solution.py:299
  (2 shorter events, 0.1 us)
Async XLA Ops:
  7.2 5.4 %collective-permute-start.2 = (f32[128,128]{1,0:T(8,128)S(1)}, f32[128,128]{1,0:T(8,128)S(1)}, u32[]{:S(2)}, u32[]{:S(2)}) collective-permute-start(f32[128,128]{1,0:T(8,128)S(1)} %get-tuple-element.9), channel_id=1, source_target_pairs={{0,3},{1,0},{2,1},{3,2},{4,7},{5,4},{6,5},{7,6},{8,11},{9,8},{10,9... | collective-permute-start | bytes 196616 | tf_op jit(solution)/shard_map/ppermute | solution.py:319
  10.3 5.8 %collective-permute-start.1 = (f32[128,128]{1,0:T(8,128)S(1)}, f32[128,128]{1,0:T(8,128)S(1)}, u32[]{:S(2)}, u32[]{:S(2)}) collective-permute-start(f32[128,128]{1,0:T(8,128)S(1)} %get-tuple-element.9), channel_id=1, source_target_pairs={{0,2},{1,3},{2,0},{3,1},{4,6},{5,7},{6,4},{7,5},{8,10},{9,11},{10,... | collective-permute-start | bytes 196616 | tf_op jit(solution)/shard_map/ppermute | solution.py:319
  10.9 5.8 %collective-permute-start = (f32[128,128]{1,0:T(8,128)S(1)}, f32[128,128]{1,0:T(8,128)S(1)}, u32[]{:S(2)}, u32[]{:S(2)}) collective-permute-start(f32[128,128]{1,0:T(8,128)S(1)} %get-tuple-element.9), channel_id=1, source_target_pairs={{0,1},{1,2},{2,3},{3,0},{4,5},{5,6},{6,7},{7,4},{8,9},{9,10},{10,1... | collective-permute-start | bytes 196616 | tf_op jit(solution)/shard_map/ppermute | solution.py:319

commit v6 on v5

--- a/solution.py
+++ b/solution.py
@@ -7,7 +7,6 @@
 from jax.sharding import PartitionSpec as P
 
 D = 8192
-SHORT = 7
 BLOCK = 128
 WIDTH = 16
 CTX = ("ctx_0", "ctx_1", "ctx_2")
@@ -49,7 +48,7 @@
 
 
 def mix_kernel(
-    place, far, short_taps, rates, residues, skip, gain, gained_out, side_out,
+    place, far, short_taps, rates, residues, skip, gain, gained_out, side_out, tail_out,
     taps_w, conv_w, lift_w, first, direct, ends, starts, squares, peaks, streams, arrived,
 ):
     blocks = streams.shape[2] // BLOCK
@@ -140,7 +139,7 @@
     takes_low = (lane >= WIDTH) & (lane < 2 * WIDTH)
     state = jnp.zeros((WIDTH, BLOCK), jnp.float32)
     powers = [decay]
-    for k in range(1, UNDER):
+    for _ in range(1, UNDER):
         powers.append(powers[-1] * decay)
     for n in range(0, blocks, UNDER):
         at = [pl.ds((n + k) * WIDTH, WIDTH) for k in range(UNDER)]
@@ -187,8 +186,9 @@
         exponent = jnp.ceil(jnp.log2(peak))
         inverse = jnp.exp2(-exponent)
         side_out[0] = total
-        side_out[1] = exponent
-        side_out[2] = inverse
+        side_out[1] = inverse
+        tail_out[:, 0:2, :] = exponent.reshape(blocks // 2, 2, BLOCK)
+        tail_out[:, 2:8, :] = jnp.zeros((blocks // 2, 6, BLOCK), jnp.float32)
 
 
 def mix(place, streams, short_taps, rates, residues, skip, gain):
@@ -218,7 +218,8 @@
             ],
             out_specs=[
                 pl.BlockSpec((blocks // 2, 2, WIDTH, BLOCK), lambda g, place: (0, 0, g, 0)),
-                pl.BlockSpec((3, blocks, BLOCK), lambda g, place: (0, 0, 0)),
+                pl.BlockSpec((2, blocks, BLOCK), lambda g, place: (0, 0, 0)),
+                pl.BlockSpec((blocks // 2, 8, BLOCK), lambda g, place: (0, 0, 0)),
             ],
             scratch_shapes=[
                 pltpu.VMEM((3, 2 * BLOCK, 2 * BLOCK), jnp.bfloat16),
@@ -236,7 +237,8 @@
         ),
         out_shape=[
             jax.ShapeDtypeStruct((blocks // 2, 2, channels, BLOCK), jnp.float32),
-            jax.ShapeDtypeStruct((3, blocks, BLOCK), jnp.float32),
+            jax.ShapeDtypeStruct((2, blocks, BLOCK), jnp.float32),
+            jax.ShapeDtypeStruct((blocks // 2, 8, BLOCK), jnp.float32),
         ],
         compiler_params=pltpu.CompilerParams(
             dimension_semantics=("arbitrary",), vmem_limit_bytes=28 * 1024 * 1024
@@ -250,42 +252,11 @@
     )
 
 
-def tail_kernel(own, *refs):
-    *others, out = refs
-    total = own[0]
-    for other in others:
-        total = total + other[...]
-    total = jnp.maximum(total, TINY)
-    exponent = jnp.ceil(jnp.log2(total))
-    total = total * jnp.exp2(-exponent)
-    high = total.astype(jnp.bfloat16).astype(jnp.float32)
-    owners = out.shape[0]
-    for at, value in enumerate((own[1], exponent, high, total - high)):
-        value = value.reshape(owners, 2, BLOCK)
-        out[:, 2 * at : 2 * at + 2, :] = value
-
-
-def tail(side, others):
-    blocks = side.shape[1]
-    return pl.pallas_call(
-        tail_kernel,
-        name="tail",
-        out_shape=jax.ShapeDtypeStruct((blocks // 2, 8, BLOCK), jnp.float32),
-        compiler_params=pltpu.CompilerParams(vmem_limit_bytes=4 * 1024 * 1024),
-    )(side, *others)
-
-
-def finish_kernel(tails, coded, out, inverse_root):
-    local = coded.shape[1] // 2
-    step = pl.program_id(0)
-
-    @pl.when(step == 0)
-    def _():
-        summed = (tails[:, 4:6, :] + tails[:, 6:8, :]) * jnp.exp2(tails[:, 2:4, :])
-        inverse_root[...] = TOP**-0.5 * lax.rsqrt(jnp.sum(summed, axis=0) / D + 1e-05)
-
+def finish_kernel(coded, mean_square, out):
+    local = (coded.shape[1] - 8) // 2
+    inverse_root = TOP**-0.5 * lax.rsqrt(mean_square[...] + 1e-05)
     for k in range(coded.shape[0]):
-        times = jnp.exp2(tails[step * coded.shape[0] + k, 0:2, :]) * inverse_root[...]
+        times = jnp.exp2(coded[k, 2 * local : 2 * local + 2, :]) * inverse_root
         for h in range(2):
             value = coded[k, h * local : (h + 1) * local, :]
             root = value * lax.rsqrt(jnp.maximum(jnp.abs(value), 1e-20))
@@ -294,46 +265,70 @@
             ).astype(jnp.bfloat16)
 
 
-def finish(coded, channels):
+def finish(coded, mean_square, channels):
     owners, rows = coded.shape[:2]
     return pl.pallas_call(
         finish_kernel,
         name="finish",
         grid=(owners // AT_ONCE,),
         in_specs=[
-            pl.BlockSpec((owners, 8, BLOCK), lambda i: (0, rows // 8 - 1, 0)),
-            pl.BlockSpec((AT_ONCE, 2 * channels, BLOCK), lambda i: (i, 0, 0)),
+            pl.BlockSpec((AT_ONCE, rows, BLOCK), lambda i: (i, 0, 0)),
+            pl.BlockSpec((2, BLOCK), lambda i: (0, 0)),
         ],
         out_specs=pl.BlockSpec((AT_ONCE * channels, 2 * BLOCK), lambda i: (i, 0)),
         out_shape=jax.ShapeDtypeStruct((owners * channels, 2 * BLOCK), jnp.bfloat16),
-        scratch_shapes=[pltpu.VMEM((2, BLOCK), jnp.float32)],
         compiler_params=pltpu.CompilerParams(
             dimension_semantics=("arbitrary",), vmem_limit_bytes=12 * 1024 * 1024
         ),
-    )(coded, coded)
-
-
-def from_others(array, axis):
-    count = lax.axis_size(axis)
-    turns = [[(i, (i + by) % count) for i in range(count)] for by in range(1, count)]
-    return [lax.ppermute(array, axis, pairs) for pairs in turns]
+    )(coded, mean_square)
+
+
+def with_partner(array, axis, bit):
+    pairs = [(i, i ^ bit) for i in range(lax.axis_size(axis))]
+    return lax.ppermute(array, axis, pairs)
+
+
+def half_summed(halves, axis, bit):
+    mine = (lax.axis_index(axis) // bit) % 2 == 0
+    kept = jnp.where(mine, halves[0], halves[1])
+    given = jnp.where(mine, halves[1], halves[0])
+    return kept + with_partner(given, axis, bit)
+
+
+def summed_for_owner(squares):
+    z, x, core = (lax.axis_size(axis) for axis in CTX)
+    bit = lax.axis_size("ch") // 2
+    while bit:
+        squares = squares + with_partner(squares, "ch", bit)
+        bit //= 2
+    squares = squares.reshape(z, x, core, 2, BLOCK).transpose(2, 1, 0, 3, 4)
+    for axis, count in ((CTX[2], core), (CTX[1], x), (CTX[0], z)):
+        bit = count // 2
+        while bit:
+            squares = squares.reshape(2, squares.shape[0] // 2, *squares.shape[1:])
+            squares = half_summed(squares, axis, bit)
+            bit //= 2
+        squares = squares.reshape(squares.shape[1:])
+    return squares
 
 
 def shards(streams, short_taps, pole_rates, residues, skip, gain):
     channels = streams.shape[1]
     place = lax.axis_index(CTX)
-    gained, side = mix(place.reshape(1), streams, short_taps, pole_rates, residues, skip, gain)
+    gained, side, tails = mix(
+        place.reshape(1), streams, short_taps, pole_rates, residues, skip, gain
+    )
     owners = gained.shape[0]
-    others = from_others(side[0], "ch")
-    part = gained * side[2].reshape(owners, 2, 1, BLOCK)
+    part = gained * side[1].reshape(owners, 2, 1, BLOCK)
     coded = (part * jnp.abs(part) * TOP).astype(jnp.float16)
     coded = jnp.pad(coded.reshape(owners, 2 * channels, BLOCK), ((0, 0), (0, 8), (0, 0)))
     coded = lax.optimization_barrier(coded)
     coded = lax.dynamic_update_slice(
-        coded, tail(side, others).astype(jnp.float16), (0, 2 * channels, 0)
+        coded, tails.astype(jnp.float16), (0, 2 * channels, 0)
     )
     moved = lax.all_to_all(coded, CTX, 0, 0, tiled=True)
-    return finish(moved.astype(jnp.float32), channels)
+    mean_square = summed_for_owner(side[0]) / D
+    return finish(moved.astype(jnp.float32), mean_square, channels)
 
 
 def solution(mesh):

time: 62.7 us -> 72.7 us (1.16)
  blocking collectives: 43.4 us -> 0 us
  waiting for transfers between devices: 4.17 us -> 33.7 us
  starting transfers between devices: 4.69 us -> 26.9 us
  local copies, waits for them, and re-layouts: 0.25 us -> 1.3 us
  other arithmetic: 0.63 us -> 1.45 us
    all_to_all x1 -> x0, blocking collectives: 43.4 us -> none  [shards(): moved = lax.all_to_all(coded, CTX, 0, 0, tiled=True)]
    ppermute x3 -> x8, waiting for transfers between devices: 4.17 us -> 33.7 us  [with_partner(): return lax.ppermute(array, axis, pairs)]
    all_to_all x0 -> x1, starting transfers between devices: none -> 12.1 us  [shards(): moved = lax.all_to_all(coded, CTX, 0, 0, tiled=True)]
    ppermute x3 -> x8, starting transfers between devices: 4.69 us -> 14.8 us  [with_partner(): return lax.ppermute(array, axis, pairs)]
    pad x1, local copies, waits for them, and re-layouts: 0.24 us -> 1.26 us  [shards(): jnp.pad(coded.reshape(owners, 2 * channels, BLOCK), ((0, 0), (0, 8), (0,...]
  transfers between devices with their start and end apart: 3 -> 9, of which waited for: 2 -> 7; matrix products, arithmetic and copies ran while one was open for 1% -> 3% of each run, Pallas kernels for 0% -> 0%
where the time goes in v6:
time: 72.7 us; the launch traced here: 72.5 us
  waiting for transfers between devices  33.7 us (46%)
  starting transfers between devices  26.9 us (37%)
  Pallas kernels  9 us (12%)
  other arithmetic  1.45 us (2%)
  local copies, waits for them, and re-layouts  1.3 us (2%)
    ppermute x8, waiting for transfers between devices, with_partner(): return lax.ppermute(array, axis, pairs)  33.7 us
    ppermute x8, starting transfers between devices, with_partner(): return lax.ppermute(array, axis, pairs)  14.8 us
    all_to_all x1, starting transfers between devices, shards(): moved = lax.all_to_all(coded, CTX, 0, 0, tiled=True)  12.1 us
    pallas_call x1, Pallas kernels, mix(): pl.pallas_call(mix_kernel, name='mix', grid_spec=pltpu.PrefetchScalarGrid...  7.18 us
    pallas_call x1, Pallas kernels, finish(): pl.pallas_call(finish_kernel, name='finish', grid=(owners // AT_ONCE,), i...  1.82 us
  transfers between devices with their start and end apart: 9, of which 7 were waited for; matrix products, arithmetic and copies ran while one was open for 3% of the time, Pallas kernels for 0%

profile of v6, /device:TPU:2, one launch (start us, length us, event | category | flops | bytes accessed | tf_op | source)
XLA Modules:
  0.0 72.5 jit_solution(17654155913039829697)
XLA Ops:
  0.0 7.2 %mix.1 = (f32[64,2,32,128]{3,2,1,0:T(8,128)S(1)}, f32[2,128,128]{2,1,0:T(8,128)S(1)}, f32[64,8,128]{2,1,0:T(8,128)S(1)}) custom-call(s32[1]{0:T(128)} %bitcast.place, bf16[3,32,16384]{2,1,0:T(8,128)(2,1)} %far.1, f32[3,7,128]{2,1,0:T(8,128)} %bitcast.31, f32[16,128]{1,0:T(8,128)} %bitcast.32, f32[16,128]{1,0:T(8,128)} %bitcast.33, f32[16,128]{1,0:T(8,128)} %bitcast.34, ...), custom_call_target="tpu_custom_call" | custom-call | tf_op jit(solution)/shard_map/mix/pallas_call | solution.py:205
  7.2 3.3 %collective-permute-start = (f32[128,128]{1,0:T(8,128)S(1)}, f32[128,128]{1,0:T(8,128)S(1)}, u32[]{:S(2)}, u32[]{:S(2)}) collective-permute-start(f32[128,128]{1,0:T(8,128)S(1)} %get-tuple-element.11), channel_id=1, source_target_pairs={{0,2},{1,3},{2,0},{3,1},{4,6},{5,7},{6,4},{7,5},{8,10},{9,11},{10,... | collective-permute-start | bytes 196616 | tf_op jit(solution)/shard_map/ppermute | solution.py:288
  10.5 2.6 %collective-permute-done = f32[128,128]{1,0:T(8,128)S(1)} collective-permute-done((f32[128,128]{1,0:T(8,128)S(1)}, f32[128,128]{1,0:T(8,128)S(1)}, u32[]{:S(2)}, u32[]{:S(2)}) %collective-permute-start) | collective-permute-done | bytes 65568 | tf_op jit(solution)/shard_map/ppermute | solution.py:288
  13.1 1.7 %collective-permute-start.1 = (f32[128,128]{1,0:T(8,128)S(1)}, f32[128,128]{1,0:T(8,128)S(1)}, u32[]{:S(2)}, u32[]{:S(2)}) collective-permute-start(f32[128,128]{1,0:T(8,128)S(1)} %fusion.2), channel_id=1, source_target_pairs={{0,1},{1,0},{2,3},{3,2},{4,5},{5,4},{6,7},{7,6},{8,9},{9,8},{10,11... | collective-permute-start | bytes 196616 | tf_op jit(solution)/shard_map/ppermute | solution.py:288
  14.7 0.4 fusion.1
  15.2 1.3 %pad.4 = f16[64,72,128]{2,1,0:T(8,128)(2,1)} pad(f16[64,64,128]{2,1,0:T(8,128)(2,1)S(1)} %bitcast.26, f16[]{:T(256)} %constant.104.clone.1), padding=0_0x0_8x0_0 | pad | bytes 2228226 | tf_op jit(solution)/shard_map/jit(_pad)/pad | solution.py:324
  16.5 1.0 %collective-permute-done.1 = f32[128,128]{1,0:T(8,128)S(1)} collective-permute-done((f32[128,128]{1,0:T(8,128)S(1)}, f32[128,128]{1,0:T(8,128)S(1)}, u32[]{:S(2)}, u32[]{:S(2)}) %collective-permute-start.1) | collective-permute-done | bytes 65568 | tf_op jit(solution)/shard_map/ppermute | solution.py:288
  17.5 0.1 collective-permute-start.2
  17.6 0.7 convert_dynamic-update-slice_fusion
  18.3 12.1 %all-to-all-start = ((f16[64,72,128]{2,1,0:T(8,128)(2,1)}), f16[64,72,128]{2,1,0:T(8,128)(2,1)S(1)}, u32[]{:S(2)}, u32[]{:S(2)}) async-start(f16[64,72,128]{2,1,0:T(8,128)(2,1)} %convert_dynamic-update-slice_fusion), calls=%async_computation | async-start | bytes 2359296 | tf_op jit(solution)/shard_map/all_to_all | solution.py:329
  30.5 0.0 collective-permute-done.2
  30.5 2.2 %collective-permute-start.3 = (f32[2,8,2,128]{3,2,1,0:T(2,128)S(1)}, f32[2,8,2,128]{3,2,1,0:T(2,128)S(1)}, u32[]{:S(2)}, u32[]{:S(2)}) collective-permute-start(f32[2,8,2,128]{3,2,1,0:T(2,128)S(1)} %select_bitcast_fusion), channel_id=1, source_target_pairs={{0,16},{8,24},{16,0},{24,8},{1,17},{9,25},{17,1},{25,9},{2,18},{10... | collective-permute-start | bytes 49160 | tf_op jit(solution)/shard_map/ppermute | solution.py:288
  32.7 3.6 %collective-permute-done.3 = f32[2,8,2,128]{3,2,1,0:T(2,128)S(1)} collective-permute-done((f32[2,8,2,128]{3,2,1,0:T(2,128)S(1)}, f32[2,8,2,128]{3,2,1,0:T(2,128)S(1)}, u32[]{:S(2)}, u32[]{:S(2)}) %collective-permute-start.3) | collective-permute-done | bytes 16416 | tf_op jit(solution)/shard_map/ppermute | solution.py:288
  36.4 0.7 %collective-permute-start.4 = (f32[1,8,2,128]{3,2,1,0:T(2,128)S(1)}, f32[1,8,2,128]{3,2,1,0:T(2,128)S(1)}, u32[]{:S(2)}, u32[]{:S(2)}) collective-permute-start(f32[1,8,2,128]{3,2,1,0:T(2,128)S(1)} %broadcast_select_fusion.1), channel_id=1, source_target_pairs={{0,8},{8,0},{16,24},{24,16},{1,9},{9,1},{17,25},{25,17},{2,10},{10... | collective-permute-start | bytes 24584 | tf_op jit(solution)/shard_map/ppermute | solution.py:288
  37.1 3.0 %collective-permute-done.4 = f32[1,8,2,128]{3,2,1,0:T(2,128)S(1)} collective-permute-done((f32[1,8,2,128]{3,2,1,0:T(2,128)S(1)}, f32[1,8,2,128]{3,2,1,0:T(2,128)S(1)}, u32[]{:S(2)}, u32[]{:S(2)}) %collective-permute-start.4) | collective-permute-done | bytes 8224 | tf_op jit(solution)/shard_map/ppermute | solution.py:288
  40.1 6.0 %collective-permute-start.5 = (f32[4,2,128]{2,1,0:T(2,128)S(1)}, f32[4,2,128]{2,1,0:T(2,128)S(1)}, u32[]{:S(2)}, u32[]{:S(2)}) collective-permute-start(f32[4,2,128]{2,1,0:T(2,128)S(1)} %select_bitcast_fusion.1), channel_id=1, source_target_pairs={{0,128},{32,160},{64,192},{96,224},{128,0},{160,32},{192,64},{224,... | collective-permute-start | bytes 12296 | tf_op jit(solution)/shard_map/ppermute | solution.py:288
  46.1 16.1 %collective-permute-done.5 = f32[4,2,128]{2,1,0:T(2,128)S(1)} collective-permute-done((f32[4,2,128]{2,1,0:T(2,128)S(1)}, f32[4,2,128]{2,1,0:T(2,128)S(1)}, u32[]{:S(2)}, u32[]{:S(2)}) %collective-permute-start.5) | collective-permute-done | bytes 4128 | tf_op jit(solution)/shard_map/ppermute | solution.py:288
  62.2 0.1 collective-permute-start.6
  62.3 4.5 %collective-permute-done.6 = f32[2,2,128]{2,1,0:T(2,128)S(1)} collective-permute-done((f32[2,2,128]{2,1,0:T(2,128)S(1)}, f32[2,2,128]{2,1,0:T(2,128)S(1)}, u32[]{:S(2)}, u32[]{:S(2)}) %collective-permute-start.6) | collective-permute-done | bytes 2080 | tf_op jit(solution)/shard_map/ppermute | solution.py:288
  66.8 0.7 collective-permute-start.7
  67.5 3.0 %collective-permute-done.7 = f32[1,2,128]{2,1,0:T(2,128)S(1)} collective-permute-done((f32[1,2,128]{2,1,0:T(2,128)S(1)}, f32[1,2,128]{2,1,0:T(2,128)S(1)}, u32[]{:S(2)}, u32[]{:S(2)}) %collective-permute-start.7) | collective-permute-done | bytes 1056 | tf_op jit(solution)/shard_map/ppermute | solution.py:288
  70.5 0.0 all-to-all-done
  70.5 0.2 convert_element_type.13.coded
  70.6 1.8 %finish.1 = bf16[2048,256]{1,0:T(8,128)(2,1)} custom-call(f32[64,72,128]{2,1,0:T(8,128)S(1)} %convert_element_type.13.coded, f32[2,128]{1,0:T(2,128)S(1)} %multiply_bitcast_fusion.mean_square), custom_call_target="tpu_custom_call" | custom-call | tf_op jit(solution)/shard_map/finish/pallas_call | solution.py:270
  (16 shorter events, 0.2 us)
Async XLA Ops:
  7.2 5.9 %collective-permute-start = (f32[128,128]{1,0:T(8,128)S(1)}, f32[128,128]{1,0:T(8,128)S(1)}, u32[]{:S(2)}, u32[]{:S(2)}) collective-permute-start(f32[128,128]{1,0:T(8,128)S(1)} %get-tuple-element.11), channel_id=1, source_target_pairs={{0,2},{1,3},{2,0},{3,1},{4,6},{5,7},{6,4},{7,5},{8,10},{9,11},{10,... | collective-permute-start | bytes 196616 | tf_op jit(solution)/shard_map/ppermute | solution.py:288
  13.1 4.4 %collective-permute-start.1 = (f32[128,128]{1,0:T(8,128)S(1)}, f32[128,128]{1,0:T(8,128)S(1)}, u32[]{:S(2)}, u32[]{:S(2)}) collective-permute-start(f32[128,128]{1,0:T(8,128)S(1)} %fusion.2), channel_id=1, source_target_pairs={{0,1},{1,0},{2,3},{3,2},{4,5},{5,4},{6,7},{7,6},{8,9},{9,8},{10,11... | collective-permute-start | bytes 196616 | tf_op jit(solution)/shard_map/ppermute | solution.py:288
  17.5 13.0 %collective-permute-start.2 = (f32[1,4,8,2,128]{4,3,2,1,0:T(2,128)S(1)}, f32[1,4,8,2,128]{4,3,2,1,0:T(2,128)S(1)}, u32[]{:S(2)}, u32[]{:S(2)}) collective-permute-start(f32[1,4,8,2,128]{4,3,2,1,0:T(2,128)S(1)} %broadcast_select_fusion), channel_id=1, source_target_pairs={{0,4},{4,0},{1,5},{5,1},{2,6},{6,2},{3,7},{7,3},{8,12},{12,8},{9,1... | collective-permute-start | bytes 98312 | tf_op jit(solution)/shard_map/ppermute | solution.py:288
  18.3 52.2 %all-to-all-start = ((f16[64,72,128]{2,1,0:T(8,128)(2,1)}), f16[64,72,128]{2,1,0:T(8,128)(2,1)S(1)}, u32[]{:S(2)}, u32[]{:S(2)}) async-start(f16[64,72,128]{2,1,0:T(8,128)(2,1)} %convert_dynamic-update-slice_fusion), calls=%async_computation | async-start | bytes 2359296 | tf_op jit(solution)/shard_map/all_to_all | solution.py:329
  30.5 5.8 %collective-permute-start.3 = (f32[2,8,2,128]{3,2,1,0:T(2,128)S(1)}, f32[2,8,2,128]{3,2,1,0:T(2,128)S(1)}, u32[]{:S(2)}, u32[]{:S(2)}) collective-permute-start(f32[2,8,2,128]{3,2,1,0:T(2,128)S(1)} %select_bitcast_fusion), channel_id=1, source_target_pairs={{0,16},{8,24},{16,0},{24,8},{1,17},{9,25},{17,1},{25,9},{2,18},{10... | collective-permute-start | bytes 49160 | tf_op jit(solution)/shard_map/ppermute | solution.py:288
  36.4 3.8 %collective-permute-start.4 = (f32[1,8,2,128]{3,2,1,0:T(2,128)S(1)}, f32[1,8,2,128]{3,2,1,0:T(2,128)S(1)}, u32[]{:S(2)}, u32[]{:S(2)}) collective-permute-start(f32[1,8,2,128]{3,2,1,0:T(2,128)S(1)} %broadcast_select_fusion.1), channel_id=1, source_target_pairs={{0,8},{8,0},{16,24},{24,16},{1,9},{9,1},{17,25},{25,17},{2,10},{10... | collective-permute-start | bytes 24584 | tf_op jit(solution)/shard_map/ppermute | solution.py:288
  40.1 22.1 %collective-permute-start.5 = (f32[4,2,128]{2,1,0:T(2,128)S(1)}, f32[4,2,128]{2,1,0:T(2,128)S(1)}, u32[]{:S(2)}, u32[]{:S(2)}) collective-permute-start(f32[4,2,128]{2,1,0:T(2,128)S(1)} %select_bitcast_fusion.1), channel_id=1, source_target_pairs={{0,128},{32,160},{64,192},{96,224},{128,0},{160,32},{192,64},{224,... | collective-permute-start | bytes 12296 | tf_op jit(solution)/shard_map/ppermute | solution.py:288
  62.2 4.6 %collective-permute-start.6 = (f32[2,2,128]{2,1,0:T(2,128)S(1)}, f32[2,2,128]{2,1,0:T(2,128)S(1)}, u32[]{:S(2)}, u32[]{:S(2)}) collective-permute-start(f32[2,2,128]{2,1,0:T(2,128)S(1)} %broadcast_select_fusion.2), channel_id=1, source_target_pairs={{0,64},{32,96},{64,0},{96,32},{128,192},{160,224},{192,128},{224,1... | collective-permute-start | bytes 6152 | tf_op jit(solution)/shard_map/ppermute | solution.py:288
  66.8 3.7 %collective-permute-start.7 = (f32[1,2,128]{2,1,0:T(2,128)S(1)}, f32[1,2,128]{2,1,0:T(2,128)S(1)}, u32[]{:S(2)}, u32[]{:S(2)}) collective-permute-start(f32[1,2,128]{2,1,0:T(2,128)S(1)} %broadcast_select_fusion.3), channel_id=1, source_target_pairs={{0,32},{32,0},{64,96},{96,64},{128,160},{160,128},{192,224},{224,1... | collective-permute-start | bytes 3080 | tf_op jit(solution)/shard_map/ppermute | solution.py:288

commit v7 on v6

--- a/solution.py
+++ b/solution.py
@@ -48,8 +48,9 @@
 
 
 def mix_kernel(
-    place, far, short_taps, rates, residues, skip, gain, gained_out, side_out, tail_out,
+    place, far, short_taps, rates, residues, skip, gain, coded_out, square_out,
     taps_w, conv_w, lift_w, first, direct, ends, starts, squares, peaks, streams, arrived,
+    gained, inverses,
 ):
     blocks = streams.shape[2] // BLOCK
     turn = pl.program_id(0)
@@ -157,9 +158,7 @@
         carried = jnp.dot(starts[span, :], lift_w[...], preferred_element_type=jnp.float32)
         gated = first[span, :] * (direct[span, :] + carried)
         sized = gated * gain_rows
-        for k in range(CHUNK):
-            n = chunk * CHUNK + k
-            gained_out[n // 2, n % 2] = sized[k * WIDTH : (k + 1) * WIDTH]
+        gained[turn, span, :] = sized
         squared = (gated * gated).reshape(CHUNK, 2, 8, BLOCK)
         squared = (squared[:, 0] + squared[:, 1]).reshape(CHUNK * 8, BLOCK)
         size = jnp.abs(sized).reshape(CHUNK, 2, 8, BLOCK)
@@ -185,10 +184,18 @@
             peak = jnp.maximum(peak, peaks[pl.ds(row, blocks, stride=8), :])
         exponent = jnp.ceil(jnp.log2(peak))
         inverse = jnp.exp2(-exponent)
-        side_out[0] = total
-        side_out[1] = inverse
-        tail_out[:, 0:2, :] = exponent.reshape(blocks // 2, 2, BLOCK)
-        tail_out[:, 2:8, :] = jnp.zeros((blocks // 2, 6, BLOCK), jnp.float32)
+        square_out[...] = total
+        inverses[...] = inverse
+        local = streams.shape[1]
+        for n in range(blocks):
+            times = jnp.broadcast_to(inverses[pl.ds(n, 1), :], (WIDTH, BLOCK))
+            for g in range(local // WIDTH):
+                part = gained[g, pl.ds(n * WIDTH, WIDTH), :] * times
+                row = (n % 2) * local + g * WIDTH
+                coded_out[n // 2, row : row + WIDTH, :] = part * jnp.abs(part) * TOP
+        owners = blocks // 2
+        coded_out[:, 2 * local : 2 * local + 2, :] = exponent.reshape(owners, 2, BLOCK)
+        coded_out[:, 2 * local + 2 :, :] = jnp.zeros((owners, 6, BLOCK), jnp.float32)
 
 
 def mix(place, streams, short_taps, rates, residues, skip, gain):
@@ -201,6 +208,7 @@
     residues = residues.T
     skip = skip.reshape(-1, BLOCK)
     gain = gain.reshape(-1, BLOCK)
+    shape = (blocks // 2, 2 * channels + 8, BLOCK)
     whole = lambda array: pl.BlockSpec(array.shape, lambda g, place: (0,) * array.ndim)
     return pl.pallas_call(
         mix_kernel,
@@ -217,9 +225,8 @@
                 whole(gain),
             ],
             out_specs=[
-                pl.BlockSpec((blocks // 2, 2, WIDTH, BLOCK), lambda g, place: (0, 0, g, 0)),
-                pl.BlockSpec((2, blocks, BLOCK), lambda g, place: (0, 0, 0)),
-                pl.BlockSpec((blocks // 2, 8, BLOCK), lambda g, place: (0, 0, 0)),
+                pl.BlockSpec(shape, lambda g, place: (0, 0, 0)),
+                pl.BlockSpec((blocks, BLOCK), lambda g, place: (0, 0)),
             ],
             scratch_shapes=[
                 pltpu.VMEM((3, 2 * BLOCK, 2 * BLOCK), jnp.bfloat16),
@@ -233,12 +240,13 @@
                 pltpu.VMEM((blocks * 8, BLOCK), jnp.float32),
                 pltpu.VMEM(streams.shape, jnp.bfloat16),
                 pltpu.SemaphoreType.DMA((groups, blocks // CHUNK)),
+                pltpu.VMEM((groups, rows, BLOCK), jnp.float32),
+                pltpu.VMEM((blocks, BLOCK), jnp.float32),
             ],
         ),
         out_shape=[
-            jax.ShapeDtypeStruct((blocks // 2, 2, channels, BLOCK), jnp.float32),
-            jax.ShapeDtypeStruct((2, blocks, BLOCK), jnp.float32),
-            jax.ShapeDtypeStruct((blocks // 2, 8, BLOCK), jnp.float32),
+            jax.ShapeDtypeStruct(shape, jnp.float32),
+            jax.ShapeDtypeStruct((blocks, BLOCK), jnp.float32),
         ],
         compiler_params=pltpu.CompilerParams(
             dimension_semantics=("arbitrary",), vmem_limit_bytes=28 * 1024 * 1024
@@ -283,51 +291,39 @@
     )(coded, mean_square)
 
 
+def scattered(pieces, axis):
+    count = lax.axis_size(axis)
+    twice = jnp.concatenate([pieces, pieces], axis=0)
+    turned = lax.dynamic_slice_in_dim(twice, lax.axis_index(axis), count, 0)
+    total = turned[0]
+    for by in range(1, count):
+        pairs = [(i, (i + by) % count) for i in range(count)]
+        total = total + lax.ppermute(turned[by], axis, pairs)
+    return total
+
+
 def with_partner(array, axis, bit):
     pairs = [(i, i ^ bit) for i in range(lax.axis_size(axis))]
-    return lax.ppermute(array, axis, pairs)
-
-
-def half_summed(halves, axis, bit):
-    mine = (lax.axis_index(axis) // bit) % 2 == 0
-    kept = jnp.where(mine, halves[0], halves[1])
-    given = jnp.where(mine, halves[1], halves[0])
-    return kept + with_partner(given, axis, bit)
+    return array + lax.ppermute(array, axis, pairs)
 
 
 def summed_for_owner(squares):
     z, x, core = (lax.axis_size(axis) for axis in CTX)
-    bit = lax.axis_size("ch") // 2
-    while bit:
-        squares = squares + with_partner(squares, "ch", bit)
-        bit //= 2
     squares = squares.reshape(z, x, core, 2, BLOCK).transpose(2, 1, 0, 3, 4)
-    for axis, count in ((CTX[2], core), (CTX[1], x), (CTX[0], z)):
-        bit = count // 2
-        while bit:
-            squares = squares.reshape(2, squares.shape[0] // 2, *squares.shape[1:])
-            squares = half_summed(squares, axis, bit)
-            bit //= 2
-        squares = squares.reshape(squares.shape[1:])
+    for axis in reversed(CTX):
+        squares = scattered(squares, axis)
     return squares
 
 
 def shards(streams, short_taps, pole_rates, residues, skip, gain):
     channels = streams.shape[1]
     place = lax.axis_index(CTX)
-    gained, side, tails = mix(
+    coded, squares = mix(
         place.reshape(1), streams, short_taps, pole_rates, residues, skip, gain
     )
-    owners = gained.shape[0]
-    part = gained * side[1].reshape(owners, 2, 1, BLOCK)
-    coded = (part * jnp.abs(part) * TOP).astype(jnp.float16)
-    coded = jnp.pad(coded.reshape(owners, 2 * channels, BLOCK), ((0, 0), (0, 8), (0, 0)))
-    coded = lax.optimization_barrier(coded)
-    coded = lax.dynamic_update_slice(
-        coded, tails.astype(jnp.float16), (0, 2 * channels, 0)
-    )
-    moved = lax.all_to_all(coded, CTX, 0, 0, tiled=True)
-    mean_square = summed_for_owner(side[0]) / D
+    squares = with_partner(squares, "ch", 1)
+    moved = lax.all_to_all(coded.astype(jnp.float16), CTX, 0, 0, tiled=True)
+    mean_square = summed_for_owner(with_partner(squares, "ch", 2)) / D
     return finish(moved.astype(jnp.float32), mean_square, channels)
 
 

time: 72.7 us -> 62.4 us (0.86)
  waiting for transfers between devices: 33.7 us -> 13.9 us
  starting transfers between devices: 26.9 us -> 37.5 us
  local copies, waits for them, and re-layouts: 1.3 us -> 0.04 us
    ppermute x8 -> x13, waiting for transfers between devices: 33.7 us -> 13.9 us  [the longest x11 8.61 us: scattered(): total = total + lax.ppermute(turned[by], axis, pairs)]
    ppermute x8 -> x13, starting transfers between devices: 14.8 us -> 25.4 us  [the longest x11 20.5 us: scattered(): total = total + lax.ppermute(turned[by], axis, pairs)]
    pad x1 -> x0, local copies, waits for them, and re-layouts: 1.26 us -> none  [shards(): jnp.pad(coded.reshape(owners, 2 * channels, BLOCK), ((0, 0), (0, 8), (0,...]
    convert_element_type x1, other arithmetic: 0.44 us -> 1.2 us  [shards(): moved = lax.all_to_all(coded.astype(jnp.float16), CTX, 0, 0, tiled=True)]
  transfers between devices with their start and end apart: 9 -> 14, of which waited for: 7 -> 6; matrix products, arithmetic and copies ran while one was open for 3% -> 0% of each run, Pallas kernels for 0% -> 0%
where the time goes in v7:
time: 62.4 us; the launch traced here: 62.2 us
  starting transfers between devices  37.5 us (60%)
  waiting for transfers between devices  13.9 us (22%)
  Pallas kernels  9.17 us (15%)
  other arithmetic  1.55 us (2%)
    ppermute x11, starting transfers between devices, scattered(): total = total + lax.ppermute(turned[by], axis, pairs)  20.5 us
    all_to_all x1, starting transfers between devices, shards(): moved = lax.all_to_all(coded.astype(jnp.float16), CTX, 0, 0, tiled=True)  12 us
    ppermute x11, waiting for transfers between devices, scattered(): total = total + lax.ppermute(turned[by], axis, pairs)  8.61 us
    pallas_call x1, Pallas kernels, mix(): pl.pallas_call(mix_kernel, name='mix', grid_spec=pltpu.PrefetchScalarGrid...  7.34 us
    ppermute x2, waiting for transfers between devices, with_partner(): return array + lax.ppermute(array, axis, pairs)  5.28 us
    ppermute x2, starting transfers between devices, with_partner(): return array + lax.ppermute(array, axis, pairs)  4.93 us
    pallas_call x1, Pallas kernels, finish(): pl.pallas_call(finish_kernel, name='finish', grid=(owners // AT_ONCE,), i...  1.82 us
  transfers between devices with their start and end apart: 14, of which 6 were waited for; matrix products, arithmetic and copies ran while one was open for 0% of the time, Pallas kernels for 0%

profile of v7, /device:TPU:2, one launch (start us, length us, event | category | flops | bytes accessed | tf_op | source)
XLA Modules:
  0.0 62.2 jit_solution(535600603203207839)
XLA Ops:
  0.0 7.3 %mix.1 = (f32[64,72,128]{2,1,0:T(8,128)S(1)}, f32[128,128]{1,0:T(8,128)S(1)}) custom-call(s32[1]{0:T(128)} %bitcast.place, bf16[3,32,16384]{2,1,0:T(8,128)(2,1)} %far.1, f32[3,7,128]{2,1,0:T(8,128)} %bitcast.62, f32[16,128]{1,0:T(8,128)} %bitcast.63, f32[16,128]{1,0:T(8,128)} %bitcast.64, f32[16,128]{1,0:T(8,128)} %bitcast.65, f32[16,128]{1,0:T(8,128)} %bitcast.66), custom_call_target="tpu_custom_call" | custom-call | tf_op jit(solution)/shard_map/mix/pallas_call | solution.py:213
  7.4 1.2 %convert_element_type.6 = f16[64,72,128]{2,1,0:T(8,128)(2,1)} convert(f32[64,72,128]{2,1,0:T(8,128)S(1)} %get-tuple-element.7) | non-fusion elementwise | flops 589824 | bytes 3538944 | tf_op jit(solution)/shard_map/convert_element_type | solution.py:325
  8.6 12.0 %all-to-all-start = ((f16[64,72,128]{2,1,0:T(8,128)(2,1)}), f16[64,72,128]{2,1,0:T(8,128)(2,1)S(1)}, u32[]{:S(2)}, u32[]{:S(2)}) async-start(f16[64,72,128]{2,1,0:T(8,128)(2,1)} %convert_element_type.6), calls=%async_computation | async-start | bytes 2359296 | tf_op jit(solution)/shard_map/all_to_all | solution.py:325
  20.6 1.7 %collective-permute-start = (f32[128,128]{1,0:T(8,128)S(1)}, f32[128,128]{1,0:T(8,128)S(1)}, u32[]{:S(2)}, u32[]{:S(2)}) collective-permute-start(f32[128,128]{1,0:T(8,128)S(1)} %get-tuple-element.8), channel_id=1, source_target_pairs={{0,1},{1,0},{2,3},{3,2},{4,5},{5,4},{6,7},{7,6},{8,9},{9,8},{10,11... | collective-permute-start | bytes 196616 | tf_op jit(solution)/shard_map/ppermute | solution.py:307
  22.2 2.7 %collective-permute-done = f32[128,128]{1,0:T(8,128)S(1)} collective-permute-done((f32[128,128]{1,0:T(8,128)S(1)}, f32[128,128]{1,0:T(8,128)S(1)}, u32[]{:S(2)}, u32[]{:S(2)}) %collective-permute-start) | collective-permute-done | bytes 65568 | tf_op jit(solution)/shard_map/ppermute | solution.py:307
  24.9 3.3 %collective-permute-start.1 = (f32[128,128]{1,0:T(8,128)S(1)}, f32[128,128]{1,0:T(8,128)S(1)}, u32[]{:S(2)}, u32[]{:S(2)}) collective-permute-start(f32[128,128]{1,0:T(8,128)S(1)} %add.56), channel_id=1, source_target_pairs={{0,2},{1,3},{2,0},{3,1},{4,6},{5,7},{6,4},{7,5},{8,10},{9,11},{10,... | collective-permute-start | bytes 196616 | tf_op jit(solution)/shard_map/ppermute | solution.py:307
  28.2 2.6 %collective-permute-done.1 = f32[128,128]{1,0:T(8,128)S(1)} collective-permute-done((f32[128,128]{1,0:T(8,128)S(1)}, f32[128,128]{1,0:T(8,128)S(1)}, u32[]{:S(2)}, u32[]{:S(2)}) %collective-permute-start.1) | collective-permute-done | bytes 65568 | tf_op jit(solution)/shard_map/ppermute | solution.py:307
  30.9 0.1 collective-permute-start.2
  31.0 1.2 %collective-permute-done.2 = f32[4,8,2,128]{3,2,1,0:T(2,128)S(1)} collective-permute-done((f32[4,8,2,128]{3,2,1,0:T(2,128)S(1)}, f32[4,8,2,128]{3,2,1,0:T(2,128)S(1)}, u32[]{:S(2)}, u32[]{:S(2)}) %collective-permute-start.2) | collective-permute-done | bytes 32800 | tf_op jit(solution)/shard_map/ppermute | solution.py:301
  32.3 1.5 %collective-permute-start.3 = (f32[8,2,128]{2,1,0:T(2,128)S(1)}, f32[8,2,128]{2,1,0:T(2,128)S(1)}, u32[]{:S(2)}, u32[]{:S(2)}) collective-permute-start(f32[8,2,128]{2,1,0:T(2,128)S(1)} %get-tuple-element.9), channel_id=1, source_target_pairs={{0,8},{8,16},{16,24},{24,0},{1,9},{9,17},{17,25},{25,1},{2,10},{10... | collective-permute-start | bytes 24584 | tf_op jit(solution)/shard_map/ppermute | solution.py:301
  33.9 1.1 %collective-permute-start.4 = (f32[8,2,128]{2,1,0:T(2,128)S(1)}, f32[8,2,128]{2,1,0:T(2,128)S(1)}, u32[]{:S(2)}, u32[]{:S(2)}) collective-permute-start(f32[8,2,128]{2,1,0:T(2,128)S(1)} %get-tuple-element.10), channel_id=1, source_target_pairs={{0,16},{8,24},{16,0},{24,8},{1,17},{9,25},{17,1},{25,9},{2,18},{10... | collective-permute-start | bytes 24584 | tf_op jit(solution)/shard_map/ppermute | solution.py:301
  34.9 2.2 %collective-permute-start.5 = (f32[8,2,128]{2,1,0:T(2,128)S(1)}, f32[8,2,128]{2,1,0:T(2,128)S(1)}, u32[]{:S(2)}, u32[]{:S(2)}) collective-permute-start(f32[8,2,128]{2,1,0:T(2,128)S(1)} %get-tuple-element.11), channel_id=1, source_target_pairs={{0,24},{8,0},{16,8},{24,16},{1,25},{9,1},{17,9},{25,17},{2,26},{10... | collective-permute-start | bytes 24584 | tf_op jit(solution)/shard_map/ppermute | solution.py:301
  37.1 2.1 %collective-permute-done.4 = f32[8,2,128]{2,1,0:T(2,128)S(1)} collective-permute-done((f32[8,2,128]{2,1,0:T(2,128)S(1)}, f32[8,2,128]{2,1,0:T(2,128)S(1)}, u32[]{:S(2)}, u32[]{:S(2)}) %collective-permute-start.4) | collective-permute-done | bytes 8224 | tf_op jit(solution)/shard_map/ppermute | solution.py:301
  39.2 4.7 %collective-permute-start.10 = (f32[2,128]{1,0:T(2,128)S(1)}, f32[2,128]{1,0:T(2,128)S(1)}, u32[]{:S(2)}, u32[]{:S(2)}) collective-permute-start(f32[2,128]{1,0:T(2,128)S(1)} %get-tuple-element.14), channel_id=1, source_target_pairs={{0,160},{32,192},{64,224},{96,0},{128,32},{160,64},{192,96},{224,1... | collective-permute-start | bytes 3080 | tf_op jit(solution)/shard_map/ppermute | solution.py:301
  44.0 1.2 %collective-permute-start.11 = (f32[2,128]{1,0:T(2,128)S(1)}, f32[2,128]{1,0:T(2,128)S(1)}, u32[]{:S(2)}, u32[]{:S(2)}) collective-permute-start(f32[2,128]{1,0:T(2,128)S(1)} %get-tuple-element.13), channel_id=1, source_target_pairs={{0,192},{32,224},{64,0},{96,32},{128,64},{160,96},{192,128},{224,1... | collective-permute-start | bytes 3080 | tf_op jit(solution)/shard_map/ppermute | solution.py:301
  45.2 0.6 collective-permute-start.12
  45.8 1.4 %collective-permute-start.6 = (f32[2,128]{1,0:T(2,128)S(1)}, f32[2,128]{1,0:T(2,128)S(1)}, u32[]{:S(2)}, u32[]{:S(2)}) collective-permute-start(f32[2,128]{1,0:T(2,128)S(1)} %get-tuple-element.12), channel_id=1, source_target_pairs={{0,32},{32,64},{64,96},{96,128},{128,160},{160,192},{192,224},{224... | collective-permute-start | bytes 3080 | tf_op jit(solution)/shard_map/ppermute | solution.py:301
  47.2 1.7 %collective-permute-start.7 = (f32[2,128]{1,0:T(2,128)S(1)}, f32[2,128]{1,0:T(2,128)S(1)}, u32[]{:S(2)}, u32[]{:S(2)}) collective-permute-start(f32[2,128]{1,0:T(2,128)S(1)} %get-tuple-element.17), channel_id=1, source_target_pairs={{0,64},{32,96},{64,128},{96,160},{128,192},{160,224},{192,0},{224,... | collective-permute-start | bytes 3080 | tf_op jit(solution)/shard_map/ppermute | solution.py:301
  48.9 3.8 %collective-permute-start.8 = (f32[2,128]{1,0:T(2,128)S(1)}, f32[2,128]{1,0:T(2,128)S(1)}, u32[]{:S(2)}, u32[]{:S(2)}) collective-permute-start(f32[2,128]{1,0:T(2,128)S(1)} %get-tuple-element.16), channel_id=1, source_target_pairs={{0,96},{32,128},{64,160},{96,192},{128,224},{160,0},{192,32},{224,... | collective-permute-start | bytes 3080 | tf_op jit(solution)/shard_map/ppermute | solution.py:301
  52.7 2.1 %collective-permute-start.9 = (f32[2,128]{1,0:T(2,128)S(1)}, f32[2,128]{1,0:T(2,128)S(1)}, u32[]{:S(2)}, u32[]{:S(2)}) collective-permute-start(f32[2,128]{1,0:T(2,128)S(1)} %get-tuple-element.15), channel_id=1, source_target_pairs={{0,128},{32,160},{64,192},{96,224},{128,0},{160,32},{192,64},{224,... | collective-permute-start | bytes 3080 | tf_op jit(solution)/shard_map/ppermute | solution.py:301
  54.9 0.6 %collective-permute-done.8 = f32[2,128]{1,0:T(2,128)S(1)} collective-permute-done((f32[2,128]{1,0:T(2,128)S(1)}, f32[2,128]{1,0:T(2,128)S(1)}, u32[]{:S(2)}, u32[]{:S(2)}) %collective-permute-start.8) | collective-permute-done | bytes 1056 | tf_op jit(solution)/shard_map/ppermute | solution.py:301
  55.5 4.7 %collective-permute-done.9 = f32[2,128]{1,0:T(2,128)S(1)} collective-permute-done((f32[2,128]{1,0:T(2,128)S(1)}, f32[2,128]{1,0:T(2,128)S(1)}, u32[]{:S(2)}, u32[]{:S(2)}) %collective-permute-start.9) | collective-permute-done | bytes 1056 | tf_op jit(solution)/shard_map/ppermute | solution.py:301
  60.2 0.2 convert_element_type.7.coded
  60.4 1.8 %finish.1 = bf16[2048,256]{1,0:T(8,128)(2,1)} custom-call(f32[64,72,128]{2,1,0:T(8,128)S(1)} %convert_element_type.7.coded, f32[2,128]{1,0:T(2,128)S(1)} %add_multiply_fusion.mean_square), custom_call_target="tpu_custom_call" | custom-call | tf_op jit(solution)/shard_map/finish/pallas_call | solution.py:278
  (20 shorter events, 0.3 us)
Async XLA Ops:
  8.6 51.7 %all-to-all-start = ((f16[64,72,128]{2,1,0:T(8,128)(2,1)}), f16[64,72,128]{2,1,0:T(8,128)(2,1)S(1)}, u32[]{:S(2)}, u32[]{:S(2)}) async-start(f16[64,72,128]{2,1,0:T(8,128)(2,1)} %convert_element_type.6), calls=%async_computation | async-start | bytes 2359296 | tf_op jit(solution)/shard_map/all_to_all | solution.py:325
  20.6 4.4 %collective-permute-start = (f32[128,128]{1,0:T(8,128)S(1)}, f32[128,128]{1,0:T(8,128)S(1)}, u32[]{:S(2)}, u32[]{:S(2)}) collective-permute-start(f32[128,128]{1,0:T(8,128)S(1)} %get-tuple-element.8), channel_id=1, source_target_pairs={{0,1},{1,0},{2,3},{3,2},{4,5},{5,4},{6,7},{7,6},{8,9},{9,8},{10,11... | collective-permute-start | bytes 196616 | tf_op jit(solution)/shard_map/ppermute | solution.py:307
  24.9 5.9 %collective-permute-start.1 = (f32[128,128]{1,0:T(8,128)S(1)}, f32[128,128]{1,0:T(8,128)S(1)}, u32[]{:S(2)}, u32[]{:S(2)}) collective-permute-start(f32[128,128]{1,0:T(8,128)S(1)} %add.56), channel_id=1, source_target_pairs={{0,2},{1,3},{2,0},{3,1},{4,6},{5,7},{6,4},{7,5},{8,10},{9,11},{10,... | collective-permute-start | bytes 196616 | tf_op jit(solution)/shard_map/ppermute | solution.py:307
  30.9 1.3 %collective-permute-start.2 = (f32[4,8,2,128]{3,2,1,0:T(2,128)S(1)}, f32[4,8,2,128]{3,2,1,0:T(2,128)S(1)}, u32[]{:S(2)}, u32[]{:S(2)}) collective-permute-start(f32[4,8,2,128]{3,2,1,0:T(2,128)S(1)} %slice_bitcast_fusion), channel_id=1, source_target_pairs={{0,4},{4,0},{1,5},{5,1},{2,6},{6,2},{3,7},{7,3},{8,12},{12,8},{9,1... | collective-permute-start | bytes 98312 | tf_op jit(solution)/shard_map/ppermute | solution.py:301
  32.3 4.8 %collective-permute-start.3 = (f32[8,2,128]{2,1,0:T(2,128)S(1)}, f32[8,2,128]{2,1,0:T(2,128)S(1)}, u32[]{:S(2)}, u32[]{:S(2)}) collective-permute-start(f32[8,2,128]{2,1,0:T(2,128)S(1)} %get-tuple-element.9), channel_id=1, source_target_pairs={{0,8},{8,16},{16,24},{24,0},{1,9},{9,17},{17,25},{25,1},{2,10},{10... | collective-permute-start | bytes 24584 | tf_op jit(solution)/shard_map/ppermute | solution.py:301
  33.9 5.3 %collective-permute-start.4 = (f32[8,2,128]{2,1,0:T(2,128)S(1)}, f32[8,2,128]{2,1,0:T(2,128)S(1)}, u32[]{:S(2)}, u32[]{:S(2)}) collective-permute-start(f32[8,2,128]{2,1,0:T(2,128)S(1)} %get-tuple-element.10), channel_id=1, source_target_pairs={{0,16},{8,24},{16,0},{24,8},{1,17},{9,25},{17,1},{25,9},{2,18},{10... | collective-permute-start | bytes 24584 | tf_op jit(solution)/shard_map/ppermute | solution.py:301
  34.9 4.2 %collective-permute-start.5 = (f32[8,2,128]{2,1,0:T(2,128)S(1)}, f32[8,2,128]{2,1,0:T(2,128)S(1)}, u32[]{:S(2)}, u32[]{:S(2)}) collective-permute-start(f32[8,2,128]{2,1,0:T(2,128)S(1)} %get-tuple-element.11), channel_id=1, source_target_pairs={{0,24},{8,0},{16,8},{24,16},{1,25},{9,1},{17,9},{25,17},{2,26},{10... | collective-permute-start | bytes 24584 | tf_op jit(solution)/shard_map/ppermute | solution.py:301
  39.2 9.7 %collective-permute-start.10 = (f32[2,128]{1,0:T(2,128)S(1)}, f32[2,128]{1,0:T(2,128)S(1)}, u32[]{:S(2)}, u32[]{:S(2)}) collective-permute-start(f32[2,128]{1,0:T(2,128)S(1)} %get-tuple-element.14), channel_id=1, source_target_pairs={{0,160},{32,192},{64,224},{96,0},{128,32},{160,64},{192,96},{224,1... | collective-permute-start | bytes 3080 | tf_op jit(solution)/shard_map/ppermute | solution.py:301
  44.0 8.8 %collective-permute-start.11 = (f32[2,128]{1,0:T(2,128)S(1)}, f32[2,128]{1,0:T(2,128)S(1)}, u32[]{:S(2)}, u32[]{:S(2)}) collective-permute-start(f32[2,128]{1,0:T(2,128)S(1)} %get-tuple-element.13), channel_id=1, source_target_pairs={{0,192},{32,224},{64,0},{96,32},{128,64},{160,96},{192,128},{224,1... | collective-permute-start | bytes 3080 | tf_op jit(solution)/shard_map/ppermute | solution.py:301
  45.2 9.7 %collective-permute-start.12 = (f32[2,128]{1,0:T(2,128)S(1)}, f32[2,128]{1,0:T(2,128)S(1)}, u32[]{:S(2)}, u32[]{:S(2)}) collective-permute-start(f32[2,128]{1,0:T(2,128)S(1)} %get-tuple-element.18), channel_id=1, source_target_pairs={{0,224},{32,0},{64,32},{96,64},{128,96},{160,128},{192,160},{224,1... | collective-permute-start | bytes 3080 | tf_op jit(solution)/shard_map/ppermute | solution.py:301
  45.8 9.1 %collective-permute-start.6 = (f32[2,128]{1,0:T(2,128)S(1)}, f32[2,128]{1,0:T(2,128)S(1)}, u32[]{:S(2)}, u32[]{:S(2)}) collective-permute-start(f32[2,128]{1,0:T(2,128)S(1)} %get-tuple-element.12), channel_id=1, source_target_pairs={{0,32},{32,64},{64,96},{96,128},{128,160},{160,192},{192,224},{224... | collective-permute-start | bytes 3080 | tf_op jit(solution)/shard_map/ppermute | solution.py:301
  47.2 7.6 %collective-permute-start.7 = (f32[2,128]{1,0:T(2,128)S(1)}, f32[2,128]{1,0:T(2,128)S(1)}, u32[]{:S(2)}, u32[]{:S(2)}) collective-permute-start(f32[2,128]{1,0:T(2,128)S(1)} %get-tuple-element.17), channel_id=1, source_target_pairs={{0,64},{32,96},{64,128},{96,160},{128,192},{160,224},{192,0},{224,... | collective-permute-start | bytes 3080 | tf_op jit(solution)/shard_map/ppermute | solution.py:301
  48.9 6.6 %collective-permute-start.8 = (f32[2,128]{1,0:T(2,128)S(1)}, f32[2,128]{1,0:T(2,128)S(1)}, u32[]{:S(2)}, u32[]{:S(2)}) collective-permute-start(f32[2,128]{1,0:T(2,128)S(1)} %get-tuple-element.16), channel_id=1, source_target_pairs={{0,96},{32,128},{64,160},{96,192},{128,224},{160,0},{192,32},{224,... | collective-permute-start | bytes 3080 | tf_op jit(solution)/shard_map/ppermute | solution.py:301
  52.7 7.5 %collective-permute-start.9 = (f32[2,128]{1,0:T(2,128)S(1)}, f32[2,128]{1,0:T(2,128)S(1)}, u32[]{:S(2)}, u32[]{:S(2)}) collective-permute-start(f32[2,128]{1,0:T(2,128)S(1)} %get-tuple-element.15), channel_id=1, source_target_pairs={{0,128},{32,160},{64,192},{96,224},{128,0},{160,32},{192,64},{224,... | collective-permute-start | bytes 3080 | tf_op jit(solution)/shard_map/ppermute | solution.py:301

commit v8 on v7

--- a/solution.py
+++ b/solution.py
@@ -11,7 +11,6 @@
 WIDTH = 16
 CTX = ("ctx_0", "ctx_1", "ctx_2")
 CH_CTX = ("ch", "ctx_0", "ctx_1", "ctx_2")
-CHUNK = 128
 UNDER = 4
 TOP = 32768.0
 TINY = 1e-37
@@ -47,31 +46,14 @@
     return pltpu.roll(spread, 0, 1, stride=1, stride_axis=0)
 
 
-def mix_kernel(
-    place, far, short_taps, rates, residues, skip, gain, coded_out, square_out,
-    taps_w, conv_w, lift_w, first, direct, ends, starts, squares, peaks, streams, arrived,
-    gained, inverses,
-):
-    blocks = streams.shape[2] // BLOCK
-    turn = pl.program_id(0)
-
-    def fetch(g, chunk):
-        lanes = pl.ds(chunk * CHUNK * BLOCK, CHUNK * BLOCK)
-        at = (slice(None), pl.ds(pl.multiple_of(g * WIDTH, WIDTH), WIDTH), lanes)
-        return pltpu.make_async_copy(far.at[at], streams.at[at], arrived.at[g, chunk])
-
-    @pl.when(turn == 0)
-    def _():
-        for g in range(streams.shape[1] // WIDTH):
-            for chunk in range(blocks // CHUNK):
-                fetch(g, chunk).start()
-
-    channel_rows = pl.ds(pl.multiple_of(turn * WIDTH, WIDTH), WIDTH)
-    group = place[0] * pl.num_programs(0) + pl.program_id(0)
+def all_rows(column, blocks):
+    width = column.shape[0]
+    return jnp.broadcast_to(column[None], (blocks, width, BLOCK)).reshape(blocks * width, BLOCK)
+
+
+def weights(group, short_taps, rates, residues, taps_w, conv_w, lift_w):
     rate = picked_column(rates[...], group, 0)
     residue = picked_column(residues[...], group, 0)
-    skip_column = channel_column(skip, group)
-    gain_column = channel_column(gain, group)
     zero = jnp.zeros((BLOCK, BLOCK), jnp.bfloat16)
 
     for m in range(3):
@@ -101,41 +83,15 @@
         [high, high, low, jnp.zeros((BLOCK - 3 * WIDTH, BLOCK), jnp.bfloat16)], axis=0
     )
 
-    skip_rows = jnp.broadcast_to(
-        skip_column[None], (CHUNK, WIDTH, BLOCK)
-    ).reshape(CHUNK * WIDTH, BLOCK)
-    gain_rows = jnp.broadcast_to(
-        gain_column[None], (CHUNK, WIDTH, BLOCK)
-    ).reshape(CHUNK * WIDTH, BLOCK)
-    for chunk in range(blocks // CHUNK):
-        span = pl.ds(chunk * CHUNK * WIDTH, CHUNK * WIDTH)
-        fetch(turn, chunk).wait()
-        filtered = []
-        for m in range(3):
-            pieces = []
-            for n in range(chunk * CHUNK, (chunk + 1) * CHUNK):
-                if n == 0:
-                    here = streams[m, channel_rows, :BLOCK]
-                    pieces.append(jnp.concatenate([jnp.zeros_like(here), here], axis=1))
-                else:
-                    pieces.append(streams[m, channel_rows, (n - 1) * BLOCK : (n + 1) * BLOCK])
-            both = jnp.dot(
-                jnp.concatenate(pieces, axis=0), taps_w[m], preferred_element_type=jnp.float32
-            )
-            filtered.append(both[:, :BLOCK] + both[:, BLOCK:])
-        product = filtered[1] * filtered[2]
-        high, low = split(product)
-        terms = jnp.dot(
-            jnp.concatenate([high, low], axis=1), conv_w[...], preferred_element_type=jnp.float32
-        )
-        first[span, :] = filtered[0]
-        direct[span, :] = (terms[:, :BLOCK] + terms[:, BLOCK : 2 * BLOCK]) + skip_rows * product
-        ends[span, :] = terms[:, 2 * BLOCK : 3 * BLOCK] + terms[:, 3 * BLOCK :]
-
     decay_column = jnp.exp(-rate * float(BLOCK))
     decay = jnp.broadcast_to(
         row_of(jnp.concatenate([decay_column] * 3, axis=0), BLOCK), (WIDTH, BLOCK)
     )
+    return decay
+
+
+def scan(decay, ends, starts):
+    blocks = ends.shape[0] // WIDTH
     lane = lax.broadcasted_iota(jnp.int32, (WIDTH, BLOCK), 1)
     takes_low = (lane >= WIDTH) & (lane < 2 * WIDTH)
     state = jnp.zeros((WIDTH, BLOCK), jnp.float32)
@@ -153,49 +109,102 @@
             starts[at[k], :] = jnp.where(takes_low, states[k] - high, high).astype(jnp.bfloat16)
         state = states[UNDER]
 
-    for chunk in range(blocks // CHUNK):
-        span = pl.ds(chunk * CHUNK * WIDTH, CHUNK * WIDTH)
-        carried = jnp.dot(starts[span, :], lift_w[...], preferred_element_type=jnp.float32)
-        gated = first[span, :] * (direct[span, :] + carried)
-        sized = gated * gain_rows
-        gained[turn, span, :] = sized
-        squared = (gated * gated).reshape(CHUNK, 2, 8, BLOCK)
-        squared = (squared[:, 0] + squared[:, 1]).reshape(CHUNK * 8, BLOCK)
-        size = jnp.abs(sized).reshape(CHUNK, 2, 8, BLOCK)
-        size = jnp.maximum(size[:, 0], size[:, 1]).reshape(CHUNK * 8, BLOCK)
-        rows = pl.ds(chunk * CHUNK * 8, CHUNK * 8)
-
-        @pl.when(pl.program_id(0) == 0)
-        def _():
-            squares[rows, :] = squared
-            peaks[rows, :] = size
-
-        @pl.when(pl.program_id(0) != 0)
-        def _():
-            squares[rows, :] = squares[rows, :] + squared
-            peaks[rows, :] = jnp.maximum(peaks[rows, :], size)
-
-    @pl.when(pl.program_id(0) == pl.num_programs(0) - 1)
-    def _():
-        total = squares[pl.ds(0, blocks, stride=8), :]
-        peak = jnp.maximum(peaks[pl.ds(0, blocks, stride=8), :], TINY)
-        for row in range(1, 8):
-            total = total + squares[pl.ds(row, blocks, stride=8), :]
-            peak = jnp.maximum(peak, peaks[pl.ds(row, blocks, stride=8), :])
-        exponent = jnp.ceil(jnp.log2(peak))
-        inverse = jnp.exp2(-exponent)
-        square_out[...] = total
-        inverses[...] = inverse
-        local = streams.shape[1]
-        for n in range(blocks):
-            times = jnp.broadcast_to(inverses[pl.ds(n, 1), :], (WIDTH, BLOCK))
-            for g in range(local // WIDTH):
-                part = gained[g, pl.ds(n * WIDTH, WIDTH), :] * times
-                row = (n % 2) * local + g * WIDTH
-                coded_out[n // 2, row : row + WIDTH, :] = part * jnp.abs(part) * TOP
-        owners = blocks // 2
-        coded_out[:, 2 * local : 2 * local + 2, :] = exponent.reshape(owners, 2, BLOCK)
-        coded_out[:, 2 * local + 2 :, :] = jnp.zeros((owners, 6, BLOCK), jnp.float32)
+
+def mix_kernel(
+    place, far, far_taps, far_rates, far_residues, far_skip, far_gain, coded_out, square_out,
+    short_taps, rates, residues, skip, gain, streams, arrived,
+    taps_w, conv_w, lift_w, first, direct, ends, starts, squares, peaks, gained, inverses,
+):
+    blocks = streams.shape[2] // BLOCK
+    local = streams.shape[1]
+    groups = local // WIDTH
+    everything = slice(None)
+    smalls = [
+        pltpu.make_async_copy(source, target, arrived.at[3 * groups + at])
+        for at, (source, target) in enumerate(
+            (
+                (far_taps, short_taps), (far_rates, rates), (far_residues, residues),
+                (far_skip, skip), (far_gain, gain),
+            )
+        )
+    ]
+    bulks = []
+    for g in range(groups):
+        for m in range(3):
+            at = (m, pl.ds(g * WIDTH, WIDTH), everything)
+            bulks.append(
+                pltpu.make_async_copy(far.at[at], streams.at[at], arrived.at[3 * g + m])
+            )
+    for copy in smalls + bulks:
+        copy.start()
+    for copy in smalls:
+        copy.wait()
+    decays = []
+    for g in range(groups):
+        decays.append(
+            weights(
+                place[0] * groups + g, short_taps, rates, residues,
+                taps_w.at[g], conv_w.at[g], lift_w.at[g],
+            )
+        )
+    for g in range(groups):
+        for copy in bulks[3 * g : 3 * g + 3]:
+            copy.wait()
+        filtered = []
+        for m in range(3):
+            pieces = []
+            for n in range(blocks):
+                rows = slice(g * WIDTH, (g + 1) * WIDTH)
+                if n == 0:
+                    here = streams[m, rows, :BLOCK]
+                    pieces.append(jnp.concatenate([jnp.zeros_like(here), here], axis=1))
+                else:
+                    pieces.append(streams[m, rows, (n - 1) * BLOCK : (n + 1) * BLOCK])
+            both = jnp.dot(
+                jnp.concatenate(pieces, axis=0), taps_w[g, m], preferred_element_type=jnp.float32
+            )
+            filtered.append(both[:, :BLOCK] + both[:, BLOCK:])
+        product = filtered[1] * filtered[2]
+        high, low = split(product)
+        terms = jnp.dot(
+            jnp.concatenate([high, low], axis=1), conv_w[g], preferred_element_type=jnp.float32
+        )
+        skip_rows = all_rows(channel_column(skip, place[0] * groups + g), blocks)
+        first[g] = filtered[0]
+        direct[g] = (terms[:, :BLOCK] + terms[:, BLOCK : 2 * BLOCK]) + skip_rows * product
+        ends[g] = terms[:, 2 * BLOCK : 3 * BLOCK] + terms[:, 3 * BLOCK :]
+        scan(decays[g], ends.at[g], starts.at[g])
+        carried = jnp.dot(starts[g], lift_w[g], preferred_element_type=jnp.float32)
+        gated = first[g] * (direct[g] + carried)
+        sized = gated * all_rows(channel_column(gain, place[0] * groups + g), blocks)
+        gained[g] = sized
+        squared = (gated * gated).reshape(blocks, 2, 8, BLOCK)
+        squared = (squared[:, 0] + squared[:, 1]).reshape(blocks * 8, BLOCK)
+        size = jnp.abs(sized).reshape(blocks, 2, 8, BLOCK)
+        size = jnp.maximum(size[:, 0], size[:, 1]).reshape(blocks * 8, BLOCK)
+        if g:
+            squared = squares[...] + squared
+            size = jnp.maximum(peaks[...], size)
+        squares[...] = squared
+        peaks[...] = size
+
+    total = squares[pl.ds(0, blocks, stride=8), :]
+    peak = jnp.maximum(peaks[pl.ds(0, blocks, stride=8), :], TINY)
+    for row in range(1, 8):
+        total = total + squares[pl.ds(row, blocks, stride=8), :]
+        peak = jnp.maximum(peak, peaks[pl.ds(row, blocks, stride=8), :])
+    exponent = jnp.ceil(jnp.log2(peak))
+    inverses[...] = jnp.exp2(-exponent)
+    square_out[...] = total
+    for n in range(blocks):
+        times = jnp.broadcast_to(inverses[pl.ds(n, 1), :], (WIDTH, BLOCK))
+        for g in range(groups):
+            part = gained[g, pl.ds(n * WIDTH, WIDTH), :] * times
+            row = (n % 2) * local + g * WIDTH
+            coded_out[n // 2, row : row + WIDTH, :] = part * jnp.abs(part) * TOP
+    owners = blocks // 2
+    coded_out[:, 2 * local : 2 * local + 2, :] = exponent.reshape(owners, 2, BLOCK)
+    coded_out[:, 2 * local + 2 :, :] = jnp.zeros((owners, 6, BLOCK), jnp.float32)
 
 
 def mix(place, streams, short_taps, rates, residues, skip, gain):
@@ -209,37 +218,31 @@
     skip = skip.reshape(-1, BLOCK)
     gain = gain.reshape(-1, BLOCK)
     shape = (blocks // 2, 2 * channels + 8, BLOCK)
-    whole = lambda array: pl.BlockSpec(array.shape, lambda g, place: (0,) * array.ndim)
+    inputs = (streams, short_taps, rates, residues, skip, gain)
     return pl.pallas_call(
         mix_kernel,
         name="mix",
         grid_spec=pltpu.PrefetchScalarGridSpec(
             num_scalar_prefetch=1,
-            grid=(groups,),
-            in_specs=[
-                pl.BlockSpec(memory_space=pltpu.HBM),
-                whole(short_taps),
-                whole(rates),
-                whole(residues),
-                whole(skip),
-                whole(gain),
-            ],
+            grid=(1,),
+            in_specs=[pl.BlockSpec(memory_space=pltpu.HBM)] * len(inputs),
             out_specs=[
                 pl.BlockSpec(shape, lambda g, place: (0, 0, 0)),
                 pl.BlockSpec((blocks, BLOCK), lambda g, place: (0, 0)),
             ],
             scratch_shapes=[
-                pltpu.VMEM((3, 2 * BLOCK, 2 * BLOCK), jnp.bfloat16),
-                pltpu.VMEM((2 * BLOCK, 4 * BLOCK), jnp.bfloat16),
-                pltpu.VMEM((BLOCK, BLOCK), jnp.bfloat16),
-                pltpu.VMEM((rows, BLOCK), jnp.float32),
-                pltpu.VMEM((rows, BLOCK), jnp.float32),
-                pltpu.VMEM((rows, BLOCK), jnp.float32),
-                pltpu.VMEM((rows, BLOCK), jnp.bfloat16),
+                *(pltpu.VMEM(array.shape, array.dtype) for array in inputs[1:]),
+                pltpu.VMEM(streams.shape, jnp.bfloat16),
+                pltpu.SemaphoreType.DMA((3 * groups + 5,)),
+                pltpu.VMEM((groups, 3, 2 * BLOCK, 2 * BLOCK), jnp.bfloat16),
+                pltpu.VMEM((groups, 2 * BLOCK, 4 * BLOCK), jnp.bfloat16),
+                pltpu.VMEM((groups, BLOCK, BLOCK), jnp.bfloat16),
+                pltpu.VMEM((groups, rows, BLOCK), jnp.float32),
+                pltpu.VMEM((groups, rows, BLOCK), jnp.float32),
+                pltpu.VMEM((groups, rows, BLOCK), jnp.float32),
+                pltpu.VMEM((groups, rows, BLOCK), jnp.bfloat16),
                 pltpu.VMEM((blocks * 8, BLOCK), jnp.float32),
                 pltpu.VMEM((blocks * 8, BLOCK), jnp.float32),
-                pltpu.VMEM(streams.shape, jnp.bfloat16),
-                pltpu.SemaphoreType.DMA((groups, blocks // CHUNK)),
                 pltpu.VMEM((groups, rows, BLOCK), jnp.float32),
                 pltpu.VMEM((blocks, BLOCK), jnp.float32),
             ],
@@ -255,7 +258,7 @@
         place,
         *(
             pltpu.with_memory_space_constraint(array, pltpu.HBM)
-            for array in (streams, short_taps, rates, residues, skip, gain)
+            for array in inputs
         ),
     )
 

time: 62.4 us -> 61.4 us (0.984)
  Pallas kernels: 9.17 us -> 8.16 us
    pallas_call x1, Pallas kernels: 7.34 us -> 6.34 us  [mix(): pl.pallas_call(mix_kernel, name='mix', grid_spec=pltpu.PrefetchScalarGrid...]
where the time goes in v8:
time: 61.4 us; the launch traced here: 61.2 us
  starting transfers between devices  37.5 us (61%)
  waiting for transfers between devices  13.9 us (23%)
  Pallas kernels  8.16 us (13%)
  other arithmetic  1.55 us (3%)
    ppermute x11, starting transfers between devices, scattered(): total = total + lax.ppermute(turned[by], axis, pairs)  20.5 us
    all_to_all x1, starting transfers between devices, shards(): moved = lax.all_to_all(coded.astype(jnp.float16), CTX, 0, 0, tiled=True)  12 us
    ppermute x11, waiting for transfers between devices, scattered(): total = total + lax.ppermute(turned[by], axis, pairs)  8.61 us
    pallas_call x1, Pallas kernels, mix(): pl.pallas_call(mix_kernel, name='mix', grid_spec=pltpu.PrefetchScalarGrid...  6.34 us
    ppermute x2, waiting for transfers between devices, with_partner(): return array + lax.ppermute(array, axis, pairs)  5.27 us
    ppermute x2, starting transfers between devices, with_partner(): return array + lax.ppermute(array, axis, pairs)  4.94 us
    pallas_call x1, Pallas kernels, finish(): pl.pallas_call(finish_kernel, name='finish', grid=(owners // AT_ONCE,), i...  1.82 us
  transfers between devices with their start and end apart: 14, of which 6 were waited for; matrix products, arithmetic and copies ran while one was open for 0% of the time, Pallas kernels for 0%

profile of v8, /device:TPU:2, one launch (start us, length us, event | category | flops | bytes accessed | tf_op | source)
XLA Modules:
  0.0 61.2 jit_solution(7077198853000646321)
XLA Ops:
  0.0 6.3 %mix.1 = (f32[64,72,128]{2,1,0:T(8,128)S(1)}, f32[128,128]{1,0:T(8,128)S(1)}) custom-call(s32[1]{0:T(128)} %bitcast.place, bf16[3,32,16384]{2,1,0:T(8,128)(2,1)} %far.1, f32[3,7,128]{2,1,0:T(8,128)} %bitcast.62, f32[16,128]{1,0:T(8,128)} %bitcast.63, f32[16,128]{1,0:T(8,128)} %bitcast.64, f32[16,128]{1,0:T(8,128)} %bitcast.65, f32[16,128]{1,0:T(8,128)} %bitcast.66), custom_call_target="tpu_custom_call" | custom-call | tf_op jit(solution)/shard_map/mix/pallas_call | solution.py:222
  6.3 1.2 %convert_element_type.6 = f16[64,72,128]{2,1,0:T(8,128)(2,1)} convert(f32[64,72,128]{2,1,0:T(8,128)S(1)} %get-tuple-element.7) | non-fusion elementwise | flops 589824 | bytes 3538944 | tf_op jit(solution)/shard_map/convert_element_type | solution.py:328
  7.5 12.0 %all-to-all-start = ((f16[64,72,128]{2,1,0:T(8,128)(2,1)}), f16[64,72,128]{2,1,0:T(8,128)(2,1)S(1)}, u32[]{:S(2)}, u32[]{:S(2)}) async-start(f16[64,72,128]{2,1,0:T(8,128)(2,1)} %convert_element_type.6), calls=%async_computation | async-start | bytes 2359296 | tf_op jit(solution)/shard_map/all_to_all | solution.py:328
  19.6 1.7 %collective-permute-start = (f32[128,128]{1,0:T(8,128)S(1)}, f32[128,128]{1,0:T(8,128)S(1)}, u32[]{:S(2)}, u32[]{:S(2)}) collective-permute-start(f32[128,128]{1,0:T(8,128)S(1)} %get-tuple-element.8), channel_id=1, source_target_pairs={{0,1},{1,0},{2,3},{3,2},{4,5},{5,4},{6,7},{7,6},{8,9},{9,8},{10,11... | collective-permute-start | bytes 196616 | tf_op jit(solution)/shard_map/ppermute | solution.py:310
  21.2 2.7 %collective-permute-done = f32[128,128]{1,0:T(8,128)S(1)} collective-permute-done((f32[128,128]{1,0:T(8,128)S(1)}, f32[128,128]{1,0:T(8,128)S(1)}, u32[]{:S(2)}, u32[]{:S(2)}) %collective-permute-start) | collective-permute-done | bytes 65568 | tf_op jit(solution)/shard_map/ppermute | solution.py:310
  23.9 3.3 %collective-permute-start.1 = (f32[128,128]{1,0:T(8,128)S(1)}, f32[128,128]{1,0:T(8,128)S(1)}, u32[]{:S(2)}, u32[]{:S(2)}) collective-permute-start(f32[128,128]{1,0:T(8,128)S(1)} %add.56), channel_id=1, source_target_pairs={{0,2},{1,3},{2,0},{3,1},{4,6},{5,7},{6,4},{7,5},{8,10},{9,11},{10,... | collective-permute-start | bytes 196616 | tf_op jit(solution)/shard_map/ppermute | solution.py:310
  27.2 2.6 %collective-permute-done.1 = f32[128,128]{1,0:T(8,128)S(1)} collective-permute-done((f32[128,128]{1,0:T(8,128)S(1)}, f32[128,128]{1,0:T(8,128)S(1)}, u32[]{:S(2)}, u32[]{:S(2)}) %collective-permute-start.1) | collective-permute-done | bytes 65568 | tf_op jit(solution)/shard_map/ppermute | solution.py:310
  29.9 0.1 collective-permute-start.2
  30.0 1.2 %collective-permute-done.2 = f32[4,8,2,128]{3,2,1,0:T(2,128)S(1)} collective-permute-done((f32[4,8,2,128]{3,2,1,0:T(2,128)S(1)}, f32[4,8,2,128]{3,2,1,0:T(2,128)S(1)}, u32[]{:S(2)}, u32[]{:S(2)}) %collective-permute-start.2) | collective-permute-done | bytes 32800 | tf_op jit(solution)/shard_map/ppermute | solution.py:304
  31.3 1.5 %collective-permute-start.3 = (f32[8,2,128]{2,1,0:T(2,128)S(1)}, f32[8,2,128]{2,1,0:T(2,128)S(1)}, u32[]{:S(2)}, u32[]{:S(2)}) collective-permute-start(f32[8,2,128]{2,1,0:T(2,128)S(1)} %get-tuple-element.9), channel_id=1, source_target_pairs={{0,8},{8,16},{16,24},{24,0},{1,9},{9,17},{17,25},{25,1},{2,10},{10... | collective-permute-start | bytes 24584 | tf_op jit(solution)/shard_map/ppermute | solution.py:304
  32.8 1.1 %collective-permute-start.4 = (f32[8,2,128]{2,1,0:T(2,128)S(1)}, f32[8,2,128]{2,1,0:T(2,128)S(1)}, u32[]{:S(2)}, u32[]{:S(2)}) collective-permute-start(f32[8,2,128]{2,1,0:T(2,128)S(1)} %get-tuple-element.10), channel_id=1, source_target_pairs={{0,16},{8,24},{16,0},{24,8},{1,17},{9,25},{17,1},{25,9},{2,18},{10... | collective-permute-start | bytes 24584 | tf_op jit(solution)/shard_map/ppermute | solution.py:304
  33.9 2.2 %collective-permute-start.5 = (f32[8,2,128]{2,1,0:T(2,128)S(1)}, f32[8,2,128]{2,1,0:T(2,128)S(1)}, u32[]{:S(2)}, u32[]{:S(2)}) collective-permute-start(f32[8,2,128]{2,1,0:T(2,128)S(1)} %get-tuple-element.11), channel_id=1, source_target_pairs={{0,24},{8,0},{16,8},{24,16},{1,25},{9,1},{17,9},{25,17},{2,26},{10... | collective-permute-start | bytes 24584 | tf_op jit(solution)/shard_map/ppermute | solution.py:304
  36.1 2.1 %collective-permute-done.4 = f32[8,2,128]{2,1,0:T(2,128)S(1)} collective-permute-done((f32[8,2,128]{2,1,0:T(2,128)S(1)}, f32[8,2,128]{2,1,0:T(2,128)S(1)}, u32[]{:S(2)}, u32[]{:S(2)}) %collective-permute-start.4) | collective-permute-done | bytes 8224 | tf_op jit(solution)/shard_map/ppermute | solution.py:304
  38.2 4.7 %collective-permute-start.10 = (f32[2,128]{1,0:T(2,128)S(1)}, f32[2,128]{1,0:T(2,128)S(1)}, u32[]{:S(2)}, u32[]{:S(2)}) collective-permute-start(f32[2,128]{1,0:T(2,128)S(1)} %get-tuple-element.14), channel_id=1, source_target_pairs={{0,160},{32,192},{64,224},{96,0},{128,32},{160,64},{192,96},{224,1... | collective-permute-start | bytes 3080 | tf_op jit(solution)/shard_map/ppermute | solution.py:304
  43.0 1.2 %collective-permute-start.11 = (f32[2,128]{1,0:T(2,128)S(1)}, f32[2,128]{1,0:T(2,128)S(1)}, u32[]{:S(2)}, u32[]{:S(2)}) collective-permute-start(f32[2,128]{1,0:T(2,128)S(1)} %get-tuple-element.13), channel_id=1, source_target_pairs={{0,192},{32,224},{64,0},{96,32},{128,64},{160,96},{192,128},{224,1... | collective-permute-start | bytes 3080 | tf_op jit(solution)/shard_map/ppermute | solution.py:304
  44.2 0.6 collective-permute-start.12
  44.8 1.4 %collective-permute-start.6 = (f32[2,128]{1,0:T(2,128)S(1)}, f32[2,128]{1,0:T(2,128)S(1)}, u32[]{:S(2)}, u32[]{:S(2)}) collective-permute-start(f32[2,128]{1,0:T(2,128)S(1)} %get-tuple-element.12), channel_id=1, source_target_pairs={{0,32},{32,64},{64,96},{96,128},{128,160},{160,192},{192,224},{224... | collective-permute-start | bytes 3080 | tf_op jit(solution)/shard_map/ppermute | solution.py:304
  46.2 1.7 %collective-permute-start.7 = (f32[2,128]{1,0:T(2,128)S(1)}, f32[2,128]{1,0:T(2,128)S(1)}, u32[]{:S(2)}, u32[]{:S(2)}) collective-permute-start(f32[2,128]{1,0:T(2,128)S(1)} %get-tuple-element.17), channel_id=1, source_target_pairs={{0,64},{32,96},{64,128},{96,160},{128,192},{160,224},{192,0},{224,... | collective-permute-start | bytes 3080 | tf_op jit(solution)/shard_map/ppermute | solution.py:304
  47.9 3.8 %collective-permute-start.8 = (f32[2,128]{1,0:T(2,128)S(1)}, f32[2,128]{1,0:T(2,128)S(1)}, u32[]{:S(2)}, u32[]{:S(2)}) collective-permute-start(f32[2,128]{1,0:T(2,128)S(1)} %get-tuple-element.16), channel_id=1, source_target_pairs={{0,96},{32,128},{64,160},{96,192},{128,224},{160,0},{192,32},{224,... | collective-permute-start | bytes 3080 | tf_op jit(solution)/shard_map/ppermute | solution.py:304
  51.7 2.1 %collective-permute-start.9 = (f32[2,128]{1,0:T(2,128)S(1)}, f32[2,128]{1,0:T(2,128)S(1)}, u32[]{:S(2)}, u32[]{:S(2)}) collective-permute-start(f32[2,128]{1,0:T(2,128)S(1)} %get-tuple-element.15), channel_id=1, source_target_pairs={{0,128},{32,160},{64,192},{96,224},{128,0},{160,32},{192,64},{224,... | collective-permute-start | bytes 3080 | tf_op jit(solution)/shard_map/ppermute | solution.py:304
  53.9 0.6 %collective-permute-done.8 = f32[2,128]{1,0:T(2,128)S(1)} collective-permute-done((f32[2,128]{1,0:T(2,128)S(1)}, f32[2,128]{1,0:T(2,128)S(1)}, u32[]{:S(2)}, u32[]{:S(2)}) %collective-permute-start.8) | collective-permute-done | bytes 1056 | tf_op jit(solution)/shard_map/ppermute | solution.py:304
  54.5 4.7 %collective-permute-done.9 = f32[2,128]{1,0:T(2,128)S(1)} collective-permute-done((f32[2,128]{1,0:T(2,128)S(1)}, f32[2,128]{1,0:T(2,128)S(1)}, u32[]{:S(2)}, u32[]{:S(2)}) %collective-permute-start.9) | collective-permute-done | bytes 1056 | tf_op jit(solution)/shard_map/ppermute | solution.py:304
  59.2 0.2 convert_element_type.7.coded
  59.4 1.8 %finish.1 = bf16[2048,256]{1,0:T(8,128)(2,1)} custom-call(f32[64,72,128]{2,1,0:T(8,128)S(1)} %convert_element_type.7.coded, f32[2,128]{1,0:T(2,128)S(1)} %add_multiply_fusion.mean_square), custom_call_target="tpu_custom_call" | custom-call | tf_op jit(solution)/shard_map/finish/pallas_call | solution.py:281
  (20 shorter events, 0.3 us)
Async XLA Ops:
  7.5 51.7 %all-to-all-start = ((f16[64,72,128]{2,1,0:T(8,128)(2,1)}), f16[64,72,128]{2,1,0:T(8,128)(2,1)S(1)}, u32[]{:S(2)}, u32[]{:S(2)}) async-start(f16[64,72,128]{2,1,0:T(8,128)(2,1)} %convert_element_type.6), calls=%async_computation | async-start | bytes 2359296 | tf_op jit(solution)/shard_map/all_to_all | solution.py:328
  19.6 4.4 %collective-permute-start = (f32[128,128]{1,0:T(8,128)S(1)}, f32[128,128]{1,0:T(8,128)S(1)}, u32[]{:S(2)}, u32[]{:S(2)}) collective-permute-start(f32[128,128]{1,0:T(8,128)S(1)} %get-tuple-element.8), channel_id=1, source_target_pairs={{0,1},{1,0},{2,3},{3,2},{4,5},{5,4},{6,7},{7,6},{8,9},{9,8},{10,11... | collective-permute-start | bytes 196616 | tf_op jit(solution)/shard_map/ppermute | solution.py:310
  23.9 5.9 %collective-permute-start.1 = (f32[128,128]{1,0:T(8,128)S(1)}, f32[128,128]{1,0:T(8,128)S(1)}, u32[]{:S(2)}, u32[]{:S(2)}) collective-permute-start(f32[128,128]{1,0:T(8,128)S(1)} %add.56), channel_id=1, source_target_pairs={{0,2},{1,3},{2,0},{3,1},{4,6},{5,7},{6,4},{7,5},{8,10},{9,11},{10,... | collective-permute-start | bytes 196616 | tf_op jit(solution)/shard_map/ppermute | solution.py:310
  29.9 1.3 %collective-permute-start.2 = (f32[4,8,2,128]{3,2,1,0:T(2,128)S(1)}, f32[4,8,2,128]{3,2,1,0:T(2,128)S(1)}, u32[]{:S(2)}, u32[]{:S(2)}) collective-permute-start(f32[4,8,2,128]{3,2,1,0:T(2,128)S(1)} %slice_bitcast_fusion), channel_id=1, source_target_pairs={{0,4},{4,0},{1,5},{5,1},{2,6},{6,2},{3,7},{7,3},{8,12},{12,8},{9,1... | collective-permute-start | bytes 98312 | tf_op jit(solution)/shard_map/ppermute | solution.py:304
  31.3 4.8 %collective-permute-start.3 = (f32[8,2,128]{2,1,0:T(2,128)S(1)}, f32[8,2,128]{2,1,0:T(2,128)S(1)}, u32[]{:S(2)}, u32[]{:S(2)}) collective-permute-start(f32[8,2,128]{2,1,0:T(2,128)S(1)} %get-tuple-element.9), channel_id=1, source_target_pairs={{0,8},{8,16},{16,24},{24,0},{1,9},{9,17},{17,25},{25,1},{2,10},{10... | collective-permute-start | bytes 24584 | tf_op jit(solution)/shard_map/ppermute | solution.py:304
  32.8 5.3 %collective-permute-start.4 = (f32[8,2,128]{2,1,0:T(2,128)S(1)}, f32[8,2,128]{2,1,0:T(2,128)S(1)}, u32[]{:S(2)}, u32[]{:S(2)}) collective-permute-start(f32[8,2,128]{2,1,0:T(2,128)S(1)} %get-tuple-element.10), channel_id=1, source_target_pairs={{0,16},{8,24},{16,0},{24,8},{1,17},{9,25},{17,1},{25,9},{2,18},{10... | collective-permute-start | bytes 24584 | tf_op jit(solution)/shard_map/ppermute | solution.py:304
  33.9 4.2 %collective-permute-start.5 = (f32[8,2,128]{2,1,0:T(2,128)S(1)}, f32[8,2,128]{2,1,0:T(2,128)S(1)}, u32[]{:S(2)}, u32[]{:S(2)}) collective-permute-start(f32[8,2,128]{2,1,0:T(2,128)S(1)} %get-tuple-element.11), channel_id=1, source_target_pairs={{0,24},{8,0},{16,8},{24,16},{1,25},{9,1},{17,9},{25,17},{2,26},{10... | collective-permute-start | bytes 24584 | tf_op jit(solution)/shard_map/ppermute | solution.py:304
  38.2 9.7 %collective-permute-start.10 = (f32[2,128]{1,0:T(2,128)S(1)}, f32[2,128]{1,0:T(2,128)S(1)}, u32[]{:S(2)}, u32[]{:S(2)}) collective-permute-start(f32[2,128]{1,0:T(2,128)S(1)} %get-tuple-element.14), channel_id=1, source_target_pairs={{0,160},{32,192},{64,224},{96,0},{128,32},{160,64},{192,96},{224,1... | collective-permute-start | bytes 3080 | tf_op jit(solution)/shard_map/ppermute | solution.py:304
  43.0 8.8 %collective-permute-start.11 = (f32[2,128]{1,0:T(2,128)S(1)}, f32[2,128]{1,0:T(2,128)S(1)}, u32[]{:S(2)}, u32[]{:S(2)}) collective-permute-start(f32[2,128]{1,0:T(2,128)S(1)} %get-tuple-element.13), channel_id=1, source_target_pairs={{0,192},{32,224},{64,0},{96,32},{128,64},{160,96},{192,128},{224,1... | collective-permute-start | bytes 3080 | tf_op jit(solution)/shard_map/ppermute | solution.py:304
  44.2 9.7 %collective-permute-start.12 = (f32[2,128]{1,0:T(2,128)S(1)}, f32[2,128]{1,0:T(2,128)S(1)}, u32[]{:S(2)}, u32[]{:S(2)}) collective-permute-start(f32[2,128]{1,0:T(2,128)S(1)} %get-tuple-element.18), channel_id=1, source_target_pairs={{0,224},{32,0},{64,32},{96,64},{128,96},{160,128},{192,160},{224,1... | collective-permute-start | bytes 3080 | tf_op jit(solution)/shard_map/ppermute | solution.py:304
  44.8 9.1 %collective-permute-start.6 = (f32[2,128]{1,0:T(2,128)S(1)}, f32[2,128]{1,0:T(2,128)S(1)}, u32[]{:S(2)}, u32[]{:S(2)}) collective-permute-start(f32[2,128]{1,0:T(2,128)S(1)} %get-tuple-element.12), channel_id=1, source_target_pairs={{0,32},{32,64},{64,96},{96,128},{128,160},{160,192},{192,224},{224... | collective-permute-start | bytes 3080 | tf_op jit(solution)/shard_map/ppermute | solution.py:304
  46.2 7.6 %collective-permute-start.7 = (f32[2,128]{1,0:T(2,128)S(1)}, f32[2,128]{1,0:T(2,128)S(1)}, u32[]{:S(2)}, u32[]{:S(2)}) collective-permute-start(f32[2,128]{1,0:T(2,128)S(1)} %get-tuple-element.17), channel_id=1, source_target_pairs={{0,64},{32,96},{64,128},{96,160},{128,192},{160,224},{192,0},{224,... | collective-permute-start | bytes 3080 | tf_op jit(solution)/shard_map/ppermute | solution.py:304
  47.9 6.6 %collective-permute-start.8 = (f32[2,128]{1,0:T(2,128)S(1)}, f32[2,128]{1,0:T(2,128)S(1)}, u32[]{:S(2)}, u32[]{:S(2)}) collective-permute-start(f32[2,128]{1,0:T(2,128)S(1)} %get-tuple-element.16), channel_id=1, source_target_pairs={{0,96},{32,128},{64,160},{96,192},{128,224},{160,0},{192,32},{224,... | collective-permute-start | bytes 3080 | tf_op jit(solution)/shard_map/ppermute | solution.py:304
  51.7 7.5 %collective-permute-start.9 = (f32[2,128]{1,0:T(2,128)S(1)}, f32[2,128]{1,0:T(2,128)S(1)}, u32[]{:S(2)}, u32[]{:S(2)}) collective-permute-start(f32[2,128]{1,0:T(2,128)S(1)} %get-tuple-element.15), channel_id=1, source_target_pairs={{0,128},{32,160},{64,192},{96,224},{128,0},{160,32},{192,64},{224,... | collective-permute-start | bytes 3080 | tf_op jit(solution)/shard_map/ppermute | solution.py:304

commit v9 on v8

--- a/solution.py
+++ b/solution.py
@@ -139,27 +139,26 @@
         copy.start()
     for copy in smalls:
         copy.wait()
-    decays = []
-    for g in range(groups):
-        decays.append(
-            weights(
-                place[0] * groups + g, short_taps, rates, residues,
-                taps_w.at[g], conv_w.at[g], lift_w.at[g],
-            )
+    decays = {}
+
+    def prepare(g):
+        decays[g] = weights(
+            place[0] * groups + g, short_taps, rates, residues,
+            taps_w.at[g], conv_w.at[g], lift_w.at[g],
         )
-    for g in range(groups):
+
+    def arrive(g):
         for copy in bulks[3 * g : 3 * g + 3]:
             copy.wait()
+
+    def front(g):
+        rows = slice(g * WIDTH, (g + 1) * WIDTH)
         filtered = []
         for m in range(3):
-            pieces = []
-            for n in range(blocks):
-                rows = slice(g * WIDTH, (g + 1) * WIDTH)
-                if n == 0:
-                    here = streams[m, rows, :BLOCK]
-                    pieces.append(jnp.concatenate([jnp.zeros_like(here), here], axis=1))
-                else:
-                    pieces.append(streams[m, rows, (n - 1) * BLOCK : (n + 1) * BLOCK])
+            here = streams[m, rows, :BLOCK]
+            pieces = [jnp.concatenate([jnp.zeros_like(here), here], axis=1)]
+            for n in range(1, blocks):
+                pieces.append(streams[m, rows, (n - 1) * BLOCK : (n + 1) * BLOCK])
             both = jnp.dot(
                 jnp.concatenate(pieces, axis=0), taps_w[g, m], preferred_element_type=jnp.float32
             )
@@ -173,6 +172,8 @@
         first[g] = filtered[0]
         direct[g] = (terms[:, :BLOCK] + terms[:, BLOCK : 2 * BLOCK]) + skip_rows * product
         ends[g] = terms[:, 2 * BLOCK : 3 * BLOCK] + terms[:, 3 * BLOCK :]
+
+    def back(g):
         scan(decays[g], ends.at[g], starts.at[g])
         carried = jnp.dot(starts[g], lift_w[g], preferred_element_type=jnp.float32)
         gated = first[g] * (direct[g] + carried)
@@ -187,6 +188,13 @@
             size = jnp.maximum(peaks[...], size)
         squares[...] = squared
         peaks[...] = size
+
+    for g in range(groups):
+        prepare(g)
+        arrive(g)
+    for g in range(groups):
+        front(g)
+        back(g)
 
     total = squares[pl.ds(0, blocks, stride=8), :]
     peak = jnp.maximum(peaks[pl.ds(0, blocks, stride=8), :], TINY)

time: 61.4 us -> 61.5 us (level)
  no operation moved by 1% of the time
where the time goes in v9:
time: 61.5 us; the launch traced here: 61.4 us
  starting transfers between devices  37.5 us (61%)
  waiting for transfers between devices  13.9 us (23%)
  Pallas kernels  8.29 us (13%)
  other arithmetic  1.55 us (3%)
    ppermute x11, starting transfers between devices, scattered(): total = total + lax.ppermute(turned[by], axis, pairs)  20.5 us
    all_to_all x1, starting transfers between devices, shards(): moved = lax.all_to_all(coded.astype(jnp.float16), CTX, 0, 0, tiled=True)  12 us
    ppermute x11, waiting for transfers between devices, scattered(): total = total + lax.ppermute(turned[by], axis, pairs)  8.61 us
    pallas_call x1, Pallas kernels, mix(): pl.pallas_call(mix_kernel, name='mix', grid_spec=pltpu.PrefetchScalarGrid...  6.47 us
    ppermute x2, waiting for transfers between devices, with_partner(): return array + lax.ppermute(array, axis, pairs)  5.26 us
    ppermute x2, starting transfers between devices, with_partner(): return array + lax.ppermute(array, axis, pairs)  4.95 us
    pallas_call x1, Pallas kernels, finish(): pl.pallas_call(finish_kernel, name='finish', grid=(owners // AT_ONCE,), i...  1.82 us
  transfers between devices with their start and end apart: 14, of which 6 were waited for; matrix products, arithmetic and copies ran while one was open for 0% of the time, Pallas kernels for 0%

profile of v9, /device:TPU:2, one launch (start us, length us, event | category | flops | bytes accessed | tf_op | source)
XLA Modules:
  0.0 61.4 jit_solution(10953545420426452515)
XLA Ops:
  0.0 6.5 %mix.1 = (f32[64,72,128]{2,1,0:T(8,128)S(1)}, f32[128,128]{1,0:T(8,128)S(1)}) custom-call(s32[1]{0:T(128)} %bitcast.place, bf16[3,32,16384]{2,1,0:T(8,128)(2,1)} %far.1, f32[3,7,128]{2,1,0:T(8,128)} %bitcast.62, f32[16,128]{1,0:T(8,128)} %bitcast.63, f32[16,128]{1,0:T(8,128)} %bitcast.64, f32[16,128]{1,0:T(8,128)} %bitcast.65, f32[16,128]{1,0:T(8,128)} %bitcast.66), custom_call_target="tpu_custom_call" | custom-call | tf_op jit(solution)/shard_map/mix/pallas_call | solution.py:230
  6.5 1.2 %convert_element_type.6 = f16[64,72,128]{2,1,0:T(8,128)(2,1)} convert(f32[64,72,128]{2,1,0:T(8,128)S(1)} %get-tuple-element.7) | non-fusion elementwise | flops 589824 | bytes 3538944 | tf_op jit(solution)/shard_map/convert_element_type | solution.py:336
  7.7 12.0 %all-to-all-start = ((f16[64,72,128]{2,1,0:T(8,128)(2,1)}), f16[64,72,128]{2,1,0:T(8,128)(2,1)S(1)}, u32[]{:S(2)}, u32[]{:S(2)}) async-start(f16[64,72,128]{2,1,0:T(8,128)(2,1)} %convert_element_type.6), calls=%async_computation | async-start | bytes 2359296 | tf_op jit(solution)/shard_map/all_to_all | solution.py:336
  19.7 1.7 %collective-permute-start = (f32[128,128]{1,0:T(8,128)S(1)}, f32[128,128]{1,0:T(8,128)S(1)}, u32[]{:S(2)}, u32[]{:S(2)}) collective-permute-start(f32[128,128]{1,0:T(8,128)S(1)} %get-tuple-element.8), channel_id=1, source_target_pairs={{0,1},{1,0},{2,3},{3,2},{4,5},{5,4},{6,7},{7,6},{8,9},{9,8},{10,11... | collective-permute-start | bytes 196616 | tf_op jit(solution)/shard_map/ppermute | solution.py:318
  21.4 2.7 %collective-permute-done = f32[128,128]{1,0:T(8,128)S(1)} collective-permute-done((f32[128,128]{1,0:T(8,128)S(1)}, f32[128,128]{1,0:T(8,128)S(1)}, u32[]{:S(2)}, u32[]{:S(2)}) %collective-permute-start) | collective-permute-done | bytes 65568 | tf_op jit(solution)/shard_map/ppermute | solution.py:318
  24.1 3.3 %collective-permute-start.1 = (f32[128,128]{1,0:T(8,128)S(1)}, f32[128,128]{1,0:T(8,128)S(1)}, u32[]{:S(2)}, u32[]{:S(2)}) collective-permute-start(f32[128,128]{1,0:T(8,128)S(1)} %add.56), channel_id=1, source_target_pairs={{0,2},{1,3},{2,0},{3,1},{4,6},{5,7},{6,4},{7,5},{8,10},{9,11},{10,... | collective-permute-start | bytes 196616 | tf_op jit(solution)/shard_map/ppermute | solution.py:318
  27.4 2.6 %collective-permute-done.1 = f32[128,128]{1,0:T(8,128)S(1)} collective-permute-done((f32[128,128]{1,0:T(8,128)S(1)}, f32[128,128]{1,0:T(8,128)S(1)}, u32[]{:S(2)}, u32[]{:S(2)}) %collective-permute-start.1) | collective-permute-done | bytes 65568 | tf_op jit(solution)/shard_map/ppermute | solution.py:318
  30.1 0.1 collective-permute-start.2
  30.2 1.2 %collective-permute-done.2 = f32[4,8,2,128]{3,2,1,0:T(2,128)S(1)} collective-permute-done((f32[4,8,2,128]{3,2,1,0:T(2,128)S(1)}, f32[4,8,2,128]{3,2,1,0:T(2,128)S(1)}, u32[]{:S(2)}, u32[]{:S(2)}) %collective-permute-start.2) | collective-permute-done | bytes 32800 | tf_op jit(solution)/shard_map/ppermute | solution.py:312
  31.4 1.5 %collective-permute-start.3 = (f32[8,2,128]{2,1,0:T(2,128)S(1)}, f32[8,2,128]{2,1,0:T(2,128)S(1)}, u32[]{:S(2)}, u32[]{:S(2)}) collective-permute-start(f32[8,2,128]{2,1,0:T(2,128)S(1)} %get-tuple-element.9), channel_id=1, source_target_pairs={{0,8},{8,16},{16,24},{24,0},{1,9},{9,17},{17,25},{25,1},{2,10},{10... | collective-permute-start | bytes 24584 | tf_op jit(solution)/shard_map/ppermute | solution.py:312
  33.0 1.1 %collective-permute-start.4 = (f32[8,2,128]{2,1,0:T(2,128)S(1)}, f32[8,2,128]{2,1,0:T(2,128)S(1)}, u32[]{:S(2)}, u32[]{:S(2)}) collective-permute-start(f32[8,2,128]{2,1,0:T(2,128)S(1)} %get-tuple-element.10), channel_id=1, source_target_pairs={{0,16},{8,24},{16,0},{24,8},{1,17},{9,25},{17,1},{25,9},{2,18},{10... | collective-permute-start | bytes 24584 | tf_op jit(solution)/shard_map/ppermute | solution.py:312
  34.0 2.2 %collective-permute-start.5 = (f32[8,2,128]{2,1,0:T(2,128)S(1)}, f32[8,2,128]{2,1,0:T(2,128)S(1)}, u32[]{:S(2)}, u32[]{:S(2)}) collective-permute-start(f32[8,2,128]{2,1,0:T(2,128)S(1)} %get-tuple-element.11), channel_id=1, source_target_pairs={{0,24},{8,0},{16,8},{24,16},{1,25},{9,1},{17,9},{25,17},{2,26},{10... | collective-permute-start | bytes 24584 | tf_op jit(solution)/shard_map/ppermute | solution.py:312
  36.2 2.1 %collective-permute-done.4 = f32[8,2,128]{2,1,0:T(2,128)S(1)} collective-permute-done((f32[8,2,128]{2,1,0:T(2,128)S(1)}, f32[8,2,128]{2,1,0:T(2,128)S(1)}, u32[]{:S(2)}, u32[]{:S(2)}) %collective-permute-start.4) | collective-permute-done | bytes 8224 | tf_op jit(solution)/shard_map/ppermute | solution.py:312
  38.3 4.7 %collective-permute-start.10 = (f32[2,128]{1,0:T(2,128)S(1)}, f32[2,128]{1,0:T(2,128)S(1)}, u32[]{:S(2)}, u32[]{:S(2)}) collective-permute-start(f32[2,128]{1,0:T(2,128)S(1)} %get-tuple-element.14), channel_id=1, source_target_pairs={{0,160},{32,192},{64,224},{96,0},{128,32},{160,64},{192,96},{224,1... | collective-permute-start | bytes 3080 | tf_op jit(solution)/shard_map/ppermute | solution.py:312
  43.1 1.2 %collective-permute-start.11 = (f32[2,128]{1,0:T(2,128)S(1)}, f32[2,128]{1,0:T(2,128)S(1)}, u32[]{:S(2)}, u32[]{:S(2)}) collective-permute-start(f32[2,128]{1,0:T(2,128)S(1)} %get-tuple-element.13), channel_id=1, source_target_pairs={{0,192},{32,224},{64,0},{96,32},{128,64},{160,96},{192,128},{224,1... | collective-permute-start | bytes 3080 | tf_op jit(solution)/shard_map/ppermute | solution.py:312
  44.3 0.6 collective-permute-start.12
  44.9 1.4 %collective-permute-start.6 = (f32[2,128]{1,0:T(2,128)S(1)}, f32[2,128]{1,0:T(2,128)S(1)}, u32[]{:S(2)}, u32[]{:S(2)}) collective-permute-start(f32[2,128]{1,0:T(2,128)S(1)} %get-tuple-element.12), channel_id=1, source_target_pairs={{0,32},{32,64},{64,96},{96,128},{128,160},{160,192},{192,224},{224... | collective-permute-start | bytes 3080 | tf_op jit(solution)/shard_map/ppermute | solution.py:312
  46.4 1.7 %collective-permute-start.7 = (f32[2,128]{1,0:T(2,128)S(1)}, f32[2,128]{1,0:T(2,128)S(1)}, u32[]{:S(2)}, u32[]{:S(2)}) collective-permute-start(f32[2,128]{1,0:T(2,128)S(1)} %get-tuple-element.17), channel_id=1, source_target_pairs={{0,64},{32,96},{64,128},{96,160},{128,192},{160,224},{192,0},{224,... | collective-permute-start | bytes 3080 | tf_op jit(solution)/shard_map/ppermute | solution.py:312
  48.1 3.8 %collective-permute-start.8 = (f32[2,128]{1,0:T(2,128)S(1)}, f32[2,128]{1,0:T(2,128)S(1)}, u32[]{:S(2)}, u32[]{:S(2)}) collective-permute-start(f32[2,128]{1,0:T(2,128)S(1)} %get-tuple-element.16), channel_id=1, source_target_pairs={{0,96},{32,128},{64,160},{96,192},{128,224},{160,0},{192,32},{224,... | collective-permute-start | bytes 3080 | tf_op jit(solution)/shard_map/ppermute | solution.py:312
  51.9 2.1 %collective-permute-start.9 = (f32[2,128]{1,0:T(2,128)S(1)}, f32[2,128]{1,0:T(2,128)S(1)}, u32[]{:S(2)}, u32[]{:S(2)}) collective-permute-start(f32[2,128]{1,0:T(2,128)S(1)} %get-tuple-element.15), channel_id=1, source_target_pairs={{0,128},{32,160},{64,192},{96,224},{128,0},{160,32},{192,64},{224,... | collective-permute-start | bytes 3080 | tf_op jit(solution)/shard_map/ppermute | solution.py:312
  54.0 0.6 %collective-permute-done.8 = f32[2,128]{1,0:T(2,128)S(1)} collective-permute-done((f32[2,128]{1,0:T(2,128)S(1)}, f32[2,128]{1,0:T(2,128)S(1)}, u32[]{:S(2)}, u32[]{:S(2)}) %collective-permute-start.8) | collective-permute-done | bytes 1056 | tf_op jit(solution)/shard_map/ppermute | solution.py:312
  54.6 4.7 %collective-permute-done.9 = f32[2,128]{1,0:T(2,128)S(1)} collective-permute-done((f32[2,128]{1,0:T(2,128)S(1)}, f32[2,128]{1,0:T(2,128)S(1)}, u32[]{:S(2)}, u32[]{:S(2)}) %collective-permute-start.9) | collective-permute-done | bytes 1056 | tf_op jit(solution)/shard_map/ppermute | solution.py:312
  59.4 0.2 convert_element_type.7.coded
  59.5 1.8 %finish.1 = bf16[2048,256]{1,0:T(8,128)(2,1)} custom-call(f32[64,72,128]{2,1,0:T(8,128)S(1)} %convert_element_type.7.coded, f32[2,128]{1,0:T(2,128)S(1)} %add_multiply_fusion.mean_square), custom_call_target="tpu_custom_call" | custom-call | tf_op jit(solution)/shard_map/finish/pallas_call | solution.py:289
  (20 shorter events, 0.3 us)
Async XLA Ops:
  7.7 51.7 %all-to-all-start = ((f16[64,72,128]{2,1,0:T(8,128)(2,1)}), f16[64,72,128]{2,1,0:T(8,128)(2,1)S(1)}, u32[]{:S(2)}, u32[]{:S(2)}) async-start(f16[64,72,128]{2,1,0:T(8,128)(2,1)} %convert_element_type.6), calls=%async_computation | async-start | bytes 2359296 | tf_op jit(solution)/shard_map/all_to_all | solution.py:336
  19.7 4.4 %collective-permute-start = (f32[128,128]{1,0:T(8,128)S(1)}, f32[128,128]{1,0:T(8,128)S(1)}, u32[]{:S(2)}, u32[]{:S(2)}) collective-permute-start(f32[128,128]{1,0:T(8,128)S(1)} %get-tuple-element.8), channel_id=1, source_target_pairs={{0,1},{1,0},{2,3},{3,2},{4,5},{5,4},{6,7},{7,6},{8,9},{9,8},{10,11... | collective-permute-start | bytes 196616 | tf_op jit(solution)/shard_map/ppermute | solution.py:318
  24.1 5.9 %collective-permute-start.1 = (f32[128,128]{1,0:T(8,128)S(1)}, f32[128,128]{1,0:T(8,128)S(1)}, u32[]{:S(2)}, u32[]{:S(2)}) collective-permute-start(f32[128,128]{1,0:T(8,128)S(1)} %add.56), channel_id=1, source_target_pairs={{0,2},{1,3},{2,0},{3,1},{4,6},{5,7},{6,4},{7,5},{8,10},{9,11},{10,... | collective-permute-start | bytes 196616 | tf_op jit(solution)/shard_map/ppermute | solution.py:318
  30.1 1.3 %collective-permute-start.2 = (f32[4,8,2,128]{3,2,1,0:T(2,128)S(1)}, f32[4,8,2,128]{3,2,1,0:T(2,128)S(1)}, u32[]{:S(2)}, u32[]{:S(2)}) collective-permute-start(f32[4,8,2,128]{3,2,1,0:T(2,128)S(1)} %slice_bitcast_fusion), channel_id=1, source_target_pairs={{0,4},{4,0},{1,5},{5,1},{2,6},{6,2},{3,7},{7,3},{8,12},{12,8},{9,1... | collective-permute-start | bytes 98312 | tf_op jit(solution)/shard_map/ppermute | solution.py:312
  31.4 4.8 %collective-permute-start.3 = (f32[8,2,128]{2,1,0:T(2,128)S(1)}, f32[8,2,128]{2,1,0:T(2,128)S(1)}, u32[]{:S(2)}, u32[]{:S(2)}) collective-permute-start(f32[8,2,128]{2,1,0:T(2,128)S(1)} %get-tuple-element.9), channel_id=1, source_target_pairs={{0,8},{8,16},{16,24},{24,0},{1,9},{9,17},{17,25},{25,1},{2,10},{10... | collective-permute-start | bytes 24584 | tf_op jit(solution)/shard_map/ppermute | solution.py:312
  33.0 5.3 %collective-permute-start.4 = (f32[8,2,128]{2,1,0:T(2,128)S(1)}, f32[8,2,128]{2,1,0:T(2,128)S(1)}, u32[]{:S(2)}, u32[]{:S(2)}) collective-permute-start(f32[8,2,128]{2,1,0:T(2,128)S(1)} %get-tuple-element.10), channel_id=1, source_target_pairs={{0,16},{8,24},{16,0},{24,8},{1,17},{9,25},{17,1},{25,9},{2,18},{10... | collective-permute-start | bytes 24584 | tf_op jit(solution)/shard_map/ppermute | solution.py:312
  34.0 4.2 %collective-permute-start.5 = (f32[8,2,128]{2,1,0:T(2,128)S(1)}, f32[8,2,128]{2,1,0:T(2,128)S(1)}, u32[]{:S(2)}, u32[]{:S(2)}) collective-permute-start(f32[8,2,128]{2,1,0:T(2,128)S(1)} %get-tuple-element.11), channel_id=1, source_target_pairs={{0,24},{8,0},{16,8},{24,16},{1,25},{9,1},{17,9},{25,17},{2,26},{10... | collective-permute-start | bytes 24584 | tf_op jit(solution)/shard_map/ppermute | solution.py:312
  38.3 9.7 %collective-permute-start.10 = (f32[2,128]{1,0:T(2,128)S(1)}, f32[2,128]{1,0:T(2,128)S(1)}, u32[]{:S(2)}, u32[]{:S(2)}) collective-permute-start(f32[2,128]{1,0:T(2,128)S(1)} %get-tuple-element.14), channel_id=1, source_target_pairs={{0,160},{32,192},{64,224},{96,0},{128,32},{160,64},{192,96},{224,1... | collective-permute-start | bytes 3080 | tf_op jit(solution)/shard_map/ppermute | solution.py:312
  43.1 8.8 %collective-permute-start.11 = (f32[2,128]{1,0:T(2,128)S(1)}, f32[2,128]{1,0:T(2,128)S(1)}, u32[]{:S(2)}, u32[]{:S(2)}) collective-permute-start(f32[2,128]{1,0:T(2,128)S(1)} %get-tuple-element.13), channel_id=1, source_target_pairs={{0,192},{32,224},{64,0},{96,32},{128,64},{160,96},{192,128},{224,1... | collective-permute-start | bytes 3080 | tf_op jit(solution)/shard_map/ppermute | solution.py:312
  44.3 9.7 %collective-permute-start.12 = (f32[2,128]{1,0:T(2,128)S(1)}, f32[2,128]{1,0:T(2,128)S(1)}, u32[]{:S(2)}, u32[]{:S(2)}) collective-permute-start(f32[2,128]{1,0:T(2,128)S(1)} %get-tuple-element.18), channel_id=1, source_target_pairs={{0,224},{32,0},{64,32},{96,64},{128,96},{160,128},{192,160},{224,1... | collective-permute-start | bytes 3080 | tf_op jit(solution)/shard_map/ppermute | solution.py:312
  44.9 9.1 %collective-permute-start.6 = (f32[2,128]{1,0:T(2,128)S(1)}, f32[2,128]{1,0:T(2,128)S(1)}, u32[]{:S(2)}, u32[]{:S(2)}) collective-permute-start(f32[2,128]{1,0:T(2,128)S(1)} %get-tuple-element.12), channel_id=1, source_target_pairs={{0,32},{32,64},{64,96},{96,128},{128,160},{160,192},{192,224},{224... | collective-permute-start | bytes 3080 | tf_op jit(solution)/shard_map/ppermute | solution.py:312
  46.4 7.6 %collective-permute-start.7 = (f32[2,128]{1,0:T(2,128)S(1)}, f32[2,128]{1,0:T(2,128)S(1)}, u32[]{:S(2)}, u32[]{:S(2)}) collective-permute-start(f32[2,128]{1,0:T(2,128)S(1)} %get-tuple-element.17), channel_id=1, source_target_pairs={{0,64},{32,96},{64,128},{96,160},{128,192},{160,224},{192,0},{224,... | collective-permute-start | bytes 3080 | tf_op jit(solution)/shard_map/ppermute | solution.py:312
  48.1 6.6 %collective-permute-start.8 = (f32[2,128]{1,0:T(2,128)S(1)}, f32[2,128]{1,0:T(2,128)S(1)}, u32[]{:S(2)}, u32[]{:S(2)}) collective-permute-start(f32[2,128]{1,0:T(2,128)S(1)} %get-tuple-element.16), channel_id=1, source_target_pairs={{0,96},{32,128},{64,160},{96,192},{128,224},{160,0},{192,32},{224,... | collective-permute-start | bytes 3080 | tf_op jit(solution)/shard_map/ppermute | solution.py:312
  51.9 7.5 %collective-permute-start.9 = (f32[2,128]{1,0:T(2,128)S(1)}, f32[2,128]{1,0:T(2,128)S(1)}, u32[]{:S(2)}, u32[]{:S(2)}) collective-permute-start(f32[2,128]{1,0:T(2,128)S(1)} %get-tuple-element.15), channel_id=1, source_target_pairs={{0,128},{32,160},{64,192},{96,224},{128,0},{160,32},{192,64},{224,... | collective-permute-start | bytes 3080 | tf_op jit(solution)/shard_map/ppermute | solution.py:312
